TPU v7x, 128 devices: a whole 4x4x4 slice. The times are simulated.
128 devices in a mesh: atoms: 128 (over y, x, z, core).
Axes of the slice: x: 4, y: 4, z: 4, core: 2. Of those that a mesh axis runs over, the one named last changes fastest.
Arguments:
- features: bfloat16 [16384, 9, 128], P('atoms'), may hold values from -6 to 6
- cotangent: bfloat16 [16384, 9, 128], P('atoms'), may hold values from -6 to 6
- wigner: float32 [9, 9, 49152], P(None, None, 'atoms'), may hold values from -1 to 1, as said below
- pair_blocks: int32 [2048, 2], P('atoms'), may hold values from 0 to 127, all different within a row; in each aligned block of 16 rows (0 to 15, 16 to 31, ...) at most 2 rows name the same one
- pair_rows: int32 [2, 6, 2048], P(None, None, 'atoms'), may hold values from 0 to 127
- edge_ends: int32 [2, 49152], P(None, 'atoms'), may hold values from 0 to 5
- first_m0: bfloat16 [768, 512], replicated, may hold values from -0.21875 to 0.21875
- first_m1: bfloat16 [2, 512, 256], replicated, may hold values from -0.1875 to 0.1875
- first_m2: bfloat16 [2, 256, 128], replicated, may hold values from -0.25 to 0.25
- second_m0: bfloat16 [384, 384], replicated, may hold values from -0.3125 to 0.3125
- second_m1: bfloat16 [2, 256, 256], replicated, may hold values from -0.25 to 0.25
- second_m2: bfloat16 [2, 128, 128], replicated, may hold values from -0.375 to 0.375
Outputs:
- messages: bfloat16 [16384, 9, 128], P('atoms')
- grad_features: float32 [16384, 9, 128], P('atoms')
- grad_first_m0: float32 [768, 512], replicated
- grad_first_m1: float32 [2, 512, 256], replicated
- grad_first_m2: float32 [2, 256, 128], replicated
- grad_second_m0: float32 [384, 384], replicated
- grad_second_m1: float32 [2, 256, 256], replicated
- grad_second_m2: float32 [2, 128, 128], replicated
Inputs may be any that keep to these rules, and one draw needn't show every extreme that they name: `pair_blocks`: among the 16 pairs of one device no atom block is named more than 2 times; the two blocks of a pair differ. `wigner`: each edge's matrix is orthogonal and block diagonal over degrees 0, 1 and 2.
All inputs are finite; a program needn't handle non-finite values.
Results may differ from a plain program's by a relative error of at most 0.0045.
Values may be sent and summed in bfloat16 or wider, within the bound.
No kernel may reach another device: no remote copies, remote signals or barrier semaphores. Data moves between devices by JAX's collectives and lax.ppermute only.
A program may use at most 128 MiB of HBM per device.

v0:
```python
import jax
import jax.numpy as jnp
from jax import lax
from jax.sharding import PartitionSpec as P

COEF_ORDER = (0, 2, 6, 3, 7, 1, 5, 8, 4)


def rotate(turned, row_block):
    return jnp.einsum(
        "ije,ejc->eic", turned, row_block.astype(jnp.float32), precision=lax.Precision.HIGHEST
    )


def unrotate(turned, row_block):
    return jnp.einsum("ije,eic->ejc", turned, row_block, precision=lax.Precision.HIGHEST)


def widen_pair(pair_weights):
    upper_half = jnp.concatenate([pair_weights[0], pair_weights[1]], axis=1)
    lower_half = jnp.concatenate([-pair_weights[1], pair_weights[0]], axis=1)
    return jnp.concatenate([upper_half, lower_half], axis=0)


def narrow(gradient):
    half_rows = gradient.shape[0] // 2
    half_cols = gradient.shape[1] // 2
    return jnp.stack(
        [
            gradient[:half_rows, :half_cols] + gradient[half_rows:, half_cols:],
            gradient[:half_rows, half_cols:] - gradient[half_rows:, :half_cols],
        ]
    )


def forward_dot(left_rows, weight):
    return jnp.dot(left_rows, weight, preferred_element_type=jnp.float32)


def backward_dot(gradient, weight):
    return lax.dot_general(
        gradient, weight, (((1,), (1,)), ((), ())), preferred_element_type=jnp.float32
    )


def weight_dot(left_rows, gradient):
    return lax.dot_general(
        left_rows, gradient, (((0,), (0,)), ((), ())), preferred_element_type=jnp.float32
    )


def forward_part(turned, source, target, weights):
    zero_a, big_one_a, big_two_a, zero_b, big_one_b, big_two_b = weights
    row_count = source.shape[0]
    channels = source.shape[2]
    rot_source = rotate(turned, source)
    rot_target = rotate(turned, target)
    lifted = jnp.concatenate(
        [
            jnp.concatenate([rot_source, rot_target], axis=2),
            jnp.concatenate([rot_target, rot_source], axis=2),
        ],
        axis=0,
    )
    lifted = lifted.astype(jnp.bfloat16).reshape(2 * row_count, 18 * channels)
    zero_part = lifted[:, : 6 * channels]
    one_part = lifted[:, 6 * channels : 14 * channels]
    two_part = lifted[:, 14 * channels :]
    first_out = forward_dot(zero_part, zero_a)
    hidden = jnp.concatenate(
        [
            first_out[:, : 3 * channels],
            forward_dot(one_part, big_one_a),
            forward_dot(two_part, big_two_a),
        ],
        axis=1,
    )
    gate_value = jax.nn.sigmoid(first_out[:, 3 * channels :])
    scalar_part = hidden[:, :channels]
    gated_part = hidden[:, channels:].reshape(2 * row_count, 8, channels)
    activated = jnp.concatenate(
        [
            jax.nn.silu(scalar_part),
            (gated_part * gate_value[:, None, :]).reshape(2 * row_count, 8 * channels),
        ],
        axis=1,
    ).astype(jnp.bfloat16)
    mixed_rows = jnp.concatenate(
        [
            forward_dot(activated[:, : 3 * channels], zero_b),
            forward_dot(activated[:, 3 * channels : 7 * channels], big_one_b),
            forward_dot(activated[:, 7 * channels :], big_two_b),
        ],
        axis=1,
    )
    mixed_rows = mixed_rows.reshape(2 * row_count, 9, channels)
    stored = (zero_part, one_part, two_part, scalar_part, gated_part, gate_value, activated)
    return (
        unrotate(turned, mixed_rows[:row_count]),
        unrotate(turned, mixed_rows[row_count:]),
        stored,
    )


def backward_part(turned, stored, grad_target_in, grad_source_in, weights):
    zero_a, big_one_a, big_two_a, zero_b, big_one_b, big_two_b = weights
    zero_part, one_part, two_part, scalar_part, gated_part, gate_value, activated = stored
    row_count = grad_target_in.shape[0]
    channels = grad_target_in.shape[2]
    all_rows = 2 * row_count
    grad_mix = jnp.concatenate(
        [rotate(turned, grad_target_in), rotate(turned, grad_source_in)], axis=0
    )
    grad_mix = grad_mix.astype(jnp.bfloat16).reshape(all_rows, 9 * channels)
    mix_zero = grad_mix[:, : 3 * channels]
    mix_one = grad_mix[:, 3 * channels : 7 * channels]
    mix_two = grad_mix[:, 7 * channels :]
    grad_act = jnp.concatenate(
        [
            backward_dot(mix_zero, zero_b),
            backward_dot(mix_one, big_one_b),
            backward_dot(mix_two, big_two_b),
        ],
        axis=1,
    )
    terms_second = (
        weight_dot(activated[:, : 3 * channels], mix_zero),
        narrow(weight_dot(activated[:, 3 * channels : 7 * channels], mix_one)),
        narrow(weight_dot(activated[:, 7 * channels :], mix_two)),
    )
    head_gate = jax.nn.sigmoid(scalar_part)
    grad_scalar = grad_act[:, :channels] * head_gate * (1.0 + scalar_part * (1.0 - head_gate))
    grad_gated = grad_act[:, channels:].reshape(all_rows, 8, channels)
    gated_grad = (grad_gated * gate_value[:, None, :]).reshape(all_rows, 8 * channels)
    grad_gate = jnp.sum(grad_gated * gated_part, axis=1) * gate_value * (1.0 - gate_value)
    grad_zero = jnp.concatenate(
        [grad_scalar, gated_grad[:, : 2 * channels], grad_gate], axis=1
    ).astype(jnp.bfloat16)
    grad_one = gated_grad[:, 2 * channels : 6 * channels].astype(jnp.bfloat16)
    grad_two = gated_grad[:, 6 * channels :].astype(jnp.bfloat16)
    grad_lifted = jnp.concatenate(
        [
            backward_dot(grad_zero, zero_a),
            backward_dot(grad_one, big_one_a),
            backward_dot(grad_two, big_two_a),
        ],
        axis=1,
    ).reshape(all_rows, 9, 2 * channels)
    terms_first = (
        weight_dot(zero_part, grad_zero),
        narrow(weight_dot(one_part, grad_one)),
        narrow(weight_dot(two_part, grad_two)),
    )
    front_grad = grad_lifted[:row_count]
    back_grad = grad_lifted[row_count:]
    grad_source = unrotate(turned, front_grad[:, :, :channels] + back_grad[:, :, channels:])
    grad_target = unrotate(turned, front_grad[:, :, channels:] + back_grad[:, :, :channels])
    return (grad_source, grad_target, terms_first + terms_second)


def slot_ranks(owners):
    end_count = owners.shape[0]
    same_owner = owners[:, None] == owners[None, :]
    positions = jnp.arange(end_count, dtype=jnp.int32)
    earlier = positions[:, None] > positions[None, :]
    return jnp.sum(jnp.logical_and(same_owner, earlier), axis=1)


def local(
    features,
    cotangent,
    wigner,
    pair_blocks,
    pair_rows,
    edge_ends,
    first_m0,
    first_m1,
    first_m2,
    second_m0,
    second_m1,
    second_m2,
):
    peer_count = lax.axis_size("atoms")
    block_atoms = features.shape[0]
    coef_count = features.shape[1]
    channels = features.shape[2]
    pair_count = pair_blocks.shape[0]
    row_width = pair_rows.shape[1]
    edge_count = edge_ends.shape[1]
    per_pair = edge_count // pair_count
    slot_count = max(2, 4 * pair_count // peer_count)
    owners = pair_blocks.reshape(2 * pair_count)
    order_rank = slot_ranks(owners)
    end_rows = jnp.transpose(pair_rows, (2, 0, 1)).reshape(2 * pair_count, row_width)
    request = (
        jnp.zeros((peer_count, slot_count, row_width), jnp.int32)
        .at[owners, order_rank]
        .set(end_rows)
    )
    requested = lax.all_to_all(request, "atoms", split_axis=0, concat_axis=0, tiled=True)
    picked = requested.reshape(peer_count * slot_count * row_width)
    buffer_shape = (peer_count, slot_count, row_width, coef_count, channels)
    got_features, got_cotangent = (
        lax.all_to_all(
            features[picked].reshape(buffer_shape), "atoms", split_axis=0, concat_axis=0, tiled=True
        ),
        lax.all_to_all(
            cotangent[picked].reshape(buffer_shape),
            "atoms",
            split_axis=0,
            concat_axis=0,
            tiled=True,
        ),
    )
    flat_shape = (peer_count * slot_count * row_width, coef_count, channels)
    flat_features = got_features.reshape(flat_shape)
    flat_cotangent = got_cotangent.reshape(flat_shape)
    end_slot = (owners * slot_count + order_rank) * row_width
    pair_of = jnp.arange(edge_count, dtype=jnp.int32) // per_pair
    target_pos = end_slot[2 * pair_of] + edge_ends[0]
    source_pos = end_slot[2 * pair_of + 1] + edge_ends[1]
    weights = (
        first_m0,
        widen_pair(first_m1),
        widen_pair(first_m2),
        second_m0,
        widen_pair(second_m1),
        widen_pair(second_m2),
    )
    plain_weights = (first_m0, first_m1, first_m2, second_m0, second_m1, second_m2)
    step_rows = min(512, edge_count)
    step_count = edge_count // step_rows
    index_order = jnp.array(COEF_ORDER, dtype=jnp.int32)
    zero_terms = tuple((jnp.zeros(weight.shape, jnp.float32) for weight in plain_weights))

    def block_inputs():
        turned = jnp.take(wigner, index_order, axis=0)
        return (turned, source_pos, target_pos)

    def collect(stacked):
        return stacked.reshape(edge_count, coef_count, channels)

    def to_slots(first_rows, first_pos, second_rows, second_pos):
        slot_sums = (
            jnp.zeros(flat_shape, jnp.float32)
            .at[first_pos]
            .add(first_rows)
            .at[second_pos]
            .add(second_rows)
        )
        return slot_sums.reshape(buffer_shape)

    def joint_step(running, block_index):
        turned, source_rows, target_rows = block_inputs()
        to_target, to_source, stored = forward_part(
            turned, flat_features[source_rows], flat_features[target_rows], weights
        )
        grad_source, grad_target, grad_terms = backward_part(
            turned, stored, flat_cotangent[target_rows], flat_cotangent[source_rows], weights
        )
        running = tuple(
            (left_term + right_term for left_term, right_term in zip(running, grad_terms))
        )
        return (running, (to_target, to_source, grad_source, grad_target))

    totals, results = lax.scan(joint_step, zero_terms, jnp.arange(step_count, dtype=jnp.int32))
    slot_msgs = to_slots(collect(results[0]), target_pos, collect(results[1]), source_pos)
    slot_grads = to_slots(collect(results[2]), source_pos, collect(results[3]), target_pos)
    back_msgs, back_grads = (
        lax.all_to_all(slot_msgs, "atoms", split_axis=0, concat_axis=0, tiled=True),
        lax.all_to_all(slot_grads, "atoms", split_axis=0, concat_axis=0, tiled=True),
    )
    messages = (
        jnp.zeros((block_atoms, coef_count, channels), jnp.float32)
        .at[picked]
        .add(back_msgs.reshape(flat_shape))
        .astype(jnp.bfloat16)
    )
    grad_features = (
        jnp.zeros((block_atoms, coef_count, channels), jnp.float32)
        .at[picked]
        .add(back_grads.reshape(flat_shape))
    )
    summed = lax.psum(totals, "atoms")
    grad_scale = (2.0 * edge_count * peer_count) ** (-0.5)
    return (
        messages,
        grad_features,
        summed[0] * grad_scale,
        summed[1] * grad_scale,
        summed[2] * grad_scale,
        summed[3] * grad_scale,
        summed[4] * grad_scale,
        summed[5] * grad_scale,
    )


def solution(mesh):
    in_specs = (
        P("atoms", None, None),
        P("atoms", None, None),
        P(None, None, "atoms"),
        P("atoms", None),
        P(None, None, "atoms"),
        P(None, "atoms"),
        P(),
        P(),
        P(),
        P(),
        P(),
        P(),
    )
    out_specs = (P("atoms", None, None), P("atoms", None, None), P(), P(), P(), P(), P(), P())
    return jax.shard_map(local, mesh=mesh, in_specs=in_specs, out_specs=out_specs, check_vma=False)
```

profile of v0, /device:TPU:1, one launch (start us, length us, event | category | flops | bytes accessed | tf_op | source)
XLA Modules:
  0.0 1062.8 jit_solution(8837809509495597720)
XLA Ops:
  11.3 21.3 %all_to_all.25 = s32[128,2,6]{2,1,0:T(2,128)S(1)} all-to-all(s32[128,2,6]{2,1,0:T(2,128)S(1)} %scatter_fusion), channel_id=1, replica_groups=mesh['atoms'=128] {'atoms'}, dimensions={0} | all-to-all | bytes 12288 | tf_op jit(solution)/shard_map/all_to_all | solution.py:200
  33.4 15.0 %gather_fusion.1 = bf16[1536,9,128]{2,0,1:T(8,128)(2,1)} fusion(bf16[128,9,128]{2,0,1:T(8,128)(2,1)S(1)} %copy-done.2, s32[2048]{0:T(1024)S(1)} %pad_clamp_fusion), kind=kCustom, calls=%fused_computation.1 | custom fusion | bytes 7084032 | tf_op jit(solution)/shard_map/gather | solution.py:205
  48.4 6.9 reshape.273
  55.2 7.0 copy.112
  81.6 15.5 %select_select_fusion = s32[384]{0:T(512)S(1)} fusion(pred[384]{0:T(512)(128)(4,1)S(1)} %compare_reduce_fusion, pred[384]{0:T(512)(128)(4,1)S(1)} %compare_reduce_fusion.1, pred[384]{0:T(512)(128)(4,1)S(1)} %compare_reduce_fusion.2, pred[384]{0:T(512)(128)(4,1)S(1)} %compare_reduce_fusion.3, pred[384]{0:T(512)(128)(4,1)S(1)} %compare_reduce_fusion.4, ...), kind=kLoop, calls=%fused_computation.200 | loop fusion | flops 9600 | bytes 12772 | tf_op jit(solution)/shard_map/gather | solution.py:221
  97.2 15.5 %select_select_fusion.1 = s32[384]{0:T(512)S(1)} fusion(pred[384]{0:T(512)(128)(4,1)S(1)} %compare_reduce_fusion.25, pred[384]{0:T(512)(128)(4,1)S(1)} %compare_reduce_fusion.26, pred[384]{0:T(512)(128)(4,1)S(1)} %compare_reduce_fusion.27, pred[384]{0:T(512)(128)(4,1)S(1)} %compare_reduce_fusion.28, pred[384]{0:T(512)(128)(4,1)S(1)} %compare_reduce_fusion.29, ...), kind=kLoop, calls=%fused_computation.201 | loop fusion | flops 9600 | bytes 12772 | tf_op jit(solution)/shard_map/gather | solution.py:220
  112.8 14.9 %gather_fusion.4 = bf16[1536,9,128]{2,0,1:T(8,128)(2,1)} fusion(bf16[128,9,128]{2,0,1:T(8,128)(2,1)S(1)} %copy-done.3, s32[2048]{0:T(1024)S(1)} %pad_clamp_fusion), kind=kCustom, calls=%fused_computation.4 | custom fusion | bytes 7084032 | tf_op jit(solution)/shard_map/gather | solution.py:208
  141.5 10.8 %all-to-all-start.3 = ((bf16[128,2,6,9,128]{4,1,3,2,0:T(2,128)(2,1)}), bf16[128,2,6,9,128]{4,1,3,2,0:T(2,128)(2,1)}, u32[]{:S(2)}, u32[]{:S(2)}) async-start(bf16[128,2,6,9,128]{4,1,3,2,0:T(2,128)(2,1)} %copy.128), calls=%async_computation.3 | async-start | bytes 7077888 | tf_op jit(solution)/shard_map/all_to_all | solution.py:207
  278.7 7.9 fusion.83
  296.5 47.4 %scatter_fusion.4 = f32[1536,9,128]{2,1,0:T(8,128)} fusion(f32[1536,9,128]{2,1,0:T(8,128)} %broadcast.239.clone.1, s32[384]{0:T(512)S(1)} %get-tuple-element.101, f32[384,9,128]{2,1,0:T(8,128)} %fusion.83), kind=kCustom, calls=%fused_computation.11 | custom fusion | flops 442368 | bytes 5309952 | tf_op jit(solution)/shard_map/scatter-add | solution.py:247
  343.9 47.4 %scatter_fusion.5 = f32[1536,9,128]{2,1,0:T(8,128)} fusion(f32[1536,9,128]{2,1,0:T(8,128)} %scatter_fusion.4, s32[384]{0:T(512)S(1)} %get-tuple-element.102, f32[384,9,128]{2,1,0:T(8,128)} %fusion.84), kind=kCustom, calls=%fused_computation.12 | custom fusion | flops 442368 | bytes 5309952 | tf_op jit(solution)/shard_map/scatter-add | solution.py:249
  391.3 14.0 %copy.145 = f32[128,2,6,9,128]{4,1,3,2,0:T(2,128)} copy(f32[128,2,6,9,128]{4,3,2,1,0:T(8,128)} %bitcast.139) | data formatting | bytes 14155776 | tf_op jit(solution)/shard_map/reshape | solution.py:251
  405.2 7.2 all-to-all-start.4
  424.3 7.7 fusion.81
  436.9 47.4 %scatter_fusion.1 = f32[1536,9,128]{2,1,0:T(8,128)} fusion(f32[1536,9,128]{2,1,0:T(8,128)} %broadcast.239.clone, s32[384]{0:T(512)S(1)} %get-tuple-element.102, f32[384,9,128]{2,1,0:T(8,128)} %fusion.81), kind=kCustom, calls=%fused_computation.8 | custom fusion | flops 442368 | bytes 5309952 | tf_op jit(solution)/shard_map/scatter-add | solution.py:247
  484.2 7.7 fusion.82
  492.0 47.4 %scatter_fusion.2 = f32[1536,9,128]{2,1,0:T(8,128)} fusion(f32[1536,9,128]{2,1,0:T(8,128)} %scatter_fusion.1, s32[384]{0:T(512)S(1)} %get-tuple-element.101, f32[384,9,128]{2,1,0:T(8,128)} %fusion.82), kind=kCustom, calls=%fused_computation.9 | custom fusion | flops 442368 | bytes 5309952 | tf_op jit(solution)/shard_map/scatter-add | solution.py:249
  539.4 14.2 %copy.125 = f32[128,2,6,9,128]{4,1,3,2,0:T(2,128)} copy(f32[128,2,6,9,128]{4,3,2,1,0:T(8,128)} %bitcast.138) | data formatting | bytes 14155776 | tf_op jit(solution)/shard_map/reshape | solution.py:251
  553.6 10.2 all-to-all-start.2
  575.3 212.3 %all-reduce.3.cloned.1.call-done = (f32[768,512]{1,0:T(8,128)}, f32[2,512,256]{2,1,0:T(8,128)}, f32[2,256,128]{2,1,0:T(8,128)}, f32[384,384]{1,0:T(8,128)}, f32[...) async-done(((f32[768,512]{1,0:T(8,128)}, f32[2,512,256]{2,1,0:T(8,128)}, f32[2,256,128]{2,1,0:T(8,128)}, f32[384,384]{1,0:T(8,128)}, f32[2,256,256]{2,1,0:T(8,128)}, ...) | async-done | bytes 4128784 | tf_op jit(solution)/shard_map/psum | solution.py:284
  796.3 9.4 copy.157
  805.8 119.3 %scatter_fusion.6 = f32[128,9,128]{2,1,0:T(8,128)S(1)} fusion(f32[128,9,128]{2,1,0:T(8,128)S(1)} %broadcast.234.clone.1, s32[1536]{0:T(1024)S(1)} %copy-done.45, f32[1536,9,128]{2,1,0:T(8,128)} %bitcast.141), kind=kCustom, calls=%fused_computation.13 | custom fusion | flops 1769472 | bytes 21239808 | tf_op jit(solution)/shard_map/scatter-add | solution.py:282
  926.1 9.4 copy.154
  935.6 119.3 %scatter_fusion.3 = f32[128,9,128]{2,1,0:T(8,128)S(1)} fusion(f32[128,9,128]{2,1,0:T(8,128)S(1)} %broadcast.234.clone, s32[1536]{0:T(1024)S(1)} %copy-done.45, f32[1536,9,128]{2,1,0:T(8,128)} %bitcast.140), kind=kCustom, calls=%fused_computation.10 | custom fusion | flops 1769472 | bytes 21239808 | tf_op jit(solution)/shard_map/scatter-add | solution.py:276
  (272 shorter events, 212.7 us)
Async XLA Ops:
  7.2 182.9 %copy-start = (bf16[768,512]{1,0:T(8,128)(2,1)S(1)}, bf16[768,512]{1,0:T(8,128)(2,1)}, u32[]{:S(2)}) copy-start(bf16[768,512]{1,0:T(8,128)(2,1)} %param.19) | copy-start | bytes 2359300
  7.2 26.2 %copy-start.2 = (bf16[128,9,128]{2,0,1:T(8,128)(2,1)S(1)}, bf16[128,9,128]{2,0,1:T(8,128)(2,1)}, u32[]{:S(2)}) copy-start(bf16[128,9,128]{2,0,1:T(8,128)(2,1)} %param.13) | copy-start | bytes 884740
  62.2 6.4 copy-start.53
  62.2 6.4 copy-start.38
  62.2 79.2 %all-to-all-start.1 = ((bf16[128,2,6,9,128]{4,1,3,2,0:T(2,128)(2,1)}), bf16[128,2,6,9,128]{4,1,3,2,0:T(2,128)(2,1)}, u32[]{:S(2)}, u32[]{:S(2)}) async-start(bf16[128,2,6,9,128]{4,1,3,2,0:T(2,128)(2,1)} %copy.112), calls=%async_computation.1 | async-start | bytes 7077888 | tf_op jit(solution)/shard_map/all_to_all | solution.py:204
  71.5 41.2 %copy-start.52 = (s32[2,384]{1,0:T(2,128)S(1)}, s32[2,384]{1,0:T(2,128)}, u32[]{:S(2)}) copy-start(s32[2,384]{1,0:T(2,128)} %param.18) | copy-start | bytes 9220
  71.5 41.3 %copy-start.3 = (bf16[128,9,128]{2,0,1:T(8,128)(2,1)S(1)}, bf16[128,9,128]{2,0,1:T(8,128)(2,1)}, u32[]{:S(2)}) copy-start(bf16[128,9,128]{2,0,1:T(8,128)(2,1)} %param.14) | copy-start | bytes 884740
  141.4 10.8 %copy-start.43 = (bf16[2,128,128]{2,1,0:T(8,128)(2,1)S(1)}, bf16[2,128,128]{2,1,0:T(8,128)(2,1)}, u32[]{:S(2)}) copy-start(bf16[2,128,128]{2,1,0:T(8,128)(2,1)} %param.24) | copy-start | bytes 196612
  141.4 10.8 %copy-start.31 = (bf16[2,256,128]{2,1,0:T(8,128)(2,1)S(1)}, bf16[2,256,128]{2,1,0:T(8,128)(2,1)}, u32[]{:S(2)}) copy-start(bf16[2,256,128]{2,1,0:T(8,128)(2,1)} %param.21) | copy-start | bytes 393220
  141.4 12.1 %copy-start.29 = (bf16[2,256,256]{2,1,0:T(8,128)(2,1)S(1)}, bf16[2,256,256]{2,1,0:T(8,128)(2,1)}, u32[]{:S(2)}) copy-start(bf16[2,256,256]{2,1,0:T(8,128)(2,1)} %param.23) | copy-start | bytes 786436
  141.4 13.5 %copy-start.26 = (bf16[2,512,256]{2,1,0:T(8,128)(2,1)S(1)}, bf16[2,512,256]{2,1,0:T(8,128)(2,1)}, u32[]{:S(2)}) copy-start(bf16[2,512,256]{2,1,0:T(8,128)(2,1)} %param.20) | copy-start | bytes 1572868
  141.5 56.0 %all-to-all-start.3 = ((bf16[128,2,6,9,128]{4,1,3,2,0:T(2,128)(2,1)}), bf16[128,2,6,9,128]{4,1,3,2,0:T(2,128)(2,1)}, u32[]{:S(2)}, u32[]{:S(2)}) async-start(bf16[128,2,6,9,128]{4,1,3,2,0:T(2,128)(2,1)} %copy.128), calls=%async_computation.3 | async-start | bytes 7077888 | tf_op jit(solution)/shard_map/all_to_all | solution.py:207
  184.8 47.6 %copy-start.7 = (bf16[384,9,256]{0,2,1:T(8,128)(2,1)}, bf16[384,9,256]{0,2,1:T(8,128)(2,1)S(1)}, u32[]{:S(2)}) copy-start(bf16[384,9,256]{0,2,1:T(8,128)(2,1)S(1)} %copy.118) | copy-start | bytes 5308420
  232.3 4.4 copy-start.15
  278.7 8.0 copy-start.6
  278.7 8.0 copy-start.13
  405.2 148.3 %all-to-all-start.4 = ((f32[128,2,6,9,128]{4,1,3,2,0:T(2,128)}), f32[128,2,6,9,128]{4,1,3,2,0:T(2,128)}, u32[]{:S(2)}, u32[]{:S(2)}) async-start(f32[128,2,6,9,128]{4,1,3,2,0:T(2,128)} %copy.145), calls=%async_computation.4 | async-start | bytes 14155776 | tf_op jit(solution)/shard_map/all_to_all | solution.py:271
  553.5 10.3 copy-start.20
  553.6 372.5 %all-to-all-start.2 = ((f32[128,2,6,9,128]{4,1,3,2,0:T(2,128)}), f32[128,2,6,9,128]{4,1,3,2,0:T(2,128)}, u32[]{:S(2)}, u32[]{:S(2)}) async-start(f32[128,2,6,9,128]{4,1,3,2,0:T(2,128)} %copy.125), calls=%async_computation.2 | async-start | bytes 14155776 | tf_op jit(solution)/shard_map/all_to_all | solution.py:270
  563.8 223.8 %all-reduce.3.cloned.1.call-start = ((), (), s32[]{:S(2)}) async-start(), calls=%async_computation.5 | async-start | bytes 8257536 | tf_op jit(solution)/shard_map/psum | solution.py:284
  787.6 5.4 copy-start.28
  787.6 6.2 copy-start.27
  796.3 9.5 copy-start.45
  935.5 120.2 %copy-start.1 = (bf16[768,512]{1,0:T(8,128)(2,1)S(1)}, bf16[768,512]{1,0:T(8,128)(2,1)}, u32[]{:S(2)}) copy-start(bf16[768,512]{1,0:T(8,128)(2,1)} %param.19) | copy-start | bytes 2359300
  (36 other events, 69.4 us)
Sparse Core Ops, SparseCore 0:
  575.5 212.1 all-reduce.2
where the time goes:
time: 1080 us; the launch traced here: 1060 us
  other arithmetic  500 us (46%)
  waiting for transfers between devices  216 us (20%)
  local copies, waits for them, and re-layouts  212 us (20%)
  matrix products  64.1 us (6%)
  starting transfers between devices  34.5 us (3%)
  blocking collectives  21.3 us (2%)
  between operations  15.1 us (1%)
    psum x1, waiting for transfers between devices, local(): summed = lax.psum(totals, 'atoms')  212 us
    scatter-add x4, other arithmetic, to_slots(): slot_sums = jnp.zeros(flat_shape, jnp.float32).at[first_pos].add(first_ro...  189 us
    scatter-add x1, other arithmetic, local(): messages = jnp.zeros((block_atoms, coef_count, channels), jnp.float32).at...  119 us
    scatter-add x1, other arithmetic, local(): grad_features = jnp.zeros((block_atoms, coef_count, channels), jnp.float3...  119 us
    dot_general x4, matrix products, unrotate(): jnp.einsum('ije,eic->ejc', turned, row_block, precision=lax.Precision.HIG...  28.4 us
    reshape x2, local copies, waits for them, and re-layouts, to_slots(): return slot_sums.reshape(buffer_shape)  28.2 us
  transfers between devices with their start and end apart: 5, of which 2 were waited for; matrix products, arithmetic and copies ran while one was open for 38% of the time, Pallas kernels for 0%

commit v1 on v0

v1 whole, which is shorter than its diff:
```python
import jax
import jax.numpy as jnp
import numpy as np
from jax import lax
from jax.experimental import pallas as pl
from jax.experimental.pallas import tpu as pltpu
from jax.sharding import PartitionSpec as P

COEF_ORDER = (0, 2, 6, 3, 7, 1, 5, 8, 4)
F32 = jnp.float32
BF16 = jnp.bfloat16
CH = 112
WROWS = 64
VMEM_LIMIT = 58 * 1024 * 1024


def chunk_maps():
    coef = np.full((CH,), -1)
    row = np.full((CH,), -1)
    for line in range(CH):
        tile, at = divmod(line, 16)
        if at < 12:
            coef[line], row[line] = tile, at
        elif tile < 6:
            coef[line], row[line] = 7 + tile // 3, 4 * (tile % 3) + at - 12
    return coef, row


def spread_tables():
    coef, row = chunk_maps()
    spread = np.zeros((32, 256), np.float32)
    rows = np.full((256,), -1.0, np.float32)
    for half in range(2):
        for line in range(CH):
            if coef[line] >= 0:
                spread[16 * half + coef[line], CH * half + line] = 1.0
                rows[CH * half + line] = row[line]
    return spread, rows


def request_columns():
    cols = np.full((64,), -1)
    cols[:12] = np.arange(12)
    for j in range(3):
        cols[16 * (j + 1) + 12 : 16 * (j + 2)] = 4 * j + np.arange(4)
    return cols


def dot(a, b):
    return jnp.dot(a, b, preferred_element_type=F32)


def dot_nt(a, b):
    return lax.dot_general(a, b, (((1,), (1,)), ((), ())), preferred_element_type=F32)


def dot_tn(a, b):
    return lax.dot_general(a, b, (((0,), (0,)), ((), ())), preferred_element_type=F32)


def whole(shape):
    return pl.BlockSpec(shape, lambda *_: (0,) * len(shape))


VM = pl.BlockSpec(memory_space=pltpu.VMEM)
SM = pl.BlockSpec(memory_space=pltpu.SMEM)


def gather_body(idx_ref, eye_ref, feat_ref, out_ref):
    turned = dot_nt(eye_ref[...], idx_ref[...].astype(F32).astype(BF16))
    lane = lax.broadcasted_iota(jnp.int32, (64, 128), 1).astype(F32)
    picks = []
    for q in range(16):
        col = jnp.broadcast_to(turned[:, q : q + 1], (64, 128))
        picks.append(jnp.where(col == lane, 1.0, 0.0).astype(BF16))
    kinds = [jnp.concatenate([x[16 * v : 16 * v + 16] for x in picks], axis=0) for v in range(4)]
    for j in range(3):
        left = jnp.concatenate([kinds[0], kinds[j + 1]], axis=1)
        right = jnp.concatenate(
            [
                jnp.concatenate([feat_ref[j], feat_ref[j + 3]], axis=1),
                jnp.concatenate([feat_ref[7], feat_ref[8]], axis=1),
            ],
            axis=0,
        )
        got = dot(left, right).astype(BF16)
        out_ref[:, 16 * j : 16 * j + 16, :] = got[:, :128].reshape(16, 16, 128)
        out_ref[:, 16 * (j + 3) : 16 * (j + 4), :] = got[:, 128:].reshape(16, 16, 128)
    last = dot(kinds[0], feat_ref[6]).astype(BF16)
    out_ref[:, 96:112, :] = last.reshape(16, 16, 128)


def pick_rows(idx, eye, feat):
    peers = idx.shape[0]
    return pl.pallas_call(
        gather_body,
        grid=(peers // 16,),
        in_specs=[
            pl.BlockSpec((16, 64), lambda c: (c, 0)),
            whole((64, 64)),
            whole((9, 128, 128)),
        ],
        out_specs=pl.BlockSpec((16, CH, 128), lambda c: (c, 0, 0)),
        out_shape=jax.ShapeDtypeStruct((peers, CH, 128), BF16),
        cost_estimate=pl.CostEstimate(flops=2 * 10**9, transcendentals=0, bytes_accessed=4 * 10**6),
        name="pick_rows",
    )(idx, eye, feat)


def prep_body(ra_ref, rb_ref, sp_ref, spt_ref, rows_ref, rowst_ref, wt_ref, ws_ref, vt_ref, vs_ref):
    a = ra_ref[0]
    a_hi = a.astype(BF16)
    a_lo = (a - a_hi.astype(F32)).astype(BF16)
    lane = lax.broadcasted_iota(jnp.int32, (224, 32), 1)
    a_both = jnp.where(lane < 16, a_hi.astype(F32), a_lo.astype(F32)).astype(BF16)
    x = dot(a_both, sp_ref[...])
    rows = jnp.broadcast_to(rows_ref[0:1, :], (224, 256))
    for at, out in ((9, wt_ref), (10, ws_ref)):
        mine = jnp.broadcast_to(a[:, at : at + 1], (224, 256))
        out[0] = jnp.where(mine == rows, x, 0.0).astype(BF16)
    b = rb_ref[0]
    b_hi = b.astype(BF16)
    b_lo = (b - b_hi.astype(F32)).astype(BF16)
    line = lax.broadcasted_iota(jnp.int32, (32, 256), 0)
    b_both = jnp.where(line < 16, b_hi.astype(F32), b_lo.astype(F32)).astype(BF16)
    y = dot(spt_ref[...], b_both)
    rowst = jnp.broadcast_to(rowst_ref[:, 0:1], (224, 256))
    for at, out in ((9, vt_ref), (10, vs_ref)):
        mine = jnp.broadcast_to(b[at : at + 1, :], (224, 256))
        out[0] = jnp.where(mine == rowst, y, 0.0).astype(BF16)


def build_turns(ra, rb):
    pairs = ra.shape[0]
    spread, rows = spread_tables()
    sp = jnp.asarray(spread, BF16)
    spt = jnp.asarray(spread[:, :224].T, BF16)
    rows8 = jnp.asarray(np.tile(rows[None], (8, 1)), F32)
    rowst = jnp.asarray(np.tile(rows[:224, None], (1, 128)), F32)
    one = jax.ShapeDtypeStruct((pairs, 224, 256), BF16)
    block = pl.BlockSpec((1, 224, 256), lambda p: (p, 0, 0))
    return pl.pallas_call(
        prep_body,
        grid=(pairs,),
        in_specs=[
            pl.BlockSpec((1, 224, 32), lambda p: (p, 0, 0)),
            pl.BlockSpec((1, 32, 256), lambda p: (p, 0, 0)),
            whole((32, 256)),
            whole((224, 32)),
            whole((8, 256)),
            whole((224, 128)),
        ],
        out_specs=[block] * 4,
        out_shape=[one] * 4,
        cost_estimate=pl.CostEstimate(flops=10**9, transcendentals=0, bytes_accessed=10**7),
        name="build_turns",
    )(ra, rb, sp, spt, rows8, rowst)


def turn(w_ref, r_ref, pair, owner):
    chunk = r_ref[owner]
    right = jnp.concatenate([chunk, chunk, jnp.zeros((32, 128), BF16)], axis=0)
    return dot(w_ref[pair], right)


def turn_back(v_ref, pair, src_ref, base):
    parts = [src_ref[pl.ds(base, 24), 128 * k : 128 * k + 128] for k in range(9)]
    x = jnp.concatenate(parts + [jnp.zeros((40, 128), F32)], axis=0)
    hi = x.astype(BF16)
    lo = (x - hi.astype(F32)).astype(BF16)
    y = dot(v_ref[pair], jnp.concatenate([hi, lo], axis=1))
    y = y[:, :128] + y[:, 128:]
    return (y[:CH] + y[CH:]).astype(BF16)


def forward_body(
    own_ref, r_ref, wt_ref, ws_ref, vt_ref, vs_ref, a0_ref, a1_ref, a2_ref, b0_ref, b1_ref, b2_ref,
    out_ref, z_ref, hid_ref, gate_ref, act_ref, mix_ref,
):
    half = z_ref.shape[0] // 2
    pairs = wt_ref.shape[0]

    def lift(d, carry):
        turned = []
        for p in (2 * d, 2 * d + 1):
            turned.append((turn(ws_ref, r_ref, p, own_ref[2 * p + 1]), turn(wt_ref, r_ref, p, own_ref[2 * p])))
        (s0, t0), (s1, t1) = turned
        at = pl.multiple_of(d * 48, 16)
        for k in range(9):
            lines = slice(24 * k, 24 * k + 24)
            s = jnp.concatenate([s0[lines], s1[lines]], axis=0).astype(BF16)
            t = jnp.concatenate([t0[lines], t1[lines]], axis=0).astype(BF16)
            z_ref[pl.ds(at, 48), 256 * k : 256 * k + 128] = s
            z_ref[pl.ds(at, 48), 256 * k + 128 : 256 * k + 256] = t
            z_ref[pl.ds(half + at, 48), 256 * k : 256 * k + 128] = t
            z_ref[pl.ds(half + at, 48), 256 * k + 128 : 256 * k + 256] = s
        return carry

    lax.fori_loop(0, pairs // 2, lift, 0)

    def layer(b, carry):
        at = pl.multiple_of(b * 256, 256)
        here = pl.ds(at, 256)
        o = dot(z_ref[here, 0:768], a0_ref[...])
        gate = jax.nn.sigmoid(o[:, 384:512])
        gate_ref[here, :] = gate
        h0 = o[:, 0:128]
        hid_ref[here, 0:384] = o[:, 0:384]
        act_ref[here, 0:128] = (h0 * jax.nn.sigmoid(h0)).astype(BF16)
        for k in range(1, 3):
            cols = slice(128 * k, 128 * k + 128)
            act_ref[here, cols] = (o[:, cols] * gate).astype(BF16)
        h1 = dot(z_ref[here, 768:1792], a1_ref[...])
        hid_ref[here, 384:896] = h1
        for k in range(4):
            act_ref[here, 384 + 128 * k : 512 + 128 * k] = (h1[:, 128 * k : 128 * k + 128] * gate).astype(BF16)
        h2 = dot(z_ref[here, 1792:2304], a2_ref[...])
        hid_ref[here, 896:1152] = h2
        for k in range(2):
            act_ref[here, 896 + 128 * k : 1024 + 128 * k] = (h2[:, 128 * k : 128 * k + 128] * gate).astype(BF16)
        mix_ref[here, 0:384] = dot(act_ref[here, 0:384], b0_ref[...])
        mix_ref[here, 384:896] = dot(act_ref[here, 384:896], b1_ref[...])
        mix_ref[here, 896:1152] = dot(act_ref[here, 896:1152], b2_ref[...])
        return carry

    lax.fori_loop(0, z_ref.shape[0] // 256, layer, 0)
    out_ref[...] = jnp.zeros(out_ref.shape, BF16)

    def unlift(p, carry):
        at = pl.multiple_of(p * 24, 8)
        t = own_ref[2 * p]
        out_ref[t] = out_ref[t] + turn_back(vt_ref, p, mix_ref, at)
        s = own_ref[2 * p + 1]
        out_ref[s] = out_ref[s] + turn_back(vs_ref, p, mix_ref, half + at)
        return carry

    lax.fori_loop(0, pairs, unlift, 0)


def forward(owners, got, turns, weights, rows):
    peers = got.shape[0]
    return pl.pallas_call(
        forward_body,
        in_specs=[SM] + [VM] * 11,
        out_specs=[VM] * 5,
        out_shape=[
            jax.ShapeDtypeStruct((peers, CH, 128), BF16),
            jax.ShapeDtypeStruct((rows, 2304), BF16),
            jax.ShapeDtypeStruct((rows, 1152), F32),
            jax.ShapeDtypeStruct((rows, 128), F32),
            jax.ShapeDtypeStruct((rows, 1152), BF16),
        ],
        scratch_shapes=[pltpu.VMEM((rows, 1152), F32)],
        compiler_params=pltpu.CompilerParams(vmem_limit_bytes=VMEM_LIMIT),
        cost_estimate=pl.CostEstimate(flops=10**10, transcendentals=10**6, bytes_accessed=3 * 10**7),
        name="forward",
    )(owners, got, *turns, *weights)


def backward_body(
    own_ref, r_ref, wt_ref, ws_ref, vt_ref, vs_ref, a0_ref, a1_ref, a2_ref, b0_ref, b1_ref, b2_ref,
    z_ref, hid_ref, gate_ref, act_ref, out_ref, dmix_ref, dd_ref, gs_ref, gt_ref, *, scale,
):
    half = z_ref.shape[0] // 2
    pairs = wt_ref.shape[0]

    def lift(d, carry):
        turned = []
        for p in (2 * d, 2 * d + 1):
            turned.append((turn(wt_ref, r_ref, p, own_ref[2 * p]), turn(ws_ref, r_ref, p, own_ref[2 * p + 1])))
        (t0, s0), (t1, s1) = turned
        at = pl.multiple_of(d * 48, 16)
        for k in range(9):
            lines = slice(24 * k, 24 * k + 24)
            cols = slice(128 * k, 128 * k + 128)
            dmix_ref[pl.ds(at, 48), cols] = jnp.concatenate([t0[lines], t1[lines]], axis=0).astype(BF16)
            dmix_ref[pl.ds(half + at, 48), cols] = jnp.concatenate([s0[lines], s1[lines]], axis=0).astype(BF16)
        return carry

    lax.fori_loop(0, pairs // 2, lift, 0)

    def layer(b, carry):
        at = pl.multiple_of(b * 128, 128)
        spots = (pl.ds(at, 128), pl.ds(half + at, 128))

        def rows_of(ref, cols):
            return jnp.concatenate([ref[spot, cols] for spot in spots], axis=0)

        def put(col, value):
            value = value.astype(BF16)
            for i, spot in enumerate(spots):
                dd_ref[spot, col : col + 128] = value[128 * i : 128 * i + 128]

        gate = rows_of(gate_ref, slice(0, 128))
        dact0 = dot_nt(rows_of(dmix_ref, slice(0, 384)), b0_ref[...])
        h0 = rows_of(hid_ref, slice(0, 128))
        head = jax.nn.sigmoid(h0)
        put(0, dact0[:, 0:128] * head * (1.0 + h0 * (1.0 - head)))
        total = None

        def gated(k, piece, col):
            put(col, piece * gate)
            return piece * rows_of(hid_ref, slice(128 * k, 128 * k + 128))

        total = gated(1, dact0[:, 128:256], 128) + gated(2, dact0[:, 256:384], 256)
        dact1 = dot_nt(rows_of(dmix_ref, slice(384, 896)), b1_ref[...])
        for k in range(4):
            total = total + gated(3 + k, dact1[:, 128 * k : 128 * k + 128], 512 + 128 * k)
        dact2 = dot_nt(rows_of(dmix_ref, slice(896, 1152)), b2_ref[...])
        for k in range(2):
            total = total + gated(7 + k, dact2[:, 128 * k : 128 * k + 128], 1024 + 128 * k)
        put(384, total * gate * (1.0 - gate))

        first = 0
        for cols, w_ref, count in ((slice(0, 512), a0_ref, 3), (slice(512, 1024), a1_ref, 4), (slice(1024, 1280), a2_ref, 2)):
            dz = dot_nt(rows_of(dd_ref, cols), w_ref[...])
            for k in range(count):
                lo = dz[:, 256 * k : 256 * k + 128]
                hi = dz[:, 256 * k + 128 : 256 * k + 256]
                to = slice(128 * (first + k), 128 * (first + k) + 128)
                gs_ref[spots[0], to] = lo[:128] + hi[128:]
                gt_ref[spots[0], to] = hi[:128] + lo[128:]
            first += count
        return carry

    lax.fori_loop(0, half // 128, layer, 0)
    out_ref[...] = jnp.zeros(out_ref.shape, BF16)

    def unlift(p, carry):
        at = pl.multiple_of(p * 24, 8)
        s = own_ref[2 * p + 1]
        out_ref[s, 0:CH] = out_ref[s, 0:CH] + turn_back(vs_ref, p, gs_ref, at)
        t = own_ref[2 * p]
        out_ref[t, 0:CH] = out_ref[t, 0:CH] + turn_back(vt_ref, p, gt_ref, at)
        return carry

    lax.fori_loop(0, pairs, unlift, 0)

    def put_rows(row, value):
        value = (value * scale).astype(BF16)
        count = value.shape[0] // WROWS
        q = row // WROWS
        out_ref[q : q + count, CH : CH + WROWS, :] = value.reshape(count, WROWS, 128)

    def plain(left_ref, left_at, height, right_ref, right_cols, row):
        for c in range(height // 128):
            g = dot_tn(left_ref[:, left_at + 128 * c : left_at + 128 * c + 128], right_ref[:, right_cols])
            for n in range(g.shape[1] // 128):
                put_rows(row + n * height + 128 * c, g[:, 128 * n : 128 * n + 128])

    def folded(left_ref, left_at, height, right_ref, right_cols, row):
        width = (right_cols.stop - right_cols.start) // 2
        blocks = width // 128
        for c in range(height // 128):
            low = left_at + 128 * c
            top = dot_tn(left_ref[:, low : low + 128], right_ref[:, right_cols])
            bot = dot_tn(left_ref[:, low + height : low + height + 128], right_ref[:, right_cols])
            same = top[:, :width] + bot[:, width:]
            cross = top[:, width:] - bot[:, :width]
            for n in range(blocks):
                cols = slice(128 * n, 128 * n + 128)
                put_rows(row + n * height + 128 * c, same[:, cols])
                put_rows(row + (blocks + n) * height + 128 * c, cross[:, cols])

    plain(z_ref, 0, 768, dd_ref, slice(0, 512), 0)
    folded(z_ref, 768, 512, dd_ref, slice(512, 1024), 3072)
    folded(z_ref, 1792, 256, dd_ref, slice(1024, 1280), 5120)
    plain(act_ref, 0, 384, dmix_ref, slice(0, 384), 5632)
    folded(act_ref, 384, 256, dmix_ref, slice(384, 896), 6784)
    folded(act_ref, 896, 128, dmix_ref, slice(896, 1152), 7808)


def backward(owners, got, turns, weights, kept, scale):
    peers = got.shape[0]
    rows = kept[0].shape[0]

    def body(*refs):
        backward_body(*refs, scale=scale)

    return pl.pallas_call(
        body,
        in_specs=[SM] + [VM] * 15,
        out_specs=VM,
        out_shape=jax.ShapeDtypeStruct((peers, CH + WROWS, 128), BF16),
        scratch_shapes=[
            pltpu.VMEM((rows, 1152), BF16),
            pltpu.VMEM((rows, 1280), BF16),
            pltpu.VMEM((rows // 2, 1152), F32),
            pltpu.VMEM((rows // 2, 1152), F32),
        ],
        compiler_params=pltpu.CompilerParams(vmem_limit_bytes=VMEM_LIMIT),
        cost_estimate=pl.CostEstimate(flops=2 * 10**10, transcendentals=10**6, bytes_accessed=3 * 10**7),
        name="backward",
    )(owners, got, *turns, *weights, *kept)


def scatter_body(idx_ref, got_ref, out_ref, *rest, with_weights):
    acc_ref, last_ref = rest[-2:]

    @pl.when(pl.program_id(0) == 0)
    def _():
        acc_ref[...] = jnp.zeros(acc_ref.shape, F32)
        last_ref[...] = jnp.zeros(last_ref.shape, F32)
        if with_weights:
            rest[0][...] = jnp.zeros(rest[0].shape, F32)

    atom = lax.broadcasted_iota(jnp.int32, (128, 256), 0)
    kinds = [
        jnp.where(jnp.broadcast_to(idx_ref[v : v + 1, :], (128, 256)) == atom, 1.0, 0.0).astype(BF16)
        for v in range(4)
    ]
    tiles = [got_ref[:, 16 * t : 16 * t + 16, :].reshape(256, 128) for t in range(7)]
    acc_ref[...] += dot(kinds[0], jnp.concatenate(tiles, axis=1))
    spare = jnp.concatenate([jnp.concatenate([tiles[j], tiles[j + 3]], axis=1) for j in range(3)], axis=0)
    last_ref[...] += dot(jnp.concatenate(kinds[1:], axis=1), spare)
    if with_weights:
        rest[0][...] += jnp.sum(got_ref[:, CH : CH + WROWS, :].astype(F32), axis=0)

    @pl.when(pl.program_id(0) == pl.num_programs(0) - 1)
    def _():
        for k in range(7):
            out_ref[k] = acc_ref[:, 128 * k : 128 * k + 128].astype(out_ref.dtype)
        for k in range(2):
            out_ref[7 + k] = last_ref[:, 128 * k : 128 * k + 128].astype(out_ref.dtype)


def add_rows(idx_rows, got, dtype, with_weights):
    peers, lines, _ = got.shape

    def body(*refs):
        scatter_body(*refs, with_weights=with_weights)

    out_specs = [whole((9, 128, 128))]
    out_shape = [jax.ShapeDtypeStruct((9, 128, 128), dtype)]
    if with_weights:
        out_specs.append(whole((WROWS, 128)))
        out_shape.append(jax.ShapeDtypeStruct((WROWS, 128), F32))
    return pl.pallas_call(
        body,
        grid=(peers // 16,),
        in_specs=[
            pl.BlockSpec((8, 256), lambda c: (0, c)),
            pl.BlockSpec((16, lines, 128), lambda c: (c, 0, 0)),
        ],
        out_specs=out_specs,
        out_shape=out_shape,
        scratch_shapes=[pltpu.VMEM((128, 896), F32), pltpu.VMEM((128, 256), F32)],
        cost_estimate=pl.CostEstimate(flops=10**9, transcendentals=0, bytes_accessed=6 * 10**6),
        name="add_rows_w" if with_weights else "add_rows",
    )(idx_rows, got)


def widen_pair(w):
    upper = jnp.concatenate([w[0], w[1]], axis=1)
    lower = jnp.concatenate([-w[1], w[0]], axis=1)
    return jnp.concatenate([upper, lower], axis=0)


def exchange(x):
    return lax.all_to_all(x, "atoms", split_axis=0, concat_axis=0, tiled=True)


def local(
    features, cotangent, wigner, pair_blocks, pair_rows, edge_ends,
    first_m0, first_m1, first_m2, second_m0, second_m1, second_m2,
):
    peers = lax.axis_size("atoms")
    pairs = pair_blocks.shape[0]
    edges = edge_ends.shape[1]
    each = edges // pairs
    owners = pair_blocks.reshape(2 * pairs)
    ends = jnp.arange(2 * pairs, dtype=jnp.int32)
    slots = jnp.sum(
        jnp.logical_and(owners[:, None] == owners[None, :], ends[:, None] > ends[None, :]), axis=1
    ).astype(jnp.int32)

    end_rows = jnp.transpose(pair_rows, (2, 0, 1)).reshape(2 * pairs, 6)
    cols = request_columns()
    row_cols = jnp.concatenate([end_rows[:, max(c, 0) % 6 : max(c, 0) % 6 + 1] for c in cols], axis=1)
    col_slot = jnp.asarray(np.where(cols < 0, -1, cols // 6), jnp.int32)
    peer = jnp.arange(peers, dtype=jnp.int32)
    hit = jnp.logical_and(
        owners[None, :, None] == peer[:, None, None], slots[None, :, None] == col_slot[None, None, :]
    )
    request = jnp.sum(jnp.where(hit, row_cols[None] + 1, 0), axis=1) - 1
    asked = exchange(request)
    asked_rows = jnp.transpose(asked.reshape(peers, 4, 16), (1, 0, 2)).reshape(4, peers * 16)
    asked_rows = jnp.concatenate([asked_rows, asked_rows], axis=0)
    eye = jnp.eye(64, dtype=BF16)

    got_f = exchange(pick_rows(asked, eye, jnp.transpose(features, (1, 0, 2))))
    got_c = exchange(pick_rows(asked, eye, jnp.transpose(cotangent, (1, 0, 2))))

    turned = jnp.stack([wigner[i] for i in COEF_ORDER]).reshape(9, 9, pairs, each)
    pos = jnp.stack(
        [
            (slots.reshape(pairs, 2)[:, side, None] * 6 + edge_ends[side].reshape(pairs, each)).astype(F32)
            for side in range(2)
        ],
        axis=0,
    )
    pos = jnp.broadcast_to(pos[:, None], (2, 9, pairs, each))
    by_j = jnp.transpose(turned, (1, 0, 2, 3))
    gap5 = jnp.zeros((5, 9, pairs, each), F32)
    gap7 = jnp.zeros((7, 9, pairs, each), F32)
    table = jnp.concatenate([by_j, pos, gap5, by_j, gap7], axis=0)
    ra = jnp.transpose(table, (2, 1, 3, 0)).reshape(pairs, 9 * each, 32)
    ra = jnp.pad(ra, ((0, 0), (0, 224 - 9 * each), (0, 0)))
    rb = jnp.transpose(table, (2, 0, 1, 3)).reshape(pairs, 32, 9 * each)
    rb = jnp.pad(rb, ((0, 0), (0, 0), (0, 256 - 9 * each)))
    turns = build_turns(ra, rb)

    weights = (
        first_m0, widen_pair(first_m1), widen_pair(first_m2),
        second_m0, widen_pair(second_m1), widen_pair(second_m2),
    )
    back_m, *kept = forward(owners, got_f, turns, weights, 2 * edges)
    got_m = exchange(back_m)
    scale = float((2.0 * edges * peers) ** (-0.5))
    back_g = backward(owners, got_c, turns, weights, kept, scale)
    back_g, got_m = lax.optimization_barrier((back_g, got_m))
    got_g = exchange(back_g)
    (messages,) = add_rows(asked_rows, got_m, BF16, False)
    grad_features, w_sum = add_rows(asked_rows, got_g, F32, True)
    messages = jnp.transpose(messages, (1, 0, 2))
    grad_features = jnp.transpose(grad_features, (1, 0, 2))

    w_all = exchange(jnp.broadcast_to(w_sum.astype(BF16)[None], (peers, WROWS, 128)))
    w_all = w_all.reshape(peers * WROWS, 128).astype(F32)

    def unpack(row, parts, height, blocks):
        x = w_all[row : row + parts * blocks * height].reshape(parts, blocks, height, 128)
        return jnp.transpose(x, (0, 2, 1, 3)).reshape(parts, height, blocks * 128)

    return (
        messages,
        grad_features,
        unpack(0, 1, 768, 4)[0],
        unpack(3072, 2, 512, 2),
        unpack(5120, 2, 256, 1),
        unpack(5632, 1, 384, 3)[0],
        unpack(6784, 2, 256, 2),
        unpack(7808, 2, 128, 1),
    )


def solution(mesh):
    rows = P("atoms", None, None)
    in_specs = (
        rows, rows, P(None, None, "atoms"), P("atoms", None), P(None, None, "atoms"), P(None, "atoms"),
        P(), P(), P(), P(), P(), P(),
    )
    out_specs = (rows, rows, P(), P(), P(), P(), P(), P())
    return jax.shard_map(local, mesh=mesh, in_specs=in_specs, out_specs=out_specs, check_vma=False)
```

time: 1080 us -> 330 us (0.31); the launches traced: 1060 us -> 329 us
  other arithmetic: 500 us -> 7.29 us
  local copies, waits for them, and re-layouts: 212 us -> 26.9 us
  Pallas kernels: 0 us -> 82 us
  matrix products: 64.1 us -> 0 us
  waiting for transfers between devices: 216 us -> 165 us
  blocking collectives: 21.3 us -> 0 us
  between operations: 15.1 us -> 0.99 us
  starting transfers between devices: 34.5 us -> 46.7 us
    scatter-add x6 -> x0, other arithmetic: 428 us -> none  [the longest x4 189 us: to_slots(): slot_sums = jnp.zeros(flat_shape, jnp.float32).at[first_pos].add(first_ro...]
    psum x1 -> x0, waiting for transfers between devices: 212 us -> none  [local(): summed = lax.psum(totals, 'atoms')]
    all_to_all x4 -> x6, waiting for transfers between devices: 3.43 us -> 165 us  [exchange(): return lax.all_to_all(x, 'atoms', split_axis=0, concat_axis=0, tiled=True)]
    reshape x12 -> x7, local copies, waits for them, and re-layouts: 87.9 us -> 4.05 us  [the longest x2 1.89 us: unpack(): return jnp.transpose(x, (0, 2, 1, 3)).reshape(parts, height, blocks * 128)]
    pallas_call x0 -> x7, Pallas kernels: none -> 82 us  [the longest x1 23.4 us: backward(): pl.pallas_call(body, in_specs=[SM] + [VM] * 15, out_specs=VM, out_shape=j...]
    dot_general x26 -> x0, matrix products: 64.1 us -> none  [the longest x4 28.4 us: unrotate(): jnp.einsum('ije,eic->ejc', turned, row_block, precision=lax.Precision.HIG...]
    gather x11 -> x0, local copies, waits for them, and re-layouts: 54.8 us -> none  [the longest x1 15 us: local(): features[picked].reshape(buffer_shape)]
    gather x57 -> x0, other arithmetic: 37.5 us -> none  [the longest x27 21 us: local(): target_pos = end_slot[2 * pair_of] + edge_ends[0]]
  transfers between devices with their start and end apart: 5 -> 6, of which waited for: 2 -> 5; matrix products, arithmetic and copies ran while one was open for 38% -> 6% of each run, Pallas kernels for 0% -> 21%
where the time goes in v1:
time: 330 us; the launch traced here: 329 us
  waiting for transfers between devices  165 us (50%)
  Pallas kernels  82 us (25%)
  starting transfers between devices  46.7 us (14%)
  local copies, waits for them, and re-layouts  26.9 us (8%)
  other arithmetic  7.29 us (2%)
    all_to_all x6, waiting for transfers between devices, exchange(): return lax.all_to_all(x, 'atoms', split_axis=0, concat_axis=0, tiled=True)  165 us
    all_to_all x6, starting transfers between devices, exchange(): return lax.all_to_all(x, 'atoms', split_axis=0, concat_axis=0, tiled=True)  46.7 us
    pallas_call x1, Pallas kernels, backward(): pl.pallas_call(body, in_specs=[SM] + [VM] * 15, out_specs=VM, out_shape=j...  23.4 us
    pallas_call x1, Pallas kernels, forward(): pl.pallas_call(forward_body, in_specs=[SM] + [VM] * 11, out_specs=[VM] *...  19.1 us
    pallas_call x2, Pallas kernels, pick_rows(): pl.pallas_call(gather_body, grid=(peers // 16,), in_specs=[pl.BlockSpec((...  14 us
    pallas_call x2, Pallas kernels, add_rows(): pl.pallas_call(body, grid=(peers // 16,), in_specs=[pl.BlockSpec((8, 256)...  13.6 us
    pallas_call x1, Pallas kernels, build_turns(): pl.pallas_call(prep_body, grid=(pairs,), in_specs=[pl.BlockSpec((1, 224,...  11.9 us
  transfers between devices with their start and end apart: 6, of which 5 were waited for; matrix products, arithmetic and copies ran while one was open for 6% of the time, Pallas kernels for 21%

profile of v1, /device:TPU:1, one launch (start us, length us, event | category | flops | bytes accessed | tf_op | source)
XLA Modules:
  0.0 328.5 jit_solution(8338969633196140349)
XLA Ops:
  5.1 11.5 %all-to-all-start = ((s32[128,1,64]{2,1,0:T(1,128)}), s32[128,1,64]{2,1,0:T(1,128)S(1)}, u32[]{:S(2)}, u32[]{:S(2)}) async-start(s32[128,1,64]{2,1,0:T(1,128)} %copy.71), calls=%async_computation | async-start | bytes 131072 | tf_op jit(solution)/shard_map/all_to_all | solution.py:460
  17.2 8.7 %all-to-all-done = s32[128,1,64]{2,1,0:T(1,128)S(1)} async-done(((s32[128,1,64]{2,1,0:T(1,128)}), s32[128,1,64]{2,1,0:T(1,128)S(1)}, u32[]{:S(2)}, u32[]{:S(2)}) %all-to-all-start) | async-done | bytes 32800 | tf_op jit(solution)/shard_map/all_to_all | solution.py:460
  26.6 7.0 %pick_rows.3 = bf16[128,112,128]{2,1,0:T(8,128)(2,1)} custom-call(s32[128,64]{1,0:T(8,128)} %bitcast.131, bf16[64,64]{1,0:T(8,128)(2,1)} %fusion.eye_ref, bf16[9,128,128]{2,1,0:T(8,128)(2,1)} %bitcast.137), custom_call_target="tpu_custom_call" | custom-call | flops 2000000000 | bytes 4000000 | tf_op jit(solution)/shard_map/pick_rows/pallas_call | solution.py:95
  33.6 5.8 %all-to-all-start.2 = ((bf16[128,112,128]{2,1,0:T(8,128)(2,1)}), bf16[128,112,128]{2,1,0:T(8,128)(2,1)}, u32[]{:S(2)}, u32[]{:S(2)}) async-start(bf16[128,112,128]{2,1,0:T(8,128)(2,1)} %pick_rows.3), calls=%async_computation.2 | async-start | bytes 7340032 | tf_op jit(solution)/shard_map/all_to_all | solution.py:460
  40.0 7.0 %pick_rows.2 = bf16[128,112,128]{2,1,0:T(8,128)(2,1)} custom-call(s32[128,64]{1,0:T(8,128)} %bitcast.132, bf16[64,64]{1,0:T(8,128)(2,1)} %fusion.eye_ref, bf16[9,128,128]{2,1,0:T(8,128)(2,1)} %bitcast.138), custom_call_target="tpu_custom_call" | custom-call | flops 2000000000 | bytes 4000000 | tf_op jit(solution)/shard_map/pick_rows/pallas_call | solution.py:95
  47.1 39.2 %all-to-all-done.2.r_ref = bf16[128,112,128]{2,1,0:T(8,128)(2,1)} async-done(((bf16[128,112,128]{2,1,0:T(8,128)(2,1)}), bf16[128,112,128]{2,1,0:T(8,128)(2,1)}, u32[]{:S(2)}, u32[]{:S(2)}) %all-to-all-start.2) | async-done | bytes 3670048 | tf_op jit(solution)/shard_map/all_to_all | solution.py:460
  86.3 5.8 %all-to-all-start.1 = ((bf16[128,112,128]{2,1,0:T(8,128)(2,1)}), bf16[128,112,128]{2,1,0:T(8,128)(2,1)}, u32[]{:S(2)}, u32[]{:S(2)}) async-start(bf16[128,112,128]{2,1,0:T(8,128)(2,1)} %pick_rows.2), calls=%async_computation.1 | async-start | bytes 7340032 | tf_op jit(solution)/shard_map/all_to_all | solution.py:460
  93.6 1.4 broadcast_in_dim.22
  95.0 1.3 broadcast_in_dim.40
  96.3 1.3 broadcast_in_dim.23
  97.6 5.3 %concatenate.55 = f32[32,9,16,24]{0,3,1,2:T(8,128)S(1)} concatenate(f32[9,9,16,24]{0,3,1,2:T(8,128)S(1)} %bitcast.118, f32[2,9,16,24]{0,3,1,2:T(8,128)} %broadcast_in_dim.22, f32[5,9,16,24]{0,3,1,2:T(8,128)} %broadcast_in_dim.23, f32[9,9,16,24]{0,3,1,2:T(8,128)S(1)} %bitcast.119, f32[7,9,16,24]{0,3,1,2:T(8,128)} %broadcast_in_dim.40), dimensions={0} | concatenate | bytes 884736 | tf_op jit(solution)/shard_map/concatenate | solution.py:506
  104.3 1.4 pad.8.ra_ref
  105.8 11.9 %build_turns.1 = (bf16[16,224,256]{2,1,0:T(8,128)(2,1)}, bf16[16,224,256]{2,1,0:T(8,128)(2,1)}, bf16[16,224,256]{2,1,0:T(8,128)(2,1)}, bf16[16,224,256]{2,1,0:T(8,128)(2,1)}) custom-call(f32[16,224,32]{2,1,0:T(8,128)} %pad.8.ra_ref, f32[16,32,256]{2,1,0:T(8,128)} %pad.9.rb_ref, bf16[32,256]{1,0:T(8,128)(2,1)} %constant.24.clone.sp_ref, ...), custom_call_target="tpu_custom_call" | custom-call | flops 1000000000 | bytes 10000000 | tf_op jit(solution)/shard_map/build_turns/pallas_call | solution.py:142
  121.2 19.1 %forward.1 = (bf16[128,112,128]{2,1,0:T(8,128)(2,1)}, bf16[768,2304]{1,0:T(8,128)(2,1)}, f32[768,1152]{1,0:T(8,128)}, f32[768,128]{1,0:T(8,128)}, bf16[768,1152]{1,0:T(8,128)(2,1)}) custom-call(s32[32]{0:T(128)} %copy-done.8, bf16[128,112,128]{2,1,0:T(8,128)(2,1)} %all-to-all-done.2.r_ref, bf16[16,224,256]{2,1,0:T(8,128)(2,1)} %get-tuple-element.21.wt_ref.refs_2_, ...), custom_call_target="tpu_custom_call" | custom-call | flops 10000000000 | bytes 30000000 | tf_op jit(solution)/shard_map/forward/pallas_call | solution.py:242
  140.2 10.3 %all-to-all-start.3 = ((bf16[128,112,128]{2,1,0:T(8,128)(2,1)}), bf16[128,112,128]{2,1,0:T(8,128)(2,1)}, u32[]{:S(2)}, u32[]{:S(2)}) async-start(bf16[128,112,128]{2,1,0:T(8,128)(2,1)} %get-tuple-element.29), calls=%async_computation.3 | async-start | bytes 7340032 | tf_op jit(solution)/shard_map/all_to_all | solution.py:460
  150.5 23.4 %backward.1 = bf16[128,176,128]{2,1,0:T(8,128)(2,1)} custom-call(s32[32]{0:T(128)} %copy-done.8, bf16[128,112,128]{2,1,0:T(8,128)(2,1)} %all-to-all-done.1.refs_1_, bf16[16,224,256]{2,1,0:T(8,128)(2,1)} %get-tuple-element.21.wt_ref.refs_2_, bf16[16,224,256]{2,1,0:T(8,128)(2,1)} %get-tuple-element.22.ws_ref.refs_3_, ...), custom_call_target="tpu_custom_call" | custom-call | flops 20000000000 | bytes 30000000 | tf_op jit(solution)/shard_map/backward/pallas_call | solution.py:380
  173.9 23.4 %all-to-all-done.3.refs_1_ = bf16[128,112,128]{2,1,0:T(8,128)(2,1)} async-done(((bf16[128,112,128]{2,1,0:T(8,128)(2,1)}), bf16[128,112,128]{2,1,0:T(8,128)(2,1)}, u32[]{:S(2)}, u32[]{:S(2)}) %all-to-all-start.3) | async-done | bytes 3670048 | tf_op jit(solution)/shard_map/all_to_all | solution.py:460
  197.3 5.8 %all-to-all-start.4 = ((bf16[128,176,128]{2,1,0:T(8,128)(2,1)}), bf16[128,176,128]{2,1,0:T(8,128)(2,1)}, u32[]{:S(2)}, u32[]{:S(2)}) async-start(bf16[128,176,128]{2,1,0:T(8,128)(2,1)} %backward.1), calls=%async_computation.4 | async-start | bytes 11534336 | tf_op jit(solution)/shard_map/all_to_all | solution.py:460
  204.2 69.7 %all-to-all-done.4.refs_1_ = bf16[128,176,128]{2,1,0:T(8,128)(2,1)} async-done(((bf16[128,176,128]{2,1,0:T(8,128)(2,1)}), bf16[128,176,128]{2,1,0:T(8,128)(2,1)}, u32[]{:S(2)}, u32[]{:S(2)}) %all-to-all-start.4) | async-done | bytes 5767200 | tf_op jit(solution)/shard_map/all_to_all | solution.py:460
  273.8 7.1 %add_rows_w.1 = (f32[9,128,128]{2,1,0:T(8,128)}, f32[64,128]{1,0:T(8,128)}) custom-call(s32[8,2048]{1,0:T(8,128)} %pad_add_fusion.refs_0_, bf16[128,176,128]{2,1,0:T(8,128)(2,1)} %all-to-all-done.4.refs_1_), custom_call_target="tpu_custom_call" | custom-call | flops 1000000000 | bytes 6000000 | tf_op jit(solution)/shard_map/add_rows_w/pallas_call | solution.py:438
  281.7 1.9 broadcast_in_dim.41
  283.5 7.5 %all-to-all-start.5 = ((bf16[128,64,128]{2,1,0:T(8,128)(2,1)}), bf16[128,64,128]{2,1,0:T(8,128)(2,1)S(1)}, u32[]{:S(2)}, u32[]{:S(2)}) async-start(bf16[128,64,128]{2,1,0:T(8,128)(2,1)} %broadcast_in_dim.41), calls=%async_computation.5 | async-start | bytes 4194304 | tf_op jit(solution)/shard_map/all_to_all | solution.py:460
  291.0 6.6 %add_rows.1 = bf16[9,128,128]{2,1,0:T(8,128)(2,1)} custom-call(s32[8,2048]{1,0:T(8,128)} %pad_add_fusion.refs_0_, bf16[128,112,128]{2,1,0:T(8,128)(2,1)} %all-to-all-done.3.refs_1_), custom_call_target="tpu_custom_call" | custom-call | flops 1000000000 | bytes 6000000 | tf_op jit(solution)/shard_map/add_rows/pallas_call | solution.py:438
  297.6 23.7 %all-to-all-done.5 = bf16[128,64,128]{2,1,0:T(8,128)(2,1)S(1)} async-done(((bf16[128,64,128]{2,1,0:T(8,128)(2,1)}), bf16[128,64,128]{2,1,0:T(8,128)(2,1)S(1)}, u32[]{:S(2)}, u32[]{:S(2)}) %all-to-all-start.5) | async-done | bytes 2097184 | tf_op jit(solution)/shard_map/all_to_all | solution.py:460
  (83 shorter events, 21.6 us)
Async XLA Ops:
  1.5 32.1 %copy-start.8 = (s32[32]{0:T(128)}, s32[32]{0:T(128)S(1)}, u32[]{:S(2)}) copy-start(s32[32]{0:T(128)S(1)} %eq.56.own_ref.refs_0_) | copy-start | bytes 388
  5.1 20.8 %all-to-all-start = ((s32[128,1,64]{2,1,0:T(1,128)}), s32[128,1,64]{2,1,0:T(1,128)S(1)}, u32[]{:S(2)}, u32[]{:S(2)}) async-start(s32[128,1,64]{2,1,0:T(1,128)} %copy.71), calls=%async_computation | async-start | bytes 131072 | tf_op jit(solution)/shard_map/all_to_all | solution.py:460
  26.0 0.6 copy-start.3
  33.6 5.9 %copy-start.7 = (s32[2,384]{1,0:T(2,128)S(1)}, s32[2,384]{1,0:T(2,128)}, u32[]{:S(2)}) copy-start(s32[2,384]{1,0:T(2,128)} %param.22) | copy-start | bytes 9220
  33.6 6.4 %copy-start.5 = (f32[9,9,384]{2,1,0:T(8,128)S(1)}, f32[9,9,384]{2,1,0:T(8,128)}, u32[]{:S(2)}) copy-start(f32[9,9,384]{2,1,0:T(8,128)} %param.19) | copy-start | bytes 373252
  33.6 52.7 %all-to-all-start.2 = ((bf16[128,112,128]{2,1,0:T(8,128)(2,1)}), bf16[128,112,128]{2,1,0:T(8,128)(2,1)}, u32[]{:S(2)}, u32[]{:S(2)}) async-start(bf16[128,112,128]{2,1,0:T(8,128)(2,1)} %pick_rows.3), calls=%async_computation.2 | async-start | bytes 7340032 | tf_op jit(solution)/shard_map/all_to_all | solution.py:460
  86.3 53.9 %all-to-all-start.1 = ((bf16[128,112,128]{2,1,0:T(8,128)(2,1)}), bf16[128,112,128]{2,1,0:T(8,128)(2,1)}, u32[]{:S(2)}, u32[]{:S(2)}) async-start(bf16[128,112,128]{2,1,0:T(8,128)(2,1)} %pick_rows.2), calls=%async_computation.1 | async-start | bytes 7340032 | tf_op jit(solution)/shard_map/all_to_all | solution.py:460
  105.8 11.9 %copy-start.6 = (bf16[2,128,128]{2,1,0:T(8,128)(2,1)S(1)}, bf16[2,128,128]{2,1,0:T(8,128)(2,1)}, u32[]{:S(2)}) copy-start(bf16[2,128,128]{2,1,0:T(8,128)(2,1)} %param.28) | copy-start | bytes 196612
  105.8 12.6 %copy-start.2 = (bf16[2,256,128]{2,1,0:T(8,128)(2,1)S(1)}, bf16[2,256,128]{2,1,0:T(8,128)(2,1)}, u32[]{:S(2)}) copy-start(bf16[2,256,128]{2,1,0:T(8,128)(2,1)} %param.25) | copy-start | bytes 393220
  105.8 13.4 %copy-start.1 = (bf16[2,256,256]{2,1,0:T(8,128)(2,1)S(1)}, bf16[2,256,256]{2,1,0:T(8,128)(2,1)}, u32[]{:S(2)}) copy-start(bf16[2,256,256]{2,1,0:T(8,128)(2,1)} %param.27) | copy-start | bytes 786436
  117.7 2.4 copy-start
  140.2 57.1 %all-to-all-start.3 = ((bf16[128,112,128]{2,1,0:T(8,128)(2,1)}), bf16[128,112,128]{2,1,0:T(8,128)(2,1)}, u32[]{:S(2)}, u32[]{:S(2)}) async-start(bf16[128,112,128]{2,1,0:T(8,128)(2,1)} %get-tuple-element.29), calls=%async_computation.3 | async-start | bytes 7340032 | tf_op jit(solution)/shard_map/all_to_all | solution.py:460
  173.9 29.2 %copy-start.4 = (s32[128,1,64]{2,1,0:T(1,128)S(1)}, s32[128,1,64]{2,1,0:T(1,128)}, u32[]{:S(2)}) copy-start(s32[128,1,64]{2,1,0:T(1,128)} %copy-done.3) | copy-start | bytes 98308
  197.3 76.5 %all-to-all-start.4 = ((bf16[128,176,128]{2,1,0:T(8,128)(2,1)}), bf16[128,176,128]{2,1,0:T(8,128)(2,1)}, u32[]{:S(2)}, u32[]{:S(2)}) async-start(bf16[128,176,128]{2,1,0:T(8,128)(2,1)} %backward.1), calls=%async_computation.4 | async-start | bytes 11534336 | tf_op jit(solution)/shard_map/all_to_all | solution.py:460
  283.5 37.7 %all-to-all-start.5 = ((bf16[128,64,128]{2,1,0:T(8,128)(2,1)}), bf16[128,64,128]{2,1,0:T(8,128)(2,1)S(1)}, u32[]{:S(2)}, u32[]{:S(2)}) async-start(bf16[128,64,128]{2,1,0:T(8,128)(2,1)} %broadcast_in_dim.41), calls=%async_computation.5 | async-start | bytes 4194304 | tf_op jit(solution)/shard_map/all_to_all | solution.py:460

commit v2 on v1

--- a/solution.py
+++ b/solution.py
@@ -10,7 +10,7 @@
 F32 = jnp.float32
 BF16 = jnp.bfloat16
 CH = 112
-WROWS = 64
+WEIGHT_ROWS = 8192
 VMEM_LIMIT = 58 * 1024 * 1024
 
 
@@ -259,7 +259,7 @@
 
 def backward_body(
     own_ref, r_ref, wt_ref, ws_ref, vt_ref, vs_ref, a0_ref, a1_ref, a2_ref, b0_ref, b1_ref, b2_ref,
-    z_ref, hid_ref, gate_ref, act_ref, out_ref, dmix_ref, dd_ref, gs_ref, gt_ref, *, scale,
+    z_ref, hid_ref, gate_ref, act_ref, out_ref, wg_ref, dmix_ref, dd_ref, gs_ref, gt_ref, *, scale,
 ):
     half = z_ref.shape[0] // 2
     pairs = wt_ref.shape[0]
@@ -329,18 +329,17 @@
     def unlift(p, carry):
         at = pl.multiple_of(p * 24, 8)
         s = own_ref[2 * p + 1]
-        out_ref[s, 0:CH] = out_ref[s, 0:CH] + turn_back(vs_ref, p, gs_ref, at)
+        out_ref[s] = out_ref[s] + turn_back(vs_ref, p, gs_ref, at)
         t = own_ref[2 * p]
-        out_ref[t, 0:CH] = out_ref[t, 0:CH] + turn_back(vt_ref, p, gt_ref, at)
+        out_ref[t] = out_ref[t] + turn_back(vt_ref, p, gt_ref, at)
         return carry
 
     lax.fori_loop(0, pairs, unlift, 0)
 
     def put_rows(row, value):
-        value = (value * scale).astype(BF16)
-        count = value.shape[0] // WROWS
-        q = row // WROWS
-        out_ref[q : q + count, CH : CH + WROWS, :] = value.reshape(count, WROWS, 128)
+        wg_ref[row : row + value.shape[0], :] = (value * scale).astype(BF16)
+
+    wg_ref[8064:8192, :] = jnp.zeros((128, 128), BF16)
 
     def plain(left_ref, left_at, height, right_ref, right_cols, row):
         for c in range(height // 128):
@@ -380,8 +379,11 @@
     return pl.pallas_call(
         body,
         in_specs=[SM] + [VM] * 15,
-        out_specs=VM,
-        out_shape=jax.ShapeDtypeStruct((peers, CH + WROWS, 128), BF16),
+        out_specs=[VM, VM],
+        out_shape=[
+            jax.ShapeDtypeStruct((peers, CH, 128), BF16),
+            jax.ShapeDtypeStruct((WEIGHT_ROWS, 128), BF16),
+        ],
         scratch_shapes=[
             pltpu.VMEM((rows, 1152), BF16),
             pltpu.VMEM((rows, 1280), BF16),
@@ -394,15 +396,11 @@
     )(owners, got, *turns, *weights, *kept)
 
 
-def scatter_body(idx_ref, got_ref, out_ref, *rest, with_weights):
-    acc_ref, last_ref = rest[-2:]
-
+def scatter_body(idx_ref, got_ref, out_ref, acc_ref, last_ref):
     @pl.when(pl.program_id(0) == 0)
     def _():
         acc_ref[...] = jnp.zeros(acc_ref.shape, F32)
         last_ref[...] = jnp.zeros(last_ref.shape, F32)
-        if with_weights:
-            rest[0][...] = jnp.zeros(rest[0].shape, F32)
 
     atom = lax.broadcasted_iota(jnp.int32, (128, 256), 0)
     kinds = [
@@ -413,8 +411,6 @@
     acc_ref[...] += dot(kinds[0], jnp.concatenate(tiles, axis=1))
     spare = jnp.concatenate([jnp.concatenate([tiles[j], tiles[j + 3]], axis=1) for j in range(3)], axis=0)
     last_ref[...] += dot(jnp.concatenate(kinds[1:], axis=1), spare)
-    if with_weights:
-        rest[0][...] += jnp.sum(got_ref[:, CH : CH + WROWS, :].astype(F32), axis=0)
 
     @pl.when(pl.program_id(0) == pl.num_programs(0) - 1)
     def _():
@@ -424,30 +420,136 @@
             out_ref[7 + k] = last_ref[:, 128 * k : 128 * k + 128].astype(out_ref.dtype)
 
 
-def add_rows(idx_rows, got, dtype, with_weights):
-    peers, lines, _ = got.shape
-
-    def body(*refs):
-        scatter_body(*refs, with_weights=with_weights)
-
-    out_specs = [whole((9, 128, 128))]
-    out_shape = [jax.ShapeDtypeStruct((9, 128, 128), dtype)]
-    if with_weights:
-        out_specs.append(whole((WROWS, 128)))
-        out_shape.append(jax.ShapeDtypeStruct((WROWS, 128), F32))
-    return pl.pallas_call(
-        body,
+def add_rows(idx_rows, got, dtype):
+    peers = got.shape[0]
+    return pl.pallas_call(
+        scatter_body,
         grid=(peers // 16,),
         in_specs=[
             pl.BlockSpec((8, 256), lambda c: (0, c)),
-            pl.BlockSpec((16, lines, 128), lambda c: (c, 0, 0)),
+            pl.BlockSpec((16, CH, 128), lambda c: (c, 0, 0)),
         ],
-        out_specs=out_specs,
-        out_shape=out_shape,
+        out_specs=whole((9, 128, 128)),
+        out_shape=jax.ShapeDtypeStruct((9, 128, 128), dtype),
         scratch_shapes=[pltpu.VMEM((128, 896), F32), pltpu.VMEM((128, 256), F32)],
         cost_estimate=pl.CostEstimate(flops=10**9, transcendentals=0, bytes_accessed=6 * 10**6),
-        name="add_rows_w" if with_weights else "add_rows",
+        name="add_rows",
     )(idx_rows, got)
+
+
+def moved(x, stride, step):
+    count = lax.axis_size("atoms")
+    plan = []
+    for i in range(count):
+        digit = (i // stride) % 4
+        plan.append((i, i + ((digit + step) % 4 - digit) * stride))
+    return lax.ppermute(x, "atoms", plan)
+
+
+def swapped(x):
+    return lax.ppermute(x, "atoms", [(i, i ^ 1) for i in range(lax.axis_size("atoms"))])
+
+
+def add_and_split(place, pieces, base, scale_rows):
+    rows = pieces[-1].shape[0] // 4
+
+    def body(place_ref, *refs):
+        ins, outs = refs[: len(pieces)], refs[len(pieces) :]
+        for d in range(4):
+            at = pl.multiple_of(((place_ref[0] + d) % 4) * rows, 8)
+            total = None
+            for n, ref in enumerate(ins):
+                skip = place_ref[1] * scale_rows if (n == 0 and base) else 0
+                value = ref[pl.ds(pl.multiple_of(skip + at, 8), rows), :].astype(F32)
+                total = value if total is None else total + value
+            outs[d][...] = total
+
+    return pl.pallas_call(
+        body,
+        in_specs=[SM] + [VM] * len(pieces),
+        out_specs=[VM] * 4,
+        out_shape=[jax.ShapeDtypeStruct((rows, 128), F32)] * 4,
+        cost_estimate=pl.CostEstimate(flops=10**6, transcendentals=0, bytes_accessed=3 * 10**6),
+        name="add_and_split",
+    )(place, *pieces)
+
+
+def add_last(pieces):
+    def body(*refs):
+        total = refs[0][...]
+        for ref in refs[1:-1]:
+            total = total + ref[...]
+        refs[-1][...] = total.astype(BF16)
+
+    return pl.pallas_call(
+        body,
+        in_specs=[VM] * len(pieces),
+        out_specs=VM,
+        out_shape=jax.ShapeDtypeStruct(pieces[0].shape, BF16),
+        name="add_last",
+    )(*pieces)
+
+
+def join(place, pieces):
+    rows = pieces[0].shape[0]
+
+    def body(place_ref, *refs):
+        for d in range(4):
+            at = pl.multiple_of(((place_ref[0] + 4 - d) % 4) * rows, 16)
+            refs[4][pl.ds(at, rows), :] = refs[d][...]
+
+    return pl.pallas_call(
+        body,
+        in_specs=[SM] + [VM] * 4,
+        out_specs=VM,
+        out_shape=jax.ShapeDtypeStruct((4 * rows, 128), BF16),
+        name="join",
+    )(place, *pieces)
+
+
+WEIGHT_PARTS = (
+    (0, 1, 768, 4), (3072, 2, 512, 2), (5120, 2, 256, 1), (5632, 1, 384, 3), (6784, 2, 256, 2), (7808, 2, 128, 1),
+)
+
+
+def unpack(core, mine, other):
+    half = mine.shape[0]
+
+    def body(core_ref, mine_ref, other_ref, *refs):
+        outs, all_ref = refs[:-1], refs[-1]
+        all_ref[pl.ds(pl.multiple_of(core_ref[0] * half, 16), half), :] = mine_ref[...]
+        all_ref[pl.ds(pl.multiple_of((1 - core_ref[0]) * half, 16), half), :] = other_ref[...]
+        for out, (row, parts, height, blocks) in zip(outs, WEIGHT_PARTS):
+            for p in range(parts):
+                for n in range(blocks):
+                    low = row + (p * blocks + n) * height
+                    out[p, :, 128 * n : 128 * n + 128] = all_ref[low : low + height, :].astype(F32)
+
+    return pl.pallas_call(
+        body,
+        in_specs=[SM, VM, VM],
+        out_specs=[VM] * 6,
+        out_shape=[jax.ShapeDtypeStruct((parts, height, 128 * blocks), F32) for _, parts, height, blocks in WEIGHT_PARTS],
+        scratch_shapes=[pltpu.VMEM((2 * half, 128), BF16)],
+        compiler_params=pltpu.CompilerParams(vmem_limit_bytes=VMEM_LIMIT // 2),
+        name="unpack",
+    )(core, mine, other)
+
+
+def sum_weights(grads):
+    me = lax.axis_index("atoms").astype(jnp.int32)
+    core = me % 2
+    places = {stride: jnp.stack([(me // stride) % 4, core]) for stride in (32, 8, 2)}
+    half = WEIGHT_ROWS // 2
+    sent = lax.dynamic_slice_in_dim(grads, (1 - core) * half, half, axis=0)
+    pieces = [grads, swapped(sent)]
+    for stride in (32, 8, 2):
+        parts = add_and_split(places[stride], pieces, stride == 32, half)
+        pieces = [parts[0]] + [moved(parts[d], stride, d) for d in (1, 2, 3)]
+    value = add_last(pieces)
+    for stride in (2, 8, 32):
+        value = join(places[stride], [value] + [moved(value, stride, d) for d in (1, 2, 3)])
+    return unpack(jnp.stack([core, core]), value, swapped(value))
 
 
 def widen_pair(w):
@@ -517,31 +619,13 @@
     back_m, *kept = forward(owners, got_f, turns, weights, 2 * edges)
     got_m = exchange(back_m)
     scale = float((2.0 * edges * peers) ** (-0.5))
-    back_g = backward(owners, got_c, turns, weights, kept, scale)
+    back_g, grads = backward(owners, got_c, turns, weights, kept, scale)
     back_g, got_m = lax.optimization_barrier((back_g, got_m))
     got_g = exchange(back_g)
-    (messages,) = add_rows(asked_rows, got_m, BF16, False)
-    grad_features, w_sum = add_rows(asked_rows, got_g, F32, True)
-    messages = jnp.transpose(messages, (1, 0, 2))
-    grad_features = jnp.transpose(grad_features, (1, 0, 2))
-
-    w_all = exchange(jnp.broadcast_to(w_sum.astype(BF16)[None], (peers, WROWS, 128)))
-    w_all = w_all.reshape(peers * WROWS, 128).astype(F32)
-
-    def unpack(row, parts, height, blocks):
-        x = w_all[row : row + parts * blocks * height].reshape(parts, blocks, height, 128)
-        return jnp.transpose(x, (0, 2, 1, 3)).reshape(parts, height, blocks * 128)
-
-    return (
-        messages,
-        grad_features,
-        unpack(0, 1, 768, 4)[0],
-        unpack(3072, 2, 512, 2),
-        unpack(5120, 2, 256, 1),
-        unpack(5632, 1, 384, 3)[0],
-        unpack(6784, 2, 256, 2),
-        unpack(7808, 2, 128, 1),
-    )
+    messages = jnp.transpose(add_rows(asked_rows, got_m, BF16), (1, 0, 2))
+    w = sum_weights(grads)
+    grad_features = jnp.transpose(add_rows(asked_rows, got_g, F32), (1, 0, 2))
+    return (messages, grad_features, w[0][0], w[1], w[2], w[3][0], w[4], w[5])
 
 
 def solution(mesh):

time: 330 us -> 354 us (1.073)
  starting transfers between devices: 46.7 us -> 71.3 us
  waiting for transfers between devices: 165 us -> 149 us
  Pallas kernels: 82 us -> 97.2 us
    all_to_all x6 -> x5, waiting for transfers between devices: 165 us -> 72.7 us  [exchange(): return lax.all_to_all(x, 'atoms', split_axis=0, concat_axis=0, tiled=True)]
    ppermute x0 -> x20, waiting for transfers between devices: none -> 76.2 us  [the longest x18 73.1 us: moved(): return lax.ppermute(x, 'atoms', plan)]
    ppermute x0 -> x20, starting transfers between devices: none -> 32 us  [the longest x18 23.4 us: moved(): return lax.ppermute(x, 'atoms', plan)]
    pallas_call x3 -> x11, Pallas kernels: 37 us -> 52.2 us  [the longest x1 21.9 us: backward(): pl.pallas_call(body, in_specs=[SM] + [VM] * 15, out_specs=[VM, VM], out_s...]
    all_to_all x6 -> x5, starting transfers between devices: 46.7 us -> 39.3 us  [exchange(): return lax.all_to_all(x, 'atoms', split_axis=0, concat_axis=0, tiled=True)]
    unnamed x29 -> x69, local copies, waits for them, and re-layouts: 3.77 us -> 8.04 us
  transfers between devices with their start and end apart: 6 -> 25, of which waited for: 5 -> 19; matrix products, arithmetic and copies ran while one was open for 6% -> 6% of each run, Pallas kernels for 21% -> 24%
where the time goes in v2:
time: 354 us; the launch traced here: 351 us
  waiting for transfers between devices  149 us (42%)
  Pallas kernels  97.2 us (27%)
  starting transfers between devices  71.3 us (20%)
  local copies, waits for them, and re-layouts  24.6 us (7%)
  other arithmetic  8.46 us (2%)
    ppermute x18, waiting for transfers between devices, moved(): return lax.ppermute(x, 'atoms', plan)  73.1 us
    all_to_all x5, waiting for transfers between devices, exchange(): return lax.all_to_all(x, 'atoms', split_axis=0, concat_axis=0, tiled=True)  72.7 us
    all_to_all x5, starting transfers between devices, exchange(): return lax.all_to_all(x, 'atoms', split_axis=0, concat_axis=0, tiled=True)  39.3 us
    ppermute x18, starting transfers between devices, moved(): return lax.ppermute(x, 'atoms', plan)  23.4 us
    pallas_call x1, Pallas kernels, backward(): pl.pallas_call(body, in_specs=[SM] + [VM] * 15, out_specs=[VM, VM], out_s...  21.9 us
    pallas_call x1, Pallas kernels, forward(): pl.pallas_call(forward_body, in_specs=[SM] + [VM] * 11, out_specs=[VM] *...  19.1 us
    pallas_call x2, Pallas kernels, pick_rows(): pl.pallas_call(gather_body, grid=(peers // 16,), in_specs=[pl.BlockSpec((...  14.1 us
    pallas_call x2, Pallas kernels, add_rows(): pl.pallas_call(scatter_body, grid=(peers // 16,), in_specs=[pl.BlockSpec(...  13.2 us
  transfers between devices with their start and end apart: 25, of which 19 were waited for; matrix products, arithmetic and copies ran while one was open for 6% of the time, Pallas kernels for 24%

profile of v2, /device:TPU:1, one launch (start us, length us, event | category | flops | bytes accessed | tf_op | source)
XLA Modules:
  0.0 351.5 jit_solution(11641906359897772830)
XLA Ops:
  5.1 11.5 %all-to-all-start = ((s32[128,1,64]{2,1,0:T(1,128)}), s32[128,1,64]{2,1,0:T(1,128)S(1)}, u32[]{:S(2)}, u32[]{:S(2)}) async-start(s32[128,1,64]{2,1,0:T(1,128)} %copy.46), calls=%async_computation | async-start | bytes 131072 | tf_op jit(solution)/shard_map/all_to_all | solution.py:562
  17.2 8.7 %all-to-all-done = s32[128,1,64]{2,1,0:T(1,128)S(1)} async-done(((s32[128,1,64]{2,1,0:T(1,128)}), s32[128,1,64]{2,1,0:T(1,128)S(1)}, u32[]{:S(2)}, u32[]{:S(2)}) %all-to-all-start) | async-done | bytes 32800 | tf_op jit(solution)/shard_map/all_to_all | solution.py:562
  26.6 7.0 %pick_rows.3 = bf16[128,112,128]{2,1,0:T(8,128)(2,1)} custom-call(s32[128,64]{1,0:T(8,128)} %bitcast.100, bf16[64,64]{1,0:T(8,128)(2,1)} %fusion.eye_ref, bf16[9,128,128]{2,1,0:T(8,128)(2,1)} %bitcast.106), custom_call_target="tpu_custom_call" | custom-call | flops 2000000000 | bytes 4000000 | tf_op jit(solution)/shard_map/pick_rows/pallas_call | solution.py:95
  33.6 5.8 %all-to-all-start.2 = ((bf16[128,112,128]{2,1,0:T(8,128)(2,1)}), bf16[128,112,128]{2,1,0:T(8,128)(2,1)}, u32[]{:S(2)}, u32[]{:S(2)}) async-start(bf16[128,112,128]{2,1,0:T(8,128)(2,1)} %pick_rows.3), calls=%async_computation.2 | async-start | bytes 7340032 | tf_op jit(solution)/shard_map/all_to_all | solution.py:562
  40.1 7.0 %pick_rows.2 = bf16[128,112,128]{2,1,0:T(8,128)(2,1)} custom-call(s32[128,64]{1,0:T(8,128)} %bitcast.101, bf16[64,64]{1,0:T(8,128)(2,1)} %fusion.eye_ref, bf16[9,128,128]{2,1,0:T(8,128)(2,1)} %bitcast.107), custom_call_target="tpu_custom_call" | custom-call | flops 2000000000 | bytes 4000000 | tf_op jit(solution)/shard_map/pick_rows/pallas_call | solution.py:95
  47.1 39.2 %all-to-all-done.2.r_ref = bf16[128,112,128]{2,1,0:T(8,128)(2,1)} async-done(((bf16[128,112,128]{2,1,0:T(8,128)(2,1)}), bf16[128,112,128]{2,1,0:T(8,128)(2,1)}, u32[]{:S(2)}, u32[]{:S(2)}) %all-to-all-start.2) | async-done | bytes 3670048 | tf_op jit(solution)/shard_map/all_to_all | solution.py:562
  86.3 5.8 %all-to-all-start.1 = ((bf16[128,112,128]{2,1,0:T(8,128)(2,1)}), bf16[128,112,128]{2,1,0:T(8,128)(2,1)}, u32[]{:S(2)}, u32[]{:S(2)}) async-start(bf16[128,112,128]{2,1,0:T(8,128)(2,1)} %pick_rows.2), calls=%async_computation.1 | async-start | bytes 7340032 | tf_op jit(solution)/shard_map/all_to_all | solution.py:562
  97.7 5.3 %concatenate.55 = f32[32,9,16,24]{0,3,1,2:T(8,128)S(1)} concatenate(f32[9,9,16,24]{0,3,1,2:T(8,128)S(1)} %bitcast.96, f32[2,9,16,24]{0,3,1,2:T(8,128)} %broadcast_in_dim.32, f32[5,9,16,24]{0,3,1,2:T(8,128)} %broadcast_in_dim.33, f32[9,9,16,24]{0,3,1,2:T(8,128)S(1)} %bitcast.97, f32[7,9,16,24]{0,3,1,2:T(8,128)} %broadcast_in_dim.34), dimensions={0} | concatenate | bytes 884736 | tf_op jit(solution)/shard_map/concatenate | solution.py:608
  106.0 11.9 %build_turns.1 = (bf16[16,224,256]{2,1,0:T(8,128)(2,1)}, bf16[16,224,256]{2,1,0:T(8,128)(2,1)}, bf16[16,224,256]{2,1,0:T(8,128)(2,1)}, bf16[16,224,256]{2,1,0:T(8,128)(2,1)}) custom-call(f32[16,224,32]{2,1,0:T(8,128)} %pad.8.ra_ref, f32[16,32,256]{2,1,0:T(8,128)} %pad.9.rb_ref, bf16[32,256]{1,0:T(8,128)(2,1)} %constant.93.clone.sp_ref, ...), custom_call_target="tpu_custom_call" | custom-call | flops 1000000000 | bytes 10000000 | tf_op jit(solution)/shard_map/build_turns/pallas_call | solution.py:142
  121.3 19.1 %forward.1 = (bf16[128,112,128]{2,1,0:T(8,128)(2,1)}, bf16[768,2304]{1,0:T(8,128)(2,1)}, f32[768,1152]{1,0:T(8,128)}, f32[768,128]{1,0:T(8,128)}, bf16[768,1152]{1,0:T(8,128)(2,1)}) custom-call(s32[32]{0:T(128)} %copy-done.29, bf16[128,112,128]{2,1,0:T(8,128)(2,1)} %all-to-all-done.2.r_ref, bf16[16,224,256]{2,1,0:T(8,128)(2,1)} %get-tuple-element.39.wt_ref.refs_2_, ...), custom_call_target="tpu_custom_call" | custom-call | flops 10000000000 | bytes 30000000 | tf_op jit(solution)/shard_map/forward/pallas_call | solution.py:242
  140.4 10.3 %all-to-all-start.3 = ((bf16[128,112,128]{2,1,0:T(8,128)(2,1)}), bf16[128,112,128]{2,1,0:T(8,128)(2,1)}, u32[]{:S(2)}, u32[]{:S(2)}) async-start(bf16[128,112,128]{2,1,0:T(8,128)(2,1)} %get-tuple-element.48), calls=%async_computation.3 | async-start | bytes 7340032 | tf_op jit(solution)/shard_map/all_to_all | solution.py:562
  150.8 21.9 %backward.1 = (bf16[128,112,128]{2,1,0:T(8,128)(2,1)}, bf16[8192,128]{1,0:T(8,128)(2,1)}) custom-call(s32[32]{0:T(128)} %copy-done.29, bf16[128,112,128]{2,1,0:T(8,128)(2,1)} %all-to-all-done.1.refs_1_, bf16[16,224,256]{2,1,0:T(8,128)(2,1)} %get-tuple-element.39.wt_ref.refs_2_, bf16[16,224,256]{2,1,0:T(8,128)(2,1)} %get-tuple-element.40.ws_ref.refs_3_, ...), custom_call_target="tpu_custom_call" | custom-call | flops 20000000000 | bytes 30000000 | tf_op jit(solution)/shard_map/backward/pallas_call | solution.py:379
  172.7 24.8 %all-to-all-done.3.got_ref = bf16[128,112,128]{2,1,0:T(8,128)(2,1)} async-done(((bf16[128,112,128]{2,1,0:T(8,128)(2,1)}), bf16[128,112,128]{2,1,0:T(8,128)(2,1)}, u32[]{:S(2)}, u32[]{:S(2)}) %all-to-all-start.3) | async-done | bytes 3670048 | tf_op jit(solution)/shard_map/all_to_all | solution.py:562
  197.5 5.9 %all-to-all-start.4 = ((bf16[128,112,128]{2,1,0:T(8,128)(2,1)}), bf16[128,112,128]{2,1,0:T(8,128)(2,1)}, u32[]{:S(2)}, u32[]{:S(2)}) async-start(bf16[128,112,128]{2,1,0:T(8,128)(2,1)} %get-tuple-element.50), calls=%async_computation.4 | async-start | bytes 7340032 | tf_op jit(solution)/shard_map/all_to_all | solution.py:562
  208.1 3.3 add_and_split.3
  216.3 41.0 %collective-permute-done.1.refs_1_ = f32[1024,128]{1,0:T(8,128)S(1)} collective-permute-done((f32[1024,128]{1,0:T(8,128)}, f32[1024,128]{1,0:T(8,128)S(1)}, u32[]{:S(2)}, u32[]{:S(2)}) %collective-permute-start.1) | collective-permute-done | bytes 524320 | tf_op jit(solution)/shard_map/ppermute | solution.py:446
  257.2 11.9 %collective-permute-done.2.refs_2_ = f32[1024,128]{1,0:T(8,128)S(1)} collective-permute-done((f32[1024,128]{1,0:T(8,128)}, f32[1024,128]{1,0:T(8,128)S(1)}, u32[]{:S(2)}, u32[]{:S(2)}) %collective-permute-start.2) | collective-permute-done | bytes 524320 | tf_op jit(solution)/shard_map/ppermute | solution.py:446
  272.5 2.8 collective-permute-start.5
  278.0 3.5 %collective-permute-done.5.refs_2_ = f32[256,128]{1,0:T(8,128)S(1)} collective-permute-done((f32[256,128]{1,0:T(8,128)}, f32[256,128]{1,0:T(8,128)S(1)}, u32[]{:S(2)}, u32[]{:S(2)}) %collective-permute-start.5) | collective-permute-done | bytes 131104 | tf_op jit(solution)/shard_map/ppermute | solution.py:446
  314.1 6.8 %collective-permute-done.16.refs_1_ = bf16[1024,128]{1,0:T(8,128)(2,1)S(1)} collective-permute-done((bf16[1024,128]{1,0:T(8,128)(2,1)}, bf16[1024,128]{1,0:T(8,128)(2,1)S(1)}, u32[]{:S(2)}, u32[]{:S(2)}) %collective-permute-start.16) | collective-permute-done | bytes 262176 | tf_op jit(solution)/shard_map/ppermute | solution.py:446
  324.7 7.2 %collective-permute-start.19 = (bf16[4096,128]{1,0:T(8,128)(2,1)}, bf16[4096,128]{1,0:T(8,128)(2,1)S(1)}, u32[]{:S(2)}, u32[]{:S(2)}) collective-permute-start(bf16[4096,128]{1,0:T(8,128)(2,1)} %join.5.mine_ref), channel_id=1, source_target_pairs={{0,1},{1,0},{2,3},{3,2},{4,5},{5,4},{6,7},{7,6},{8,9},{9,8},{10,11... | collective-permute-start | bytes 3145736 | tf_op jit(solution)/shard_map/ppermute | solution.py:450
  335.6 2.7 unpack.1
  338.3 6.5 %add_rows.2 = bf16[9,128,128]{2,1,0:T(8,128)(2,1)} custom-call(s32[8,2048]{1,0:T(8,128)} %pad_add_fusion.idx_ref, bf16[128,112,128]{2,1,0:T(8,128)(2,1)} %all-to-all-done.3.got_ref), custom_call_target="tpu_custom_call" | custom-call | flops 1000000000 | bytes 6000000 | tf_op jit(solution)/shard_map/add_rows/pallas_call | solution.py:425
  344.8 6.7 %add_rows.3 = f32[9,128,128]{2,1,0:T(8,128)} custom-call(s32[8,2048]{1,0:T(8,128)} %pad_add_fusion.idx_ref, bf16[128,112,128]{2,1,0:T(8,128)(2,1)} %all-to-all-done.4.got_ref), custom_call_target="tpu_custom_call" | custom-call | flops 1000000000 | bytes 6000000 | tf_op jit(solution)/shard_map/add_rows/pallas_call | solution.py:425
  (162 shorter events, 73.8 us)
Async XLA Ops:
  5.1 20.8 %all-to-all-start = ((s32[128,1,64]{2,1,0:T(1,128)}), s32[128,1,64]{2,1,0:T(1,128)S(1)}, u32[]{:S(2)}, u32[]{:S(2)}) async-start(s32[128,1,64]{2,1,0:T(1,128)} %copy.46), calls=%async_computation | async-start | bytes 131072 | tf_op jit(solution)/shard_map/all_to_all | solution.py:562
  33.6 52.7 %all-to-all-start.2 = ((bf16[128,112,128]{2,1,0:T(8,128)(2,1)}), bf16[128,112,128]{2,1,0:T(8,128)(2,1)}, u32[]{:S(2)}, u32[]{:S(2)}) async-start(bf16[128,112,128]{2,1,0:T(8,128)(2,1)} %pick_rows.3), calls=%async_computation.2 | async-start | bytes 7340032 | tf_op jit(solution)/shard_map/all_to_all | solution.py:562
  86.3 54.1 %all-to-all-start.1 = ((bf16[128,112,128]{2,1,0:T(8,128)(2,1)}), bf16[128,112,128]{2,1,0:T(8,128)(2,1)}, u32[]{:S(2)}, u32[]{:S(2)}) async-start(bf16[128,112,128]{2,1,0:T(8,128)(2,1)} %pick_rows.2), calls=%async_computation.1 | async-start | bytes 7340032 | tf_op jit(solution)/shard_map/all_to_all | solution.py:562
  140.4 57.1 %all-to-all-start.3 = ((bf16[128,112,128]{2,1,0:T(8,128)(2,1)}), bf16[128,112,128]{2,1,0:T(8,128)(2,1)}, u32[]{:S(2)}, u32[]{:S(2)}) async-start(bf16[128,112,128]{2,1,0:T(8,128)(2,1)} %get-tuple-element.48), calls=%async_computation.3 | async-start | bytes 7340032 | tf_op jit(solution)/shard_map/all_to_all | solution.py:562
  197.5 147.3 %all-to-all-start.4 = ((bf16[128,112,128]{2,1,0:T(8,128)(2,1)}), bf16[128,112,128]{2,1,0:T(8,128)(2,1)}, u32[]{:S(2)}, u32[]{:S(2)}) async-start(bf16[128,112,128]{2,1,0:T(8,128)(2,1)} %get-tuple-element.50), calls=%async_computation.4 | async-start | bytes 7340032 | tf_op jit(solution)/shard_map/all_to_all | solution.py:562
  203.5 3.6 %collective-permute-start = (bf16[4096,128]{1,0:T(8,128)(2,1)S(1)}, bf16[4096,128]{1,0:T(8,128)(2,1)S(1)}, u32[]{:S(2)}, u32[]{:S(2)}) collective-permute-start(bf16[4096,128]{1,0:T(8,128)(2,1)S(1)} %constant_dynamic-slice_fusion), channel_id=1, source_target_pairs={{0,1},{1,0},{2,3},{3,2},{4,5},{5,4},{6,7},{7,6},{8,9},{9,8},{10,11... | collective-permute-start | bytes 3145736 | tf_op jit(solution)/shard_map/ppermute | solution.py:450
  211.4 45.8 %collective-permute-start.1 = (f32[1024,128]{1,0:T(8,128)}, f32[1024,128]{1,0:T(8,128)S(1)}, u32[]{:S(2)}, u32[]{:S(2)}) collective-permute-start(f32[1024,128]{1,0:T(8,128)} %get-tuple-element.53), channel_id=1, source_target_pairs={{0,32},{1,33},{2,34},{3,35},{4,36},{5,37},{6,38},{7,39},{8,40},{9,... | collective-permute-start | bytes 1572872 | tf_op jit(solution)/shard_map/ppermute | solution.py:446
  212.0 57.1 %collective-permute-start.2 = (f32[1024,128]{1,0:T(8,128)}, f32[1024,128]{1,0:T(8,128)S(1)}, u32[]{:S(2)}, u32[]{:S(2)}) collective-permute-start(f32[1024,128]{1,0:T(8,128)} %get-tuple-element.54), channel_id=1, source_target_pairs={{0,64},{1,65},{2,66},{3,67},{4,68},{5,69},{6,70},{7,71},{8,72},{9,... | collective-permute-start | bytes 1572872 | tf_op jit(solution)/shard_map/ppermute | solution.py:446
  214.5 54.6 %collective-permute-start.3 = (f32[1024,128]{1,0:T(8,128)}, f32[1024,128]{1,0:T(8,128)S(1)}, u32[]{:S(2)}, u32[]{:S(2)}) collective-permute-start(f32[1024,128]{1,0:T(8,128)} %get-tuple-element.55), channel_id=1, source_target_pairs={{0,96},{1,97},{2,98},{3,99},{4,100},{5,101},{6,102},{7,103},{8,104... | collective-permute-start | bytes 1572872 | tf_op jit(solution)/shard_map/ppermute | solution.py:446
  272.5 5.6 %collective-permute-start.4 = (f32[256,128]{1,0:T(8,128)}, f32[256,128]{1,0:T(8,128)S(1)}, u32[]{:S(2)}, u32[]{:S(2)}) collective-permute-start(f32[256,128]{1,0:T(8,128)} %get-tuple-element.57), channel_id=1, source_target_pairs={{0,8},{1,9},{2,10},{3,11},{4,12},{5,13},{6,14},{7,15},{8,16},{9,17... | collective-permute-start | bytes 393224 | tf_op jit(solution)/shard_map/ppermute | solution.py:446
  272.5 9.0 %collective-permute-start.5 = (f32[256,128]{1,0:T(8,128)}, f32[256,128]{1,0:T(8,128)S(1)}, u32[]{:S(2)}, u32[]{:S(2)}) collective-permute-start(f32[256,128]{1,0:T(8,128)} %get-tuple-element.58), channel_id=1, source_target_pairs={{0,16},{1,17},{2,18},{3,19},{4,20},{5,21},{6,22},{7,23},{8,24},{9,... | collective-permute-start | bytes 393224 | tf_op jit(solution)/shard_map/ppermute | solution.py:446
  275.4 6.2 %collective-permute-start.6 = (f32[256,128]{1,0:T(8,128)}, f32[256,128]{1,0:T(8,128)S(1)}, u32[]{:S(2)}, u32[]{:S(2)}) collective-permute-start(f32[256,128]{1,0:T(8,128)} %get-tuple-element.59), channel_id=1, source_target_pairs={{0,24},{1,25},{2,26},{3,27},{4,28},{5,29},{6,30},{7,31},{8,0},{9,1... | collective-permute-start | bytes 393224 | tf_op jit(solution)/shard_map/ppermute | solution.py:446
  284.0 4.7 %collective-permute-start.7 = (f32[64,128]{1,0:T(8,128)}, f32[64,128]{1,0:T(8,128)S(1)}, u32[]{:S(2)}, u32[]{:S(2)}) collective-permute-start(f32[64,128]{1,0:T(8,128)} %get-tuple-element.61), channel_id=1, source_target_pairs={{0,2},{1,3},{2,4},{3,5},{4,6},{5,7},{6,0},{7,1},{8,10},{9,11},{10,... | collective-permute-start | bytes 98312 | tf_op jit(solution)/shard_map/ppermute | solution.py:446
  285.8 4.5 %collective-permute-start.8 = (f32[64,128]{1,0:T(8,128)}, f32[64,128]{1,0:T(8,128)S(1)}, u32[]{:S(2)}, u32[]{:S(2)}) collective-permute-start(f32[64,128]{1,0:T(8,128)} %get-tuple-element.62), channel_id=1, source_target_pairs={{0,4},{1,5},{2,6},{3,7},{4,0},{5,1},{6,2},{7,3},{8,12},{9,13},{10,... | collective-permute-start | bytes 98312 | tf_op jit(solution)/shard_map/ppermute | solution.py:446
  288.1 3.3 collective-permute-start.9
  293.4 4.0 %collective-permute-start.10 = (bf16[64,128]{1,0:T(8,128)(2,1)}, bf16[64,128]{1,0:T(8,128)(2,1)S(1)}, u32[]{:S(2)}, u32[]{:S(2)}) collective-permute-start(bf16[64,128]{1,0:T(8,128)(2,1)} %add_last.1.refs_0_), channel_id=1, source_target_pairs={{0,2},{1,3},{2,4},{3,5},{4,6},{5,7},{6,0},{7,1},{8,10},{9,11},{10,... | collective-permute-start | bytes 49160 | tf_op jit(solution)/shard_map/ppermute | solution.py:446
  293.4 4.3 %collective-permute-start.11 = (bf16[64,128]{1,0:T(8,128)(2,1)}, bf16[64,128]{1,0:T(8,128)(2,1)S(1)}, u32[]{:S(2)}, u32[]{:S(2)}) collective-permute-start(bf16[64,128]{1,0:T(8,128)(2,1)} %add_last.1.refs_0_), channel_id=1, source_target_pairs={{0,4},{1,5},{2,6},{3,7},{4,0},{5,1},{6,2},{7,3},{8,12},{9,13},{10,... | collective-permute-start | bytes 49160 | tf_op jit(solution)/shard_map/ppermute | solution.py:446
  301.0 5.5 %collective-permute-start.13 = (bf16[256,128]{1,0:T(8,128)(2,1)}, bf16[256,128]{1,0:T(8,128)(2,1)S(1)}, u32[]{:S(2)}, u32[]{:S(2)}) collective-permute-start(bf16[256,128]{1,0:T(8,128)(2,1)} %join.3.refs_0_), channel_id=1, source_target_pairs={{0,8},{1,9},{2,10},{3,11},{4,12},{5,13},{6,14},{7,15},{8,16},{9,17... | collective-permute-start | bytes 196616 | tf_op jit(solution)/shard_map/ppermute | solution.py:446
  303.5 4.9 %collective-permute-start.14 = (bf16[256,128]{1,0:T(8,128)(2,1)}, bf16[256,128]{1,0:T(8,128)(2,1)S(1)}, u32[]{:S(2)}, u32[]{:S(2)}) collective-permute-start(bf16[256,128]{1,0:T(8,128)(2,1)} %join.3.refs_0_), channel_id=1, source_target_pairs={{0,16},{1,17},{2,18},{3,19},{4,20},{5,21},{6,22},{7,23},{8,24},{9,... | collective-permute-start | bytes 196616 | tf_op jit(solution)/shard_map/ppermute | solution.py:446
  305.8 3.3 collective-permute-start.15
  311.5 9.5 %collective-permute-start.16 = (bf16[1024,128]{1,0:T(8,128)(2,1)}, bf16[1024,128]{1,0:T(8,128)(2,1)S(1)}, u32[]{:S(2)}, u32[]{:S(2)}) collective-permute-start(bf16[1024,128]{1,0:T(8,128)(2,1)} %join.4.refs_0_), channel_id=1, source_target_pairs={{0,32},{1,33},{2,34},{3,35},{4,36},{5,37},{6,38},{7,39},{8,40},{9,... | collective-permute-start | bytes 786440 | tf_op jit(solution)/shard_map/ppermute | solution.py:446
  311.5 9.5 %collective-permute-start.17 = (bf16[1024,128]{1,0:T(8,128)(2,1)}, bf16[1024,128]{1,0:T(8,128)(2,1)S(1)}, u32[]{:S(2)}, u32[]{:S(2)}) collective-permute-start(bf16[1024,128]{1,0:T(8,128)(2,1)} %join.4.refs_0_), channel_id=1, source_target_pairs={{0,64},{1,65},{2,66},{3,67},{4,68},{5,69},{6,70},{7,71},{8,72},{9,... | collective-permute-start | bytes 786440 | tf_op jit(solution)/shard_map/ppermute | solution.py:446
  313.0 8.6 %collective-permute-start.18 = (bf16[1024,128]{1,0:T(8,128)(2,1)}, bf16[1024,128]{1,0:T(8,128)(2,1)S(1)}, u32[]{:S(2)}, u32[]{:S(2)}) collective-permute-start(bf16[1024,128]{1,0:T(8,128)(2,1)} %join.4.refs_0_), channel_id=1, source_target_pairs={{0,96},{1,97},{2,98},{3,99},{4,100},{5,101},{6,102},{7,103},{8,104... | collective-permute-start | bytes 786440 | tf_op jit(solution)/shard_map/ppermute | solution.py:446
  324.7 9.7 %collective-permute-start.19 = (bf16[4096,128]{1,0:T(8,128)(2,1)}, bf16[4096,128]{1,0:T(8,128)(2,1)S(1)}, u32[]{:S(2)}, u32[]{:S(2)}) collective-permute-start(bf16[4096,128]{1,0:T(8,128)(2,1)} %join.5.mine_ref), channel_id=1, source_target_pairs={{0,1},{1,0},{2,3},{3,2},{4,5},{5,4},{6,7},{7,6},{8,9},{9,8},{10,11... | collective-permute-start | bytes 3145736 | tf_op jit(solution)/shard_map/ppermute | solution.py:450
  (31 other events, 187.1 us)

commit v3 on v2

--- a/solution.py
+++ b/solution.py
@@ -11,6 +11,7 @@
 BF16 = jnp.bfloat16
 CH = 112
 WEIGHT_ROWS = 8192
+WR = 32
 VMEM_LIMIT = 58 * 1024 * 1024
 
 
@@ -437,74 +438,46 @@
     )(idx_rows, got)
 
 
-def moved(x, stride, step):
-    count = lax.axis_size("atoms")
-    plan = []
-    for i in range(count):
-        digit = (i // stride) % 4
-        plan.append((i, i + ((digit + step) % 4 - digit) * stride))
-    return lax.ppermute(x, "atoms", plan)
-
-
 def swapped(x):
     return lax.ppermute(x, "atoms", [(i, i ^ 1) for i in range(lax.axis_size("atoms"))])
 
 
-def add_and_split(place, pieces, base, scale_rows):
-    rows = pieces[-1].shape[0] // 4
-
-    def body(place_ref, *refs):
-        ins, outs = refs[: len(pieces)], refs[len(pieces) :]
-        for d in range(4):
-            at = pl.multiple_of(((place_ref[0] + d) % 4) * rows, 8)
-            total = None
-            for n, ref in enumerate(ins):
-                skip = place_ref[1] * scale_rows if (n == 0 and base) else 0
-                value = ref[pl.ds(pl.multiple_of(skip + at, 8), rows), :].astype(F32)
-                total = value if total is None else total + value
-            outs[d][...] = total
+def add_pair(core, grads, other):
+    half = other.shape[0]
+
+    def body(core_ref, grads_ref, other_ref, out_ref):
+        mine = grads_ref[pl.ds(pl.multiple_of(core_ref[0] * half, 16), half), :]
+        total = mine.astype(F32) + other_ref[...].astype(F32)
+        out_ref[...] = total.astype(BF16).reshape(half // WR, WR, 128)
 
     return pl.pallas_call(
         body,
-        in_specs=[SM] + [VM] * len(pieces),
-        out_specs=[VM] * 4,
-        out_shape=[jax.ShapeDtypeStruct((rows, 128), F32)] * 4,
+        in_specs=[SM, VM, VM],
+        out_specs=VM,
+        out_shape=jax.ShapeDtypeStruct((half // WR, WR, 128), BF16),
+        cost_estimate=pl.CostEstimate(flops=10**6, transcendentals=0, bytes_accessed=4 * 10**6),
+        name="add_pair",
+    )(core, grads, other)
+
+
+def add_peers(got):
+    peers = got.shape[0]
+    chips = peers // 2
+
+    def body(got_ref, out_ref):
+        x = got_ref[...].astype(F32).reshape(chips, 2, 16, 128)
+        total = jnp.sum(x, axis=0).astype(BF16)
+        out_ref[...] = jnp.broadcast_to(total[None], (chips, 2, 16, 128))
+
+    return pl.pallas_call(
+        body,
+        grid=(WR // 16,),
+        in_specs=[pl.BlockSpec((peers, 16, 128), lambda i: (0, CH // 16 + i, 0))],
+        out_specs=pl.BlockSpec((chips, 2, 16, 128), lambda i: (0, 0, i, 0)),
+        out_shape=jax.ShapeDtypeStruct((chips, 2, WR, 128), BF16),
         cost_estimate=pl.CostEstimate(flops=10**6, transcendentals=0, bytes_accessed=3 * 10**6),
-        name="add_and_split",
-    )(place, *pieces)
-
-
-def add_last(pieces):
-    def body(*refs):
-        total = refs[0][...]
-        for ref in refs[1:-1]:
-            total = total + ref[...]
-        refs[-1][...] = total.astype(BF16)
-
-    return pl.pallas_call(
-        body,
-        in_specs=[VM] * len(pieces),
-        out_specs=VM,
-        out_shape=jax.ShapeDtypeStruct(pieces[0].shape, BF16),
-        name="add_last",
-    )(*pieces)
-
-
-def join(place, pieces):
-    rows = pieces[0].shape[0]
-
-    def body(place_ref, *refs):
-        for d in range(4):
-            at = pl.multiple_of(((place_ref[0] + 4 - d) % 4) * rows, 16)
-            refs[4][pl.ds(at, rows), :] = refs[d][...]
-
-    return pl.pallas_call(
-        body,
-        in_specs=[SM] + [VM] * 4,
-        out_specs=VM,
-        out_shape=jax.ShapeDtypeStruct((4 * rows, 128), BF16),
-        name="join",
-    )(place, *pieces)
+        name="add_peers",
+    )(got)
 
 
 WEIGHT_PARTS = (
@@ -513,43 +486,36 @@
 
 
 def unpack(core, mine, other):
-    half = mine.shape[0]
+    chips = mine.shape[0]
 
     def body(core_ref, mine_ref, other_ref, *refs):
         outs, all_ref = refs[:-1], refs[-1]
-        all_ref[pl.ds(pl.multiple_of(core_ref[0] * half, 16), half), :] = mine_ref[...]
-        all_ref[pl.ds(pl.multiple_of((1 - core_ref[0]) * half, 16), half), :] = other_ref[...]
+
+        def place(chip, carry):
+            for half in range(2):
+                at = half * 2 * chips + 2 * chip
+                all_ref[at + core_ref[0]] = mine_ref[chip, half]
+                all_ref[at + 1 - core_ref[0]] = other_ref[chip, half]
+            return carry
+
+        lax.fori_loop(0, chips, place, 0, unroll=4)
         for out, (row, parts, height, blocks) in zip(outs, WEIGHT_PARTS):
             for p in range(parts):
                 for n in range(blocks):
-                    low = row + (p * blocks + n) * height
-                    out[p, :, 128 * n : 128 * n + 128] = all_ref[low : low + height, :].astype(F32)
+                    low = (row + (p * blocks + n) * height) // WR
+                    value = all_ref[low : low + height // WR].reshape(height, 128)
+                    out[p, :, 128 * n : 128 * n + 128] = value.astype(F32)
 
     return pl.pallas_call(
         body,
         in_specs=[SM, VM, VM],
         out_specs=[VM] * 6,
         out_shape=[jax.ShapeDtypeStruct((parts, height, 128 * blocks), F32) for _, parts, height, blocks in WEIGHT_PARTS],
-        scratch_shapes=[pltpu.VMEM((2 * half, 128), BF16)],
+        scratch_shapes=[pltpu.VMEM((4 * chips, WR, 128), BF16)],
         compiler_params=pltpu.CompilerParams(vmem_limit_bytes=VMEM_LIMIT // 2),
+        cost_estimate=pl.CostEstimate(flops=10**6, transcendentals=0, bytes_accessed=6 * 10**6),
         name="unpack",
     )(core, mine, other)
-
-
-def sum_weights(grads):
-    me = lax.axis_index("atoms").astype(jnp.int32)
-    core = me % 2
-    places = {stride: jnp.stack([(me // stride) % 4, core]) for stride in (32, 8, 2)}
-    half = WEIGHT_ROWS // 2
-    sent = lax.dynamic_slice_in_dim(grads, (1 - core) * half, half, axis=0)
-    pieces = [grads, swapped(sent)]
-    for stride in (32, 8, 2):
-        parts = add_and_split(places[stride], pieces, stride == 32, half)
-        pieces = [parts[0]] + [moved(parts[d], stride, d) for d in (1, 2, 3)]
-    value = add_last(pieces)
-    for stride in (2, 8, 32):
-        value = join(places[stride], [value] + [moved(value, stride, d) for d in (1, 2, 3)])
-    return unpack(jnp.stack([core, core]), value, swapped(value))
 
 
 def widen_pair(w):
@@ -620,11 +586,25 @@
     got_m = exchange(back_m)
     scale = float((2.0 * edges * peers) ** (-0.5))
     back_g, grads = backward(owners, got_c, turns, weights, kept, scale)
-    back_g, got_m = lax.optimization_barrier((back_g, got_m))
-    got_g = exchange(back_g)
-    messages = jnp.transpose(add_rows(asked_rows, got_m, BF16), (1, 0, 2))
-    w = sum_weights(grads)
-    grad_features = jnp.transpose(add_rows(asked_rows, got_g, F32), (1, 0, 2))
+    core = (lax.axis_index("atoms") % 2).astype(jnp.int32)
+    cores = jnp.stack([core, core])
+    half = WEIGHT_ROWS // 2
+    sent = lax.dynamic_slice_in_dim(grads, (1 - core) * half, half, axis=0)
+    w_rows = add_pair(cores, grads, swapped(sent))
+    both = jnp.concatenate([back_g, w_rows], axis=1)
+    both, got_m = lax.optimization_barrier((both, got_m))
+    messages = add_rows(asked_rows, got_m, BF16)
+    got_g, messages = lax.optimization_barrier((exchange(both), messages))
+    same_core = [list(range(c, peers, 2)) for c in range(2)]
+    w_mine = lax.all_to_all(
+        add_peers(got_g).reshape(peers // 2, 2 * WR, 128), "atoms",
+        split_axis=0, concat_axis=0, tiled=True, axis_index_groups=same_core,
+    ).reshape(peers // 2, 2, WR, 128)
+    grad_features = add_rows(asked_rows, got_g, F32)
+    w_mine, grad_features = lax.optimization_barrier((w_mine, grad_features))
+    messages = jnp.transpose(messages, (1, 0, 2))
+    grad_features = jnp.transpose(grad_features, (1, 0, 2))
+    w = unpack(cores, w_mine, swapped(w_mine))
     return (messages, grad_features, w[0][0], w[1], w[2], w[3][0], w[4], w[5])
 
 

time: 354 us -> 296 us (0.84)
  waiting for transfers between devices: 149 us -> 124 us
  starting transfers between devices: 71.3 us -> 48.8 us
  Pallas kernels: 97.2 us -> 88.2 us
  local copies, waits for them, and re-layouts: 24.6 us -> 20.1 us
    ppermute x18 -> x0, waiting for transfers between devices: 73.1 us -> none  [moved(): return lax.ppermute(x, 'atoms', plan)]
    all_to_all x5, waiting for transfers between devices: 72.7 us -> 110 us  [exchange(): return lax.all_to_all(x, 'atoms', split_axis=0, concat_axis=0, tiled=True)]
    ppermute x18 -> x0, starting transfers between devices: 23.4 us -> none  [moved(): return lax.ppermute(x, 'atoms', plan)]
    all_to_all x0 -> x1, waiting for transfers between devices: none -> 10.5 us  [local(): lax.all_to_all(add_peers(got_g).reshape(peers // 2, 2 * WR, 128), 'atoms'...]
    pallas_call x7 -> x2, Pallas kernels: 14.3 us -> 5.21 us  [the longest x1 3.07 us: add_pair(): pl.pallas_call(body, in_specs=[SM, VM, VM], out_specs=VM, out_shape=jax.S...]
    all_to_all x0 -> x1, starting transfers between devices: none -> 5.67 us  [local(): lax.all_to_all(add_peers(got_g).reshape(peers // 2, 2 * WR, 128), 'atoms'...]
    unnamed x69 -> x31, local copies, waits for them, and re-layouts: 8.04 us -> 2.43 us
    concatenate x0 -> x1, other arithmetic: none -> 4.78 us  [local(): both = jnp.concatenate([back_g, w_rows], axis=1)]
  transfers between devices with their start and end apart: 25 -> 8, of which waited for: 19 -> 7; matrix products, arithmetic and copies ran while one was open for 6% -> 9% of each run, Pallas kernels for 24% -> 26%
where the time goes in v3:
time: 296 us; the launch traced here: 294 us
  waiting for transfers between devices  124 us (42%)
  Pallas kernels  88.2 us (30%)
  starting transfers between devices  48.8 us (16%)
  local copies, waits for them, and re-layouts  20.1 us (7%)
  other arithmetic  11.9 us (4%)
    all_to_all x5, waiting for transfers between devices, exchange(): return lax.all_to_all(x, 'atoms', split_axis=0, concat_axis=0, tiled=True)  110 us
    all_to_all x5, starting transfers between devices, exchange(): return lax.all_to_all(x, 'atoms', split_axis=0, concat_axis=0, tiled=True)  39.2 us
    pallas_call x1, Pallas kernels, backward(): pl.pallas_call(body, in_specs=[SM] + [VM] * 15, out_specs=[VM, VM], out_s...  21.9 us
    pallas_call x1, Pallas kernels, forward(): pl.pallas_call(forward_body, in_specs=[SM] + [VM] * 11, out_specs=[VM] *...  19.3 us
    pallas_call x2, Pallas kernels, pick_rows(): pl.pallas_call(gather_body, grid=(peers // 16,), in_specs=[pl.BlockSpec((...  13.9 us
    pallas_call x2, Pallas kernels, add_rows(): pl.pallas_call(scatter_body, grid=(peers // 16,), in_specs=[pl.BlockSpec(...  13.2 us
    pallas_call x1, Pallas kernels, build_turns(): pl.pallas_call(prep_body, grid=(pairs,), in_specs=[pl.BlockSpec((1, 224,...  11.8 us
    all_to_all x1, waiting for transfers between devices, local(): lax.all_to_all(add_peers(got_g).reshape(peers // 2, 2 * WR, 128), 'atoms'...  10.5 us
  transfers between devices with their start and end apart: 8, of which 7 were waited for; matrix products, arithmetic and copies ran while one was open for 9% of the time, Pallas kernels for 26%

profile of v3, /device:TPU:1, one launch (start us, length us, event | category | flops | bytes accessed | tf_op | source)
XLA Modules:
  0.0 294.4 jit_solution(4724996474906372248)
XLA Ops:
  5.1 11.5 %all-to-all-start = ((s32[128,1,64]{2,1,0:T(1,128)}), s32[128,1,64]{2,1,0:T(1,128)S(1)}, u32[]{:S(2)}, u32[]{:S(2)}) async-start(s32[128,1,64]{2,1,0:T(1,128)} %copy.46), calls=%async_computation | async-start | bytes 131072 | tf_op jit(solution)/shard_map/all_to_all | solution.py:528
  17.2 8.7 %all-to-all-done = s32[128,1,64]{2,1,0:T(1,128)S(1)} async-done(((s32[128,1,64]{2,1,0:T(1,128)}), s32[128,1,64]{2,1,0:T(1,128)S(1)}, u32[]{:S(2)}, u32[]{:S(2)}) %all-to-all-start) | async-done | bytes 32800 | tf_op jit(solution)/shard_map/all_to_all | solution.py:528
  26.6 7.0 %pick_rows.3 = bf16[128,112,128]{2,1,0:T(8,128)(2,1)} custom-call(s32[128,64]{1,0:T(8,128)} %bitcast.102, bf16[64,64]{1,0:T(8,128)(2,1)} %fusion.eye_ref, bf16[9,128,128]{2,1,0:T(8,128)(2,1)} %bitcast.108), custom_call_target="tpu_custom_call" | custom-call | flops 2000000000 | bytes 4000000 | tf_op jit(solution)/shard_map/pick_rows/pallas_call | solution.py:96
  33.6 5.8 %all-to-all-start.2 = ((bf16[128,112,128]{2,1,0:T(8,128)(2,1)}), bf16[128,112,128]{2,1,0:T(8,128)(2,1)}, u32[]{:S(2)}, u32[]{:S(2)}) async-start(bf16[128,112,128]{2,1,0:T(8,128)(2,1)} %pick_rows.3), calls=%async_computation.2 | async-start | bytes 7340032 | tf_op jit(solution)/shard_map/all_to_all | solution.py:528
  40.0 7.0 %pick_rows.2 = bf16[128,112,128]{2,1,0:T(8,128)(2,1)} custom-call(s32[128,64]{1,0:T(8,128)} %bitcast.103, bf16[64,64]{1,0:T(8,128)(2,1)} %fusion.eye_ref, bf16[9,128,128]{2,1,0:T(8,128)(2,1)} %bitcast.109), custom_call_target="tpu_custom_call" | custom-call | flops 2000000000 | bytes 4000000 | tf_op jit(solution)/shard_map/pick_rows/pallas_call | solution.py:96
  47.0 39.3 %all-to-all-done.2.r_ref = bf16[128,112,128]{2,1,0:T(8,128)(2,1)} async-done(((bf16[128,112,128]{2,1,0:T(8,128)(2,1)}), bf16[128,112,128]{2,1,0:T(8,128)(2,1)}, u32[]{:S(2)}, u32[]{:S(2)}) %all-to-all-start.2) | async-done | bytes 3670048 | tf_op jit(solution)/shard_map/all_to_all | solution.py:528
  86.3 5.8 %all-to-all-start.1 = ((bf16[128,112,128]{2,1,0:T(8,128)(2,1)}), bf16[128,112,128]{2,1,0:T(8,128)(2,1)}, u32[]{:S(2)}, u32[]{:S(2)}) async-start(bf16[128,112,128]{2,1,0:T(8,128)(2,1)} %pick_rows.2), calls=%async_computation.1 | async-start | bytes 7340032 | tf_op jit(solution)/shard_map/all_to_all | solution.py:528
  97.7 5.3 %concatenate.57 = f32[32,9,16,24]{0,3,1,2:T(8,128)S(1)} concatenate(f32[9,9,16,24]{0,3,1,2:T(8,128)S(1)} %bitcast.97, f32[2,9,16,24]{0,3,1,2:T(8,128)} %broadcast_in_dim.32, f32[5,9,16,24]{0,3,1,2:T(8,128)} %broadcast_in_dim.33, f32[9,9,16,24]{0,3,1,2:T(8,128)S(1)} %bitcast.98, f32[7,9,16,24]{0,3,1,2:T(8,128)} %broadcast_in_dim.34), dimensions={0} | concatenate | bytes 884736 | tf_op jit(solution)/shard_map/concatenate | solution.py:574
  105.8 11.8 %build_turns.1 = (bf16[16,224,256]{2,1,0:T(8,128)(2,1)}, bf16[16,224,256]{2,1,0:T(8,128)(2,1)}, bf16[16,224,256]{2,1,0:T(8,128)(2,1)}, bf16[16,224,256]{2,1,0:T(8,128)(2,1)}) custom-call(f32[16,224,32]{2,1,0:T(8,128)} %pad.8.ra_ref, f32[16,32,256]{2,1,0:T(8,128)} %pad.9.rb_ref, bf16[32,256]{1,0:T(8,128)(2,1)} %constant.44.clone.sp_ref, ...), custom_call_target="tpu_custom_call" | custom-call | flops 1000000000 | bytes 10000000 | tf_op jit(solution)/shard_map/build_turns/pallas_call | solution.py:143
  121.1 19.3 %forward.1 = (bf16[128,112,128]{2,1,0:T(8,128)(2,1)}, bf16[768,2304]{1,0:T(8,128)(2,1)}, f32[768,1152]{1,0:T(8,128)}, f32[768,128]{1,0:T(8,128)}, bf16[768,1152]{1,0:T(8,128)(2,1)}) custom-call(s32[32]{0:T(128)} %copy-done.10, bf16[128,112,128]{2,1,0:T(8,128)(2,1)} %all-to-all-done.2.r_ref, bf16[16,224,256]{2,1,0:T(8,128)(2,1)} %get-tuple-element.31.wt_ref.refs_2_, ...), custom_call_target="tpu_custom_call" | custom-call | flops 10000000000 | bytes 30000000 | tf_op jit(solution)/shard_map/forward/pallas_call | solution.py:243
  140.4 10.3 %all-to-all-start.3 = ((bf16[128,112,128]{2,1,0:T(8,128)(2,1)}), bf16[128,112,128]{2,1,0:T(8,128)(2,1)}, u32[]{:S(2)}, u32[]{:S(2)}) async-start(bf16[128,112,128]{2,1,0:T(8,128)(2,1)} %get-tuple-element.41), calls=%async_computation.3 | async-start | bytes 7340032 | tf_op jit(solution)/shard_map/all_to_all | solution.py:528
  150.7 21.9 %backward.1 = (bf16[128,112,128]{2,1,0:T(8,128)(2,1)}, bf16[8192,128]{1,0:T(8,128)(2,1)}) custom-call(s32[32]{0:T(128)} %copy-done.10, bf16[128,112,128]{2,1,0:T(8,128)(2,1)} %all-to-all-done.1.refs_1_, bf16[16,224,256]{2,1,0:T(8,128)(2,1)} %get-tuple-element.31.wt_ref.refs_2_, bf16[16,224,256]{2,1,0:T(8,128)(2,1)} %get-tuple-element.32.ws_ref.refs_3_, ...), custom_call_target="tpu_custom_call" | custom-call | flops 20000000000 | bytes 30000000 | tf_op jit(solution)/shard_map/backward/pallas_call | solution.py:380
  178.6 3.1 %add_pair.1 = bf16[128,32,128]{2,1,0:T(8,128)(2,1)} custom-call(s32[2]{0:T(128)} %pad_add_fusion.1.core_ref, bf16[8192,128]{1,0:T(8,128)(2,1)} %get-tuple-element.40.grads_ref, bf16[4096,128]{1,0:T(8,128)(2,1)} %copy-done.2), custom_call_target="tpu_custom_call" | custom-call | flops 1000000 | bytes 4000000 | tf_op jit(solution)/shard_map/add_pair/pallas_call | solution.py:453
  181.7 4.8 %pad_maximum_fusion = bf16[128,144,128]{2,1,0:T(8,128)(2,1)} fusion(bf16[128,32,128]{2,1,0:T(8,128)(2,1)} %add_pair.1, bf16[128,112,128]{2,1,0:T(8,128)(2,1)} %get-tuple-element.39), kind=kLoop, calls=%fused_computation | loop fusion | flops 9437184 | bytes 9437184 | tf_op jit(solution)/shard_map/concatenate | solution.py:594
  186.5 11.0 %all-to-all-done.3.got_ref = bf16[128,112,128]{2,1,0:T(8,128)(2,1)} async-done(((bf16[128,112,128]{2,1,0:T(8,128)(2,1)}), bf16[128,112,128]{2,1,0:T(8,128)(2,1)}, u32[]{:S(2)}, u32[]{:S(2)}) %all-to-all-start.3) | async-done | bytes 3670048 | tf_op jit(solution)/shard_map/all_to_all | solution.py:528
  197.5 5.8 %all-to-all-start.4 = ((bf16[128,144,128]{2,1,0:T(8,128)(2,1)}), bf16[128,144,128]{2,1,0:T(8,128)(2,1)}, u32[]{:S(2)}, u32[]{:S(2)}) async-start(bf16[128,144,128]{2,1,0:T(8,128)(2,1)} %pad_maximum_fusion), calls=%async_computation.4 | async-start | bytes 9437184 | tf_op jit(solution)/shard_map/all_to_all | solution.py:528
  204.3 6.5 %add_rows.2 = bf16[9,128,128]{2,1,0:T(8,128)(2,1)} custom-call(s32[8,2048]{1,0:T(8,128)} %pad_add_fusion.idx_ref, bf16[128,112,128]{2,1,0:T(8,128)(2,1)} %all-to-all-done.3.got_ref), custom_call_target="tpu_custom_call" | custom-call | flops 1000000000 | bytes 6000000 | tf_op jit(solution)/shard_map/add_rows/pallas_call | solution.py:426
  210.9 50.8 %all-to-all-done.4.got_ref = bf16[128,144,128]{2,1,0:T(8,128)(2,1)} async-done(((bf16[128,144,128]{2,1,0:T(8,128)(2,1)}), bf16[128,144,128]{2,1,0:T(8,128)(2,1)}, u32[]{:S(2)}, u32[]{:S(2)}) %all-to-all-start.4) | async-done | bytes 4718624 | tf_op jit(solution)/shard_map/all_to_all | solution.py:528
  263.9 5.7 %all-to-all-start.5 = ((bf16[64,64,128]{2,1,0:T(8,128)(2,1)}), bf16[64,64,128]{2,1,0:T(8,128)(2,1)S(1)}, u32[]{:S(2)}, u32[]{:S(2)}) async-start(bf16[64,64,128]{2,1,0:T(8,128)(2,1)} %bitcast.99), calls=%async_computation.5 | async-start | bytes 2097152 | tf_op jit(solution)/shard_map/all_to_all | solution.py:599
  269.6 6.7 %add_rows.3 = f32[9,128,128]{2,1,0:T(8,128)} custom-call(s32[8,2048]{1,0:T(8,128)} %pad_add_fusion.idx_ref, bf16[128,144,128]{2,1,0:T(8,128)(2,1)} %all-to-all-done.4.got_ref), custom_call_target="tpu_custom_call" | custom-call | flops 1000000000 | bytes 6000000 | tf_op jit(solution)/shard_map/add_rows/pallas_call | solution.py:426
  276.2 10.5 %all-to-all-done.5 = bf16[64,64,128]{2,1,0:T(8,128)(2,1)S(1)} async-done(((bf16[64,64,128]{2,1,0:T(8,128)(2,1)}), bf16[64,64,128]{2,1,0:T(8,128)(2,1)S(1)}, u32[]{:S(2)}, u32[]{:S(2)}) %all-to-all-start.5) | async-done | bytes 1048608 | tf_op jit(solution)/shard_map/all_to_all | solution.py:599
  286.7 2.5 collective-permute-start.1
  289.2 2.3 collective-permute-done.1.other_ref
  291.5 2.9 unpack.1
  (83 shorter events, 27.2 us)
Async XLA Ops:
  2.4 31.1 %copy-start.10 = (s32[32]{0:T(128)}, s32[32]{0:T(128)S(1)}, u32[]{:S(2)}) copy-start(s32[32]{0:T(128)S(1)} %reshape.525.own_ref.refs_0_) | copy-start | bytes 388
  5.1 20.8 %all-to-all-start = ((s32[128,1,64]{2,1,0:T(1,128)}), s32[128,1,64]{2,1,0:T(1,128)S(1)}, u32[]{:S(2)}, u32[]{:S(2)}) async-start(s32[128,1,64]{2,1,0:T(1,128)} %copy.46), calls=%async_computation | async-start | bytes 131072 | tf_op jit(solution)/shard_map/all_to_all | solution.py:528
  26.0 0.6 copy-start.5
  33.5 5.9 %copy-start.9 = (s32[2,384]{1,0:T(2,128)S(1)}, s32[2,384]{1,0:T(2,128)}, u32[]{:S(2)}) copy-start(s32[2,384]{1,0:T(2,128)} %param.22) | copy-start | bytes 9220
  33.5 6.4 %copy-start.7 = (f32[9,9,384]{2,1,0:T(8,128)S(1)}, f32[9,9,384]{2,1,0:T(8,128)}, u32[]{:S(2)}) copy-start(f32[9,9,384]{2,1,0:T(8,128)} %param.19) | copy-start | bytes 373252
  33.6 52.7 %all-to-all-start.2 = ((bf16[128,112,128]{2,1,0:T(8,128)(2,1)}), bf16[128,112,128]{2,1,0:T(8,128)(2,1)}, u32[]{:S(2)}, u32[]{:S(2)}) async-start(bf16[128,112,128]{2,1,0:T(8,128)(2,1)} %pick_rows.3), calls=%async_computation.2 | async-start | bytes 7340032 | tf_op jit(solution)/shard_map/all_to_all | solution.py:528
  86.3 54.1 %all-to-all-start.1 = ((bf16[128,112,128]{2,1,0:T(8,128)(2,1)}), bf16[128,112,128]{2,1,0:T(8,128)(2,1)}, u32[]{:S(2)}, u32[]{:S(2)}) async-start(bf16[128,112,128]{2,1,0:T(8,128)(2,1)} %pick_rows.2), calls=%async_computation.1 | async-start | bytes 7340032 | tf_op jit(solution)/shard_map/all_to_all | solution.py:528
  105.8 11.9 %copy-start.8 = (bf16[2,128,128]{2,1,0:T(8,128)(2,1)S(1)}, bf16[2,128,128]{2,1,0:T(8,128)(2,1)}, u32[]{:S(2)}) copy-start(bf16[2,128,128]{2,1,0:T(8,128)(2,1)} %param.28) | copy-start | bytes 196612
  105.8 12.6 %copy-start.4 = (bf16[2,256,128]{2,1,0:T(8,128)(2,1)S(1)}, bf16[2,256,128]{2,1,0:T(8,128)(2,1)}, u32[]{:S(2)}) copy-start(bf16[2,256,128]{2,1,0:T(8,128)(2,1)} %param.25) | copy-start | bytes 393220
  105.8 13.3 %copy-start.3 = (bf16[2,256,256]{2,1,0:T(8,128)(2,1)S(1)}, bf16[2,256,256]{2,1,0:T(8,128)(2,1)}, u32[]{:S(2)}) copy-start(bf16[2,256,256]{2,1,0:T(8,128)(2,1)} %param.27) | copy-start | bytes 786436
  117.7 2.4 copy-start.1
  140.4 57.1 %all-to-all-start.3 = ((bf16[128,112,128]{2,1,0:T(8,128)(2,1)}), bf16[128,112,128]{2,1,0:T(8,128)(2,1)}, u32[]{:S(2)}, u32[]{:S(2)}) async-start(bf16[128,112,128]{2,1,0:T(8,128)(2,1)} %get-tuple-element.41), calls=%async_computation.3 | async-start | bytes 7340032 | tf_op jit(solution)/shard_map/all_to_all | solution.py:528
  174.0 3.7 %collective-permute-start = (bf16[4096,128]{1,0:T(8,128)(2,1)S(1)}, bf16[4096,128]{1,0:T(8,128)(2,1)S(1)}, u32[]{:S(2)}, u32[]{:S(2)}) collective-permute-start(bf16[4096,128]{1,0:T(8,128)(2,1)S(1)} %constant_dynamic-slice_fusion), channel_id=1, source_target_pairs={{0,1},{1,0},{2,3},{3,2},{4,5},{5,4},{6,7},{7,6},{8,9},{9,8},{10,11... | collective-permute-start | bytes 3145736 | tf_op jit(solution)/shard_map/ppermute | solution.py:442
  177.6 1.0 copy-start.2
  186.5 16.9 %copy-start.6 = (s32[128,1,64]{2,1,0:T(1,128)S(1)}, s32[128,1,64]{2,1,0:T(1,128)}, u32[]{:S(2)}) copy-start(s32[128,1,64]{2,1,0:T(1,128)} %copy-done.5) | copy-start | bytes 98308
  197.5 64.3 %all-to-all-start.4 = ((bf16[128,144,128]{2,1,0:T(8,128)(2,1)}), bf16[128,144,128]{2,1,0:T(8,128)(2,1)}, u32[]{:S(2)}, u32[]{:S(2)}) async-start(bf16[128,144,128]{2,1,0:T(8,128)(2,1)} %pad_maximum_fusion), calls=%async_computation.4 | async-start | bytes 9437184 | tf_op jit(solution)/shard_map/all_to_all | solution.py:528
  263.9 22.9 %all-to-all-start.5 = ((bf16[64,64,128]{2,1,0:T(8,128)(2,1)}), bf16[64,64,128]{2,1,0:T(8,128)(2,1)S(1)}, u32[]{:S(2)}, u32[]{:S(2)}) async-start(bf16[64,64,128]{2,1,0:T(8,128)(2,1)} %bitcast.99), calls=%async_computation.5 | async-start | bytes 2097152 | tf_op jit(solution)/shard_map/all_to_all | solution.py:599
  269.5 22.0 %copy-start = (s32[2]{0:T(128)S(1)}, s32[2]{0:T(128)}, u32[]{:S(2)}) copy-start(s32[2]{0:T(128)} %pad_add_fusion.1.core_ref) | copy-start | bytes 28
  286.7 4.8 %collective-permute-start.1 = (bf16[64,2,32,128]{3,2,1,0:T(8,128)(2,1)S(1)}, bf16[64,2,32,128]{3,2,1,0:T(8,128)(2,1)S(1)}, u32[]{:S(2)}, u32[]{:S(2)}) collective-permute-start(bf16[64,2,32,128]{3,2,1,0:T(8,128)(2,1)S(1)} %bitcast.49), channel_id=1, source_target_pairs={{0,1},{1,0},{2,3},{3,2},{4,5},{5,4},{6,7},{7,6},{8,9},{9,8},{10,11... | collective-permute-start | bytes 3145736 | tf_op jit(solution)/shard_map/ppermute | solution.py:442

commit v4 on v3

--- a/solution.py
+++ b/solution.py
@@ -12,6 +12,7 @@
 CH = 112
 WEIGHT_ROWS = 8192
 WR = 32
+PICK = 64
 VMEM_LIMIT = 58 * 1024 * 1024
 
 
@@ -71,7 +72,7 @@
     turned = dot_nt(eye_ref[...], idx_ref[...].astype(F32).astype(BF16))
     lane = lax.broadcasted_iota(jnp.int32, (64, 128), 1).astype(F32)
     picks = []
-    for q in range(16):
+    for q in range(PICK):
         col = jnp.broadcast_to(turned[:, q : q + 1], (64, 128))
         picks.append(jnp.where(col == lane, 1.0, 0.0).astype(BF16))
     kinds = [jnp.concatenate([x[16 * v : 16 * v + 16] for x in picks], axis=0) for v in range(4)]
@@ -85,24 +86,25 @@
             axis=0,
         )
         got = dot(left, right).astype(BF16)
-        out_ref[:, 16 * j : 16 * j + 16, :] = got[:, :128].reshape(16, 16, 128)
-        out_ref[:, 16 * (j + 3) : 16 * (j + 4), :] = got[:, 128:].reshape(16, 16, 128)
+        out_ref[:, 16 * j : 16 * j + 16, :] = got[:, :128].reshape(PICK, 16, 128)
+        out_ref[:, 16 * (j + 3) : 16 * (j + 4), :] = got[:, 128:].reshape(PICK, 16, 128)
     last = dot(kinds[0], feat_ref[6]).astype(BF16)
-    out_ref[:, 96:112, :] = last.reshape(16, 16, 128)
+    out_ref[:, 96:112, :] = last.reshape(PICK, 16, 128)
 
 
 def pick_rows(idx, eye, feat):
     peers = idx.shape[0]
     return pl.pallas_call(
         gather_body,
-        grid=(peers // 16,),
+        grid=(peers // PICK,),
         in_specs=[
-            pl.BlockSpec((16, 64), lambda c: (c, 0)),
+            pl.BlockSpec((PICK, 64), lambda c: (c, 0)),
             whole((64, 64)),
             whole((9, 128, 128)),
         ],
-        out_specs=pl.BlockSpec((16, CH, 128), lambda c: (c, 0, 0)),
+        out_specs=pl.BlockSpec((PICK, CH, 128), lambda c: (c, 0, 0)),
         out_shape=jax.ShapeDtypeStruct((peers, CH, 128), BF16),
+        compiler_params=pltpu.CompilerParams(vmem_limit_bytes=VMEM_LIMIT // 2),
         cost_estimate=pl.CostEstimate(flops=2 * 10**9, transcendentals=0, bytes_accessed=4 * 10**6),
         name="pick_rows",
     )(idx, eye, feat)
@@ -557,7 +559,6 @@
     eye = jnp.eye(64, dtype=BF16)
 
     got_f = exchange(pick_rows(asked, eye, jnp.transpose(features, (1, 0, 2))))
-    got_c = exchange(pick_rows(asked, eye, jnp.transpose(cotangent, (1, 0, 2))))
 
     turned = jnp.stack([wigner[i] for i in COEF_ORDER]).reshape(9, 9, pairs, each)
     pos = jnp.stack(
@@ -582,6 +583,9 @@
         first_m0, widen_pair(first_m1), widen_pair(first_m2),
         second_m0, widen_pair(second_m1), widen_pair(second_m2),
     )
+    picked_c = pick_rows(asked, eye, jnp.transpose(cotangent, (1, 0, 2)))
+    picked_c, turns, weights = lax.optimization_barrier((picked_c, turns, weights))
+    got_c = exchange(picked_c)
     back_m, *kept = forward(owners, got_f, turns, weights, 2 * edges)
     got_m = exchange(back_m)
     scale = float((2.0 * edges * peers) ** (-0.5))

time: 296 us -> 288 us (0.973)
  local copies, waits for them, and re-layouts: 20.1 us -> 33.4 us
  Pallas kernels: 88.2 us -> 78.7 us
  waiting for transfers between devices: 124 us -> 117 us
  starting transfers between devices: 48.8 us -> 44.5 us
    unnamed x31, local copies, waits for them, and re-layouts: 2.43 us -> 12.4 us
    pallas_call x2, Pallas kernels: 13.9 us -> 4.6 us  [pick_rows(): pl.pallas_call(gather_body, grid=(peers // PICK,), in_specs=[pl.BlockSpec...]
    all_to_all x5, waiting for transfers between devices: 110 us -> 103 us  [exchange(): return lax.all_to_all(x, 'atoms', split_axis=0, concat_axis=0, tiled=True)]
    all_to_all x5, starting transfers between devices: 39.2 us -> 34.8 us  [exchange(): return lax.all_to_all(x, 'atoms', split_axis=0, concat_axis=0, tiled=True)]
  transfers between devices with their start and end apart: 8 -> 8, of which waited for: 7 -> 8; matrix products, arithmetic and copies ran while one was open for 9% -> 12% of each run, Pallas kernels for 26% -> 25%
where the time goes in v4:
time: 288 us; the launch traced here: 286 us
  waiting for transfers between devices  117 us (41%)
  Pallas kernels  78.7 us (27%)
  starting transfers between devices  44.5 us (15%)
  local copies, waits for them, and re-layouts  33.4 us (12%)
  other arithmetic  11.3 us (4%)
    all_to_all x5, waiting for transfers between devices, exchange(): return lax.all_to_all(x, 'atoms', split_axis=0, concat_axis=0, tiled=True)  103 us
    all_to_all x5, starting transfers between devices, exchange(): return lax.all_to_all(x, 'atoms', split_axis=0, concat_axis=0, tiled=True)  34.8 us
    pallas_call x1, Pallas kernels, backward(): pl.pallas_call(body, in_specs=[SM] + [VM] * 15, out_specs=[VM, VM], out_s...  21.9 us
    pallas_call x1, Pallas kernels, forward(): pl.pallas_call(forward_body, in_specs=[SM] + [VM] * 11, out_specs=[VM] *...  19.1 us
    pallas_call x2, Pallas kernels, add_rows(): pl.pallas_call(scatter_body, grid=(peers // 16,), in_specs=[pl.BlockSpec(...  13.2 us
    unnamed x31, local copies, waits for them, and re-layouts  12.4 us
    pallas_call x1, Pallas kernels, build_turns(): pl.pallas_call(prep_body, grid=(pairs,), in_specs=[pl.BlockSpec((1, 224,...  11.8 us
    all_to_all x1, waiting for transfers between devices, local(): lax.all_to_all(add_peers(got_g).reshape(peers // 2, 2 * WR, 128), 'atoms'...  10.5 us
  transfers between devices with their start and end apart: 8, of which 8 were waited for; matrix products, arithmetic and copies ran while one was open for 12% of the time, Pallas kernels for 25%

profile of v4, /device:TPU:1, one launch (start us, length us, event | category | flops | bytes accessed | tf_op | source)
XLA Modules:
  0.0 286.0 jit_solution(1715056043295944842)
XLA Ops:
  5.1 11.5 %all-to-all-start = ((s32[128,1,64]{2,1,0:T(1,128)}), s32[128,1,64]{2,1,0:T(1,128)S(1)}, u32[]{:S(2)}, u32[]{:S(2)}) async-start(s32[128,1,64]{2,1,0:T(1,128)} %copy.46), calls=%async_computation | async-start | bytes 131072 | tf_op jit(solution)/shard_map/all_to_all | solution.py:530
  21.6 4.3 %all-to-all-done = s32[128,1,64]{2,1,0:T(1,128)S(1)} async-done(((s32[128,1,64]{2,1,0:T(1,128)}), s32[128,1,64]{2,1,0:T(1,128)S(1)}, u32[]{:S(2)}, u32[]{:S(2)}) %all-to-all-start) | async-done | bytes 32800 | tf_op jit(solution)/shard_map/all_to_all | solution.py:530
  26.9 2.3 pick_rows.3
  31.1 5.9 %all-to-all-start.2 = ((bf16[128,112,128]{2,1,0:T(8,128)(2,1)}), bf16[128,112,128]{2,1,0:T(8,128)(2,1)}, u32[]{:S(2)}, u32[]{:S(2)}) async-start(bf16[128,112,128]{2,1,0:T(8,128)(2,1)} %copy-done), calls=%async_computation.2 | async-start | bytes 7340032 | tf_op jit(solution)/shard_map/all_to_all | solution.py:530
  46.8 5.8 %concatenate.57 = f32[32,9,16,24]{0,3,1,2:T(8,128)S(1)} concatenate(f32[9,9,16,24]{0,3,1,2:T(8,128)} %bitcast.101, f32[2,9,16,24]{0,3,1,2:T(8,128)} %broadcast_in_dim.32, f32[5,9,16,24]{0,3,1,2:T(8,128)} %broadcast_in_dim.33, f32[9,9,16,24]{0,3,1,2:T(8,128)} %bitcast.102, f32[7,9,16,24]{0,3,1,2:T(8,128)} %broadcast_in_dim.34), dimensions={0} | concatenate | bytes 884736 | tf_op jit(solution)/shard_map/concatenate | solution.py:575
  55.5 11.8 %build_turns.1 = (bf16[16,224,256]{2,1,0:T(8,128)(2,1)}, bf16[16,224,256]{2,1,0:T(8,128)(2,1)}, bf16[16,224,256]{2,1,0:T(8,128)(2,1)}, bf16[16,224,256]{2,1,0:T(8,128)(2,1)}) custom-call(f32[16,224,32]{2,1,0:T(8,128)} %pad.8.ra_ref, f32[16,32,256]{2,1,0:T(8,128)} %pad.9.rb_ref, bf16[32,256]{1,0:T(8,128)(2,1)} %constant.44.clone.sp_ref, ...), custom_call_target="tpu_custom_call" | custom-call | flops 1000000000 | bytes 10000000 | tf_op jit(solution)/shard_map/build_turns/pallas_call | solution.py:145
  70.8 2.3 pick_rows.2
  75.0 8.7 %all-to-all-done.2.r_ref = bf16[128,112,128]{2,1,0:T(8,128)(2,1)} async-done(((bf16[128,112,128]{2,1,0:T(8,128)(2,1)}), bf16[128,112,128]{2,1,0:T(8,128)(2,1)}, u32[]{:S(2)}, u32[]{:S(2)}) %all-to-all-start.2) | async-done | bytes 3670048 | tf_op jit(solution)/shard_map/all_to_all | solution.py:530
  83.7 5.8 %all-to-all-start.1 = ((bf16[128,112,128]{2,1,0:T(8,128)(2,1)}), bf16[128,112,128]{2,1,0:T(8,128)(2,1)}, u32[]{:S(2)}, u32[]{:S(2)}) async-start(bf16[128,112,128]{2,1,0:T(8,128)(2,1)} %copy-done.1), calls=%async_computation.1 | async-start | bytes 7340032 | tf_op jit(solution)/shard_map/all_to_all | solution.py:530
  89.5 19.1 %forward.1 = (bf16[128,112,128]{2,1,0:T(8,128)(2,1)}, bf16[768,2304]{1,0:T(8,128)(2,1)}, f32[768,1152]{1,0:T(8,128)}, f32[768,128]{1,0:T(8,128)}, bf16[768,1152]{1,0:T(8,128)(2,1)}) custom-call(s32[32]{0:T(128)} %copy-done.10, bf16[128,112,128]{2,1,0:T(8,128)(2,1)} %all-to-all-done.2.r_ref, bf16[16,224,256]{2,1,0:T(8,128)(2,1)} %get-tuple-element.47.wt_ref.refs_2_, ...), custom_call_target="tpu_custom_call" | custom-call | flops 10000000000 | bytes 30000000 | tf_op jit(solution)/shard_map/forward/pallas_call | solution.py:245
  108.6 27.8 %all-to-all-done.1.refs_1_ = bf16[128,112,128]{2,1,0:T(8,128)(2,1)} async-done(((bf16[128,112,128]{2,1,0:T(8,128)(2,1)}), bf16[128,112,128]{2,1,0:T(8,128)(2,1)}, u32[]{:S(2)}, u32[]{:S(2)}) %all-to-all-start.1) | async-done | bytes 3670048 | tf_op jit(solution)/shard_map/all_to_all | solution.py:530
  136.4 5.8 %all-to-all-start.3 = ((bf16[128,112,128]{2,1,0:T(8,128)(2,1)}), bf16[128,112,128]{2,1,0:T(8,128)(2,1)}, u32[]{:S(2)}, u32[]{:S(2)}) async-start(bf16[128,112,128]{2,1,0:T(8,128)(2,1)} %get-tuple-element.63), calls=%async_computation.3 | async-start | bytes 7340032 | tf_op jit(solution)/shard_map/all_to_all | solution.py:530
  142.2 21.9 %backward.1 = (bf16[128,112,128]{2,1,0:T(8,128)(2,1)}, bf16[8192,128]{1,0:T(8,128)(2,1)}) custom-call(s32[32]{0:T(128)} %copy-done.10, bf16[128,112,128]{2,1,0:T(8,128)(2,1)} %all-to-all-done.1.refs_1_, bf16[16,224,256]{2,1,0:T(8,128)(2,1)} %get-tuple-element.47.wt_ref.refs_2_, bf16[16,224,256]{2,1,0:T(8,128)(2,1)} %get-tuple-element.48.ws_ref.refs_3_, ...), custom_call_target="tpu_custom_call" | custom-call | flops 20000000000 | bytes 30000000 | tf_op jit(solution)/shard_map/backward/pallas_call | solution.py:382
  170.2 3.1 %add_pair.1 = bf16[128,32,128]{2,1,0:T(8,128)(2,1)} custom-call(s32[2]{0:T(128)} %pad_add_fusion.1.core_ref, bf16[8192,128]{1,0:T(8,128)(2,1)} %get-tuple-element.62.grads_ref, bf16[4096,128]{1,0:T(8,128)(2,1)} %copy-done.6), custom_call_target="tpu_custom_call" | custom-call | flops 1000000 | bytes 4000000 | tf_op jit(solution)/shard_map/add_pair/pallas_call | solution.py:455
  173.3 4.8 %pad_maximum_fusion = bf16[128,144,128]{2,1,0:T(8,128)(2,1)} fusion(bf16[128,32,128]{2,1,0:T(8,128)(2,1)} %add_pair.1, bf16[128,112,128]{2,1,0:T(8,128)(2,1)} %get-tuple-element.61), kind=kLoop, calls=%fused_computation | loop fusion | flops 9437184 | bytes 9437184 | tf_op jit(solution)/shard_map/concatenate | solution.py:598
  178.1 11.0 %all-to-all-done.3.got_ref = bf16[128,112,128]{2,1,0:T(8,128)(2,1)} async-done(((bf16[128,112,128]{2,1,0:T(8,128)(2,1)}), bf16[128,112,128]{2,1,0:T(8,128)(2,1)}, u32[]{:S(2)}, u32[]{:S(2)}) %all-to-all-start.3) | async-done | bytes 3670048 | tf_op jit(solution)/shard_map/all_to_all | solution.py:530
  189.1 5.8 %all-to-all-start.4 = ((bf16[128,144,128]{2,1,0:T(8,128)(2,1)}), bf16[128,144,128]{2,1,0:T(8,128)(2,1)}, u32[]{:S(2)}, u32[]{:S(2)}) async-start(bf16[128,144,128]{2,1,0:T(8,128)(2,1)} %pad_maximum_fusion), calls=%async_computation.4 | async-start | bytes 9437184 | tf_op jit(solution)/shard_map/all_to_all | solution.py:530
  196.0 6.5 %add_rows.2 = bf16[9,128,128]{2,1,0:T(8,128)(2,1)} custom-call(s32[8,2048]{1,0:T(8,128)} %pad_add_fusion.idx_ref, bf16[128,112,128]{2,1,0:T(8,128)(2,1)} %all-to-all-done.3.got_ref), custom_call_target="tpu_custom_call" | custom-call | flops 1000000000 | bytes 6000000 | tf_op jit(solution)/shard_map/add_rows/pallas_call | solution.py:428
  202.5 50.9 %all-to-all-done.4.got_ref = bf16[128,144,128]{2,1,0:T(8,128)(2,1)} async-done(((bf16[128,144,128]{2,1,0:T(8,128)(2,1)}), bf16[128,144,128]{2,1,0:T(8,128)(2,1)}, u32[]{:S(2)}, u32[]{:S(2)}) %all-to-all-start.4) | async-done | bytes 4718624 | tf_op jit(solution)/shard_map/all_to_all | solution.py:530
  255.5 5.7 %all-to-all-start.5 = ((bf16[64,64,128]{2,1,0:T(8,128)(2,1)}), bf16[64,64,128]{2,1,0:T(8,128)(2,1)S(1)}, u32[]{:S(2)}, u32[]{:S(2)}) async-start(bf16[64,64,128]{2,1,0:T(8,128)(2,1)} %bitcast.103), calls=%async_computation.5 | async-start | bytes 2097152 | tf_op jit(solution)/shard_map/all_to_all | solution.py:603
  261.2 6.7 %add_rows.3 = f32[9,128,128]{2,1,0:T(8,128)} custom-call(s32[8,2048]{1,0:T(8,128)} %pad_add_fusion.idx_ref, bf16[128,144,128]{2,1,0:T(8,128)(2,1)} %all-to-all-done.4.got_ref), custom_call_target="tpu_custom_call" | custom-call | flops 1000000000 | bytes 6000000 | tf_op jit(solution)/shard_map/add_rows/pallas_call | solution.py:428
  267.9 10.5 %all-to-all-done.5 = bf16[64,64,128]{2,1,0:T(8,128)(2,1)S(1)} async-done(((bf16[64,64,128]{2,1,0:T(8,128)(2,1)}), bf16[64,64,128]{2,1,0:T(8,128)(2,1)S(1)}, u32[]{:S(2)}, u32[]{:S(2)}) %all-to-all-start.5) | async-done | bytes 1048608 | tf_op jit(solution)/shard_map/all_to_all | solution.py:603
  278.3 2.5 collective-permute-start.1
  283.1 2.9 unpack.1
  (83 shorter events, 41.7 us)
Async XLA Ops:
  2.4 26.8 %copy-start.10 = (s32[32]{0:T(128)}, s32[32]{0:T(128)S(1)}, u32[]{:S(2)}) copy-start(s32[32]{0:T(128)S(1)} %reshape.525.own_ref.refs_0_) | copy-start | bytes 388
  5.1 20.8 %all-to-all-start = ((s32[128,1,64]{2,1,0:T(1,128)}), s32[128,1,64]{2,1,0:T(1,128)S(1)}, u32[]{:S(2)}, u32[]{:S(2)}) async-start(s32[128,1,64]{2,1,0:T(1,128)} %copy.46), calls=%async_computation | async-start | bytes 131072 | tf_op jit(solution)/shard_map/all_to_all | solution.py:530
  26.0 1.0 copy-start.3
  29.2 1.8 copy-start
  31.1 52.6 %all-to-all-start.2 = ((bf16[128,112,128]{2,1,0:T(8,128)(2,1)}), bf16[128,112,128]{2,1,0:T(8,128)(2,1)}, u32[]{:S(2)}, u32[]{:S(2)}) async-start(bf16[128,112,128]{2,1,0:T(8,128)(2,1)} %copy-done), calls=%async_computation.2 | async-start | bytes 7340032 | tf_op jit(solution)/shard_map/all_to_all | solution.py:530
  55.5 11.9 %copy-start.9 = (bf16[2,128,128]{2,1,0:T(8,128)(2,1)S(1)}, bf16[2,128,128]{2,1,0:T(8,128)(2,1)}, u32[]{:S(2)}) copy-start(bf16[2,128,128]{2,1,0:T(8,128)(2,1)} %param.28) | copy-start | bytes 196612
  55.5 12.6 %copy-start.8 = (bf16[2,256,128]{2,1,0:T(8,128)(2,1)S(1)}, bf16[2,256,128]{2,1,0:T(8,128)(2,1)}, u32[]{:S(2)}) copy-start(bf16[2,256,128]{2,1,0:T(8,128)(2,1)} %param.25) | copy-start | bytes 393220
  55.5 13.3 %copy-start.7 = (bf16[2,256,256]{2,1,0:T(8,128)(2,1)S(1)}, bf16[2,256,256]{2,1,0:T(8,128)(2,1)}, u32[]{:S(2)}) copy-start(bf16[2,256,256]{2,1,0:T(8,128)(2,1)} %param.27) | copy-start | bytes 786436
  67.3 2.4 copy-start.5
  68.8 2.0 copy-start.4
  73.1 1.9 copy-start.1
  83.7 52.7 %all-to-all-start.1 = ((bf16[128,112,128]{2,1,0:T(8,128)(2,1)}), bf16[128,112,128]{2,1,0:T(8,128)(2,1)}, u32[]{:S(2)}, u32[]{:S(2)}) async-start(bf16[128,112,128]{2,1,0:T(8,128)(2,1)} %copy-done.1), calls=%async_computation.1 | async-start | bytes 7340032 | tf_op jit(solution)/shard_map/all_to_all | solution.py:530
  136.4 52.7 %all-to-all-start.3 = ((bf16[128,112,128]{2,1,0:T(8,128)(2,1)}), bf16[128,112,128]{2,1,0:T(8,128)(2,1)}, u32[]{:S(2)}, u32[]{:S(2)}) async-start(bf16[128,112,128]{2,1,0:T(8,128)(2,1)} %get-tuple-element.63), calls=%async_computation.3 | async-start | bytes 7340032 | tf_op jit(solution)/shard_map/all_to_all | solution.py:530
  165.4 3.8 %collective-permute-start = (bf16[4096,128]{1,0:T(8,128)(2,1)S(1)}, bf16[4096,128]{1,0:T(8,128)(2,1)S(1)}, u32[]{:S(2)}, u32[]{:S(2)}) collective-permute-start(bf16[4096,128]{1,0:T(8,128)(2,1)S(1)} %constant_dynamic-slice_fusion), channel_id=1, source_target_pairs={{0,1},{1,0},{2,3},{3,2},{4,5},{5,4},{6,7},{7,6},{8,9},{9,8},{10,11... | collective-permute-start | bytes 3145736 | tf_op jit(solution)/shard_map/ppermute | solution.py:444
  169.3 1.0 copy-start.6
  189.1 64.2 %all-to-all-start.4 = ((bf16[128,144,128]{2,1,0:T(8,128)(2,1)}), bf16[128,144,128]{2,1,0:T(8,128)(2,1)}, u32[]{:S(2)}, u32[]{:S(2)}) async-start(bf16[128,144,128]{2,1,0:T(8,128)(2,1)} %pad_maximum_fusion), calls=%async_computation.4 | async-start | bytes 9437184 | tf_op jit(solution)/shard_map/all_to_all | solution.py:530
  255.5 22.9 %all-to-all-start.5 = ((bf16[64,64,128]{2,1,0:T(8,128)(2,1)}), bf16[64,64,128]{2,1,0:T(8,128)(2,1)S(1)}, u32[]{:S(2)}, u32[]{:S(2)}) async-start(bf16[64,64,128]{2,1,0:T(8,128)(2,1)} %bitcast.103), calls=%async_computation.5 | async-start | bytes 2097152 | tf_op jit(solution)/shard_map/all_to_all | solution.py:603
  261.2 22.0 %copy-start.2 = (s32[2]{0:T(128)S(1)}, s32[2]{0:T(128)}, u32[]{:S(2)}) copy-start(s32[2]{0:T(128)} %pad_add_fusion.1.core_ref) | copy-start | bytes 28
  278.3 4.8 %collective-permute-start.1 = (bf16[64,2,32,128]{3,2,1,0:T(8,128)(2,1)S(1)}, bf16[64,2,32,128]{3,2,1,0:T(8,128)(2,1)S(1)}, u32[]{:S(2)}, u32[]{:S(2)}) collective-permute-start(bf16[64,2,32,128]{3,2,1,0:T(8,128)(2,1)S(1)} %bitcast.49), channel_id=1, source_target_pairs={{0,1},{1,0},{2,3},{3,2},{4,5},{5,4},{6,7},{7,6},{8,9},{9,8},{10,11... | collective-permute-start | bytes 3145736 | tf_op jit(solution)/shard_map/ppermute | solution.py:444

commit v5 on v4

--- a/solution.py
+++ b/solution.py
@@ -10,6 +10,7 @@
 F32 = jnp.float32
 BF16 = jnp.bfloat16
 CH = 112
+GROUPS = 27
 WEIGHT_ROWS = 8192
 WR = 32
 PICK = 64
@@ -86,10 +87,10 @@
             axis=0,
         )
         got = dot(left, right).astype(BF16)
-        out_ref[:, 16 * j : 16 * j + 16, :] = got[:, :128].reshape(PICK, 16, 128)
-        out_ref[:, 16 * (j + 3) : 16 * (j + 4), :] = got[:, 128:].reshape(PICK, 16, 128)
+        out_ref[:, 4 * j : 4 * j + 4] = got[:, :128].reshape(PICK, 4, 4, 128)
+        out_ref[:, 4 * (j + 3) : 4 * (j + 4)] = got[:, 128:].reshape(PICK, 4, 4, 128)
     last = dot(kinds[0], feat_ref[6]).astype(BF16)
-    out_ref[:, 96:112, :] = last.reshape(PICK, 16, 128)
+    out_ref[:, 24:27] = last.reshape(PICK, 4, 4, 128)[:, :3]
 
 
 def pick_rows(idx, eye, feat):
@@ -102,8 +103,8 @@
             whole((64, 64)),
             whole((9, 128, 128)),
         ],
-        out_specs=pl.BlockSpec((PICK, CH, 128), lambda c: (c, 0, 0)),
-        out_shape=jax.ShapeDtypeStruct((peers, CH, 128), BF16),
+        out_specs=pl.BlockSpec((PICK, GROUPS, 4, 128), lambda c: (c, 0, 0, 0)),
+        out_shape=jax.ShapeDtypeStruct((peers, GROUPS, 4, 128), BF16),
         compiler_params=pltpu.CompilerParams(vmem_limit_bytes=VMEM_LIMIT // 2),
         cost_estimate=pl.CostEstimate(flops=2 * 10**9, transcendentals=0, bytes_accessed=4 * 10**6),
         name="pick_rows",
@@ -161,7 +162,9 @@
 
 
 def turn(w_ref, r_ref, pair, owner):
-    chunk = r_ref[owner]
+    groups = r_ref[owner]
+    last = jnp.concatenate([groups[24:27], jnp.zeros((1, 4, 128), BF16)], axis=0).reshape(16, 128)
+    chunk = jnp.concatenate([groups[:24].reshape(96, 128), last], axis=0)
     right = jnp.concatenate([chunk, chunk, jnp.zeros((32, 128), BF16)], axis=0)
     return dot(w_ref[pair], right)
 
@@ -173,7 +176,8 @@
     lo = (x - hi.astype(F32)).astype(BF16)
     y = dot(v_ref[pair], jnp.concatenate([hi, lo], axis=1))
     y = y[:, :128] + y[:, 128:]
-    return (y[:CH] + y[CH:]).astype(BF16)
+    y = (y[:CH] + y[CH:]).astype(BF16)
+    return y.reshape(GROUPS + 1, 4, 128)[:GROUPS]
 
 
 def forward_body(
@@ -247,7 +251,7 @@
         in_specs=[SM] + [VM] * 11,
         out_specs=[VM] * 5,
         out_shape=[
-            jax.ShapeDtypeStruct((peers, CH, 128), BF16),
+            jax.ShapeDtypeStruct((peers, GROUPS, 4, 128), BF16),
             jax.ShapeDtypeStruct((rows, 2304), BF16),
             jax.ShapeDtypeStruct((rows, 1152), F32),
             jax.ShapeDtypeStruct((rows, 128), F32),
@@ -384,7 +388,7 @@
         in_specs=[SM] + [VM] * 15,
         out_specs=[VM, VM],
         out_shape=[
-            jax.ShapeDtypeStruct((peers, CH, 128), BF16),
+            jax.ShapeDtypeStruct((peers, GROUPS, 4, 128), BF16),
             jax.ShapeDtypeStruct((WEIGHT_ROWS, 128), BF16),
         ],
         scratch_shapes=[
@@ -399,7 +403,7 @@
     )(owners, got, *turns, *weights, *kept)
 
 
-def scatter_body(idx_ref, got_ref, out_ref, acc_ref, last_ref):
+def scatter_body(idx_ref, got_ref, out_ref, acc_ref, last_ref, *, first):
     @pl.when(pl.program_id(0) == 0)
     def _():
         acc_ref[...] = jnp.zeros(acc_ref.shape, F32)
@@ -410,7 +414,9 @@
         jnp.where(jnp.broadcast_to(idx_ref[v : v + 1, :], (128, 256)) == atom, 1.0, 0.0).astype(BF16)
         for v in range(4)
     ]
-    tiles = [got_ref[:, 16 * t : 16 * t + 16, :].reshape(256, 128) for t in range(7)]
+    tiles = [got_ref[:, first + 4 * t : first + 4 * t + 4].reshape(256, 128) for t in range(6)]
+    last = got_ref[:, first + 24 : first + 27]
+    tiles.append(jnp.concatenate([last, jnp.zeros((16, 1, 4, 128), BF16)], axis=1).reshape(256, 128))
     acc_ref[...] += dot(kinds[0], jnp.concatenate(tiles, axis=1))
     spare = jnp.concatenate([jnp.concatenate([tiles[j], tiles[j + 3]], axis=1) for j in range(3)], axis=0)
     last_ref[...] += dot(jnp.concatenate(kinds[1:], axis=1), spare)
@@ -424,13 +430,17 @@
 
 
 def add_rows(idx_rows, got, dtype):
-    peers = got.shape[0]
-    return pl.pallas_call(
-        scatter_body,
+    peers, groups = got.shape[:2]
+
+    def body(*refs):
+        scatter_body(*refs, first=groups - GROUPS)
+
+    return pl.pallas_call(
+        body,
         grid=(peers // 16,),
         in_specs=[
             pl.BlockSpec((8, 256), lambda c: (0, c)),
-            pl.BlockSpec((16, CH, 128), lambda c: (c, 0, 0)),
+            pl.BlockSpec((16, groups, 4, 128), lambda c: (c, 0, 0, 0)),
         ],
         out_specs=whole((9, 128, 128)),
         out_shape=jax.ShapeDtypeStruct((9, 128, 128), dtype),
@@ -450,13 +460,13 @@
     def body(core_ref, grads_ref, other_ref, out_ref):
         mine = grads_ref[pl.ds(pl.multiple_of(core_ref[0] * half, 16), half), :]
         total = mine.astype(F32) + other_ref[...].astype(F32)
-        out_ref[...] = total.astype(BF16).reshape(half // WR, WR, 128)
+        out_ref[...] = total.astype(BF16).reshape(half // WR, WR // 4, 4, 128)
 
     return pl.pallas_call(
         body,
         in_specs=[SM, VM, VM],
         out_specs=VM,
-        out_shape=jax.ShapeDtypeStruct((half // WR, WR, 128), BF16),
+        out_shape=jax.ShapeDtypeStruct((half // WR, WR // 4, 4, 128), BF16),
         cost_estimate=pl.CostEstimate(flops=10**6, transcendentals=0, bytes_accessed=4 * 10**6),
         name="add_pair",
     )(core, grads, other)
@@ -467,16 +477,17 @@
     chips = peers // 2
 
     def body(got_ref, out_ref):
-        x = got_ref[...].astype(F32).reshape(chips, 2, 16, 128)
+        x = got_ref[...].reshape(peers, WR, 128).astype(F32).reshape(chips, 2, WR, 128)
         total = jnp.sum(x, axis=0).astype(BF16)
-        out_ref[...] = jnp.broadcast_to(total[None], (chips, 2, 16, 128))
+        out_ref[...] = jnp.broadcast_to(total[None], (chips, 2, WR, 128))
 
     return pl.pallas_call(
         body,
-        grid=(WR // 16,),
-        in_specs=[pl.BlockSpec((peers, 16, 128), lambda i: (0, CH // 16 + i, 0))],
-        out_specs=pl.BlockSpec((chips, 2, 16, 128), lambda i: (0, 0, i, 0)),
+        grid=(1,),
+        in_specs=[pl.BlockSpec((peers, WR // 4, 4, 128), lambda i: (0, 0, 0, 0))],
+        out_specs=whole((chips, 2, WR, 128)),
         out_shape=jax.ShapeDtypeStruct((chips, 2, WR, 128), BF16),
+        compiler_params=pltpu.CompilerParams(vmem_limit_bytes=VMEM_LIMIT // 2),
         cost_estimate=pl.CostEstimate(flops=10**6, transcendentals=0, bytes_accessed=3 * 10**6),
         name="add_peers",
     )(got)
@@ -595,7 +606,7 @@
     half = WEIGHT_ROWS // 2
     sent = lax.dynamic_slice_in_dim(grads, (1 - core) * half, half, axis=0)
     w_rows = add_pair(cores, grads, swapped(sent))
-    both = jnp.concatenate([back_g, w_rows], axis=1)
+    both = jnp.concatenate([w_rows, back_g], axis=1)
     both, got_m = lax.optimization_barrier((both, got_m))
     messages = add_rows(asked_rows, got_m, BF16)
     got_g, messages = lax.optimization_barrier((exchange(both), messages))

time: 288 us -> 282 us (0.979)
  waiting for transfers between devices: 117 us -> 107 us
  Pallas kernels: 78.7 us -> 83.8 us
  local copies, waits for them, and re-layouts: 33.4 us -> 29.8 us
    all_to_all x5, waiting for transfers between devices: 103 us -> 93.3 us  [exchange(): return lax.all_to_all(x, 'atoms', split_axis=0, concat_axis=0, tiled=True)]
    unnamed x31 -> x27, local copies, waits for them, and re-layouts: 12.4 us -> 8.65 us
  transfers between devices with their start and end apart: 8 -> 8, of which waited for: 8 -> 8; matrix products, arithmetic and copies ran while one was open for 12% -> 13% of each run, Pallas kernels for 25% -> 27%
where the time goes in v5:
time: 282 us; the launch traced here: 280 us
  waiting for transfers between devices  107 us (38%)
  Pallas kernels  83.8 us (30%)
  starting transfers between devices  44.5 us (16%)
  local copies, waits for them, and re-layouts  29.8 us (11%)
  other arithmetic  13.9 us (5%)
    all_to_all x5, waiting for transfers between devices, exchange(): return lax.all_to_all(x, 'atoms', split_axis=0, concat_axis=0, tiled=True)  93.3 us
    all_to_all x5, starting transfers between devices, exchange(): return lax.all_to_all(x, 'atoms', split_axis=0, concat_axis=0, tiled=True)  35 us
    pallas_call x1, Pallas kernels, backward(): pl.pallas_call(body, in_specs=[SM] + [VM] * 15, out_specs=[VM, VM], out_s...  22.5 us
    pallas_call x1, Pallas kernels, forward(): pl.pallas_call(forward_body, in_specs=[SM] + [VM] * 11, out_specs=[VM] *...  19.6 us
    pallas_call x2, Pallas kernels, add_rows(): pl.pallas_call(body, grid=(peers // 16,), in_specs=[pl.BlockSpec((8, 256)...  13.7 us
    pallas_call x1, Pallas kernels, build_turns(): pl.pallas_call(prep_body, grid=(pairs,), in_specs=[pl.BlockSpec((1, 224,...  11.9 us
    all_to_all x1, waiting for transfers between devices, local(): lax.all_to_all(add_peers(got_g).reshape(peers // 2, 2 * WR, 128), 'atoms'...  10.2 us
    unnamed x27, local copies, waits for them, and re-layouts  8.65 us
  transfers between devices with their start and end apart: 8, of which 8 were waited for; matrix products, arithmetic and copies ran while one was open for 13% of the time, Pallas kernels for 27%

profile of v5, /device:TPU:1, one launch (start us, length us, event | category | flops | bytes accessed | tf_op | source)
XLA Modules:
  0.0 280.4 jit_solution(12639456344014790189)
XLA Ops:
  5.1 11.5 %all-to-all-start = ((s32[128,1,64]{2,1,0:T(1,128)}), s32[128,1,64]{2,1,0:T(1,128)S(1)}, u32[]{:S(2)}, u32[]{:S(2)}) async-start(s32[128,1,64]{2,1,0:T(1,128)} %copy.46), calls=%async_computation | async-start | bytes 131072 | tf_op jit(solution)/shard_map/all_to_all | solution.py:541
  21.8 4.1 %all-to-all-done = s32[128,1,64]{2,1,0:T(1,128)S(1)} async-done(((s32[128,1,64]{2,1,0:T(1,128)}), s32[128,1,64]{2,1,0:T(1,128)S(1)}, u32[]{:S(2)}, u32[]{:S(2)}) %all-to-all-start) | async-done | bytes 32800 | tf_op jit(solution)/shard_map/all_to_all | solution.py:541
  26.9 3.6 %pick_rows.3 = bf16[128,27,4,128]{3,2,1,0:T(4,128)(2,1)} custom-call(s32[128,64]{1,0:T(8,128)S(1)} %bitcast.51, bf16[64,64]{1,0:T(8,128)(2,1)S(1)} %fusion.eye_ref, bf16[9,128,128]{2,1,0:T(8,128)(2,1)S(1)} %bitcast.53), custom_call_target="tpu_custom_call" | custom-call | flops 2000000000 | bytes 4000000 | tf_op jit(solution)/shard_map/pick_rows/pallas_call | solution.py:98
  30.5 6.0 %all-to-all-start.2 = ((bf16[128,27,4,128]{3,2,1,0:T(4,128)(2,1)}), bf16[128,27,4,128]{3,2,1,0:T(4,128)(2,1)}, u32[]{:S(2)}, u32[]{:S(2)}) async-start(bf16[128,27,4,128]{3,2,1,0:T(4,128)(2,1)} %pick_rows.3), calls=%async_computation.2 | async-start | bytes 7077888 | tf_op jit(solution)/shard_map/all_to_all | solution.py:541
  46.3 6.0 %concatenate.57 = f32[32,9,16,24]{0,3,1,2:T(8,128)S(1)} concatenate(f32[9,9,16,24]{0,3,1,2:T(8,128)} %bitcast.101, f32[2,9,16,24]{0,3,1,2:T(8,128)} %broadcast_in_dim.32, f32[5,9,16,24]{0,3,1,2:T(8,128)} %broadcast_in_dim.33, f32[9,9,16,24]{0,3,1,2:T(8,128)} %bitcast.102, f32[7,9,16,24]{0,3,1,2:T(8,128)} %broadcast_in_dim.34), dimensions={0} | concatenate | bytes 884736 | tf_op jit(solution)/shard_map/concatenate | solution.py:586
  55.1 11.9 %build_turns.1 = (bf16[16,224,256]{2,1,0:T(8,128)(2,1)}, bf16[16,224,256]{2,1,0:T(8,128)(2,1)}, bf16[16,224,256]{2,1,0:T(8,128)(2,1)}, bf16[16,224,256]{2,1,0:T(8,128)(2,1)}) custom-call(f32[16,224,32]{2,1,0:T(8,128)} %pad.8.ra_ref, f32[16,32,256]{2,1,0:T(8,128)} %pad.9.rb_ref, bf16[32,256]{1,0:T(8,128)(2,1)} %constant.44.clone.sp_ref, ...), custom_call_target="tpu_custom_call" | custom-call | flops 1000000000 | bytes 10000000 | tf_op jit(solution)/shard_map/build_turns/pallas_call | solution.py:146
  70.5 3.7 %pick_rows.2 = bf16[128,27,4,128]{3,2,1,0:T(4,128)(2,1)} custom-call(s32[128,64]{1,0:T(8,128)S(1)} %bitcast.52, bf16[64,64]{1,0:T(8,128)(2,1)S(1)} %fusion.eye_ref, bf16[9,128,128]{2,1,0:T(8,128)(2,1)S(1)} %bitcast.54), custom_call_target="tpu_custom_call" | custom-call | flops 2000000000 | bytes 4000000 | tf_op jit(solution)/shard_map/pick_rows/pallas_call | solution.py:98
  74.2 7.7 %all-to-all-done.2.r_ref = bf16[128,27,4,128]{3,2,1,0:T(4,128)(2,1)} async-done(((bf16[128,27,4,128]{3,2,1,0:T(4,128)(2,1)}), bf16[128,27,4,128]{3,2,1,0:T(4,128)(2,1)}, u32[]{:S(2)}, u32[]{:S(2)}) %all-to-all-start.2) | async-done | bytes 3538976 | tf_op jit(solution)/shard_map/all_to_all | solution.py:541
  81.9 5.8 %all-to-all-start.1 = ((bf16[128,27,4,128]{3,2,1,0:T(4,128)(2,1)}), bf16[128,27,4,128]{3,2,1,0:T(4,128)(2,1)}, u32[]{:S(2)}, u32[]{:S(2)}) async-start(bf16[128,27,4,128]{3,2,1,0:T(4,128)(2,1)} %pick_rows.2), calls=%async_computation.1 | async-start | bytes 7077888 | tf_op jit(solution)/shard_map/all_to_all | solution.py:541
  87.8 19.6 %forward.1 = (bf16[128,27,4,128]{3,2,1,0:T(4,128)(2,1)}, bf16[768,2304]{1,0:T(8,128)(2,1)}, f32[768,1152]{1,0:T(8,128)}, f32[768,128]{1,0:T(8,128)}, bf16[768,1152]{1,0:T(8,128)(2,1)}) custom-call(s32[32]{0:T(128)} %copy-done.8, bf16[128,27,4,128]{3,2,1,0:T(4,128)(2,1)} %all-to-all-done.2.r_ref, bf16[16,224,256]{2,1,0:T(8,128)(2,1)} %get-tuple-element.47.wt_ref.refs_2_, ...), custom_call_target="tpu_custom_call" | custom-call | flops 10000000000 | bytes 30000000 | tf_op jit(solution)/shard_map/forward/pallas_call | solution.py:249
  107.4 25.8 %all-to-all-done.1.refs_1_ = bf16[128,27,4,128]{3,2,1,0:T(4,128)(2,1)} async-done(((bf16[128,27,4,128]{3,2,1,0:T(4,128)(2,1)}), bf16[128,27,4,128]{3,2,1,0:T(4,128)(2,1)}, u32[]{:S(2)}, u32[]{:S(2)}) %all-to-all-start.1) | async-done | bytes 3538976 | tf_op jit(solution)/shard_map/all_to_all | solution.py:541
  133.2 5.8 %all-to-all-start.3 = ((bf16[128,27,4,128]{3,2,1,0:T(4,128)(2,1)}), bf16[128,27,4,128]{3,2,1,0:T(4,128)(2,1)}, u32[]{:S(2)}, u32[]{:S(2)}) async-start(bf16[128,27,4,128]{3,2,1,0:T(4,128)(2,1)} %get-tuple-element.63), calls=%async_computation.3 | async-start | bytes 7077888 | tf_op jit(solution)/shard_map/all_to_all | solution.py:541
  139.1 22.5 %backward.1 = (bf16[128,27,4,128]{3,2,1,0:T(4,128)(2,1)}, bf16[8192,128]{1,0:T(8,128)(2,1)}) custom-call(s32[32]{0:T(128)} %copy-done.8, bf16[128,27,4,128]{3,2,1,0:T(4,128)(2,1)} %all-to-all-done.1.refs_1_, bf16[16,224,256]{2,1,0:T(8,128)(2,1)} %get-tuple-element.47.wt_ref.refs_2_, bf16[16,224,256]{2,1,0:T(8,128)(2,1)} %get-tuple-element.48.ws_ref.refs_3_, ...), custom_call_target="tpu_custom_call" | custom-call | flops 20000000000 | bytes 30000000 | tf_op jit(solution)/shard_map/backward/pallas_call | solution.py:386
  167.6 3.2 %add_pair.1 = bf16[128,8,4,128]{3,2,1,0:T(4,128)(2,1)} custom-call(s32[2]{0:T(128)} %pad_add_fusion.1.core_ref, bf16[8192,128]{1,0:T(8,128)(2,1)} %get-tuple-element.61.grads_ref, bf16[4096,128]{1,0:T(8,128)(2,1)} %copy-done.4), custom_call_target="tpu_custom_call" | custom-call | flops 1000000 | bytes 4000000 | tf_op jit(solution)/shard_map/add_pair/pallas_call | solution.py:465
  170.9 7.4 %pad_maximum_fusion = bf16[128,35,4,128]{3,2,1,0:T(4,128)(2,1)} fusion(bf16[128,27,4,128]{3,2,1,0:T(4,128)(2,1)} %get-tuple-element.62, bf16[128,8,4,128]{3,2,1,0:T(4,128)(2,1)} %add_pair.1), kind=kLoop, calls=%fused_computation | loop fusion | flops 2293760 | bytes 9175040 | tf_op jit(solution)/shard_map/concatenate | solution.py:609
  178.3 6.2 %all-to-all-done.3.refs_1_ = bf16[128,27,4,128]{3,2,1,0:T(4,128)(2,1)} async-done(((bf16[128,27,4,128]{3,2,1,0:T(4,128)(2,1)}), bf16[128,27,4,128]{3,2,1,0:T(4,128)(2,1)}, u32[]{:S(2)}, u32[]{:S(2)}) %all-to-all-start.3) | async-done | bytes 3538976 | tf_op jit(solution)/shard_map/all_to_all | solution.py:541
  184.5 5.8 %all-to-all-start.4 = ((bf16[128,35,4,128]{3,2,1,0:T(4,128)(2,1)}), bf16[128,35,4,128]{3,2,1,0:T(4,128)(2,1)}, u32[]{:S(2)}, u32[]{:S(2)}) async-start(bf16[128,35,4,128]{3,2,1,0:T(4,128)(2,1)} %pad_maximum_fusion), calls=%async_computation.4 | async-start | bytes 9175040 | tf_op jit(solution)/shard_map/all_to_all | solution.py:541
  191.4 6.7 %add_rows.2 = bf16[9,128,128]{2,1,0:T(8,128)(2,1)} custom-call(s32[8,2048]{1,0:T(8,128)} %pad_add_fusion.refs_0_, bf16[128,27,4,128]{3,2,1,0:T(4,128)(2,1)} %all-to-all-done.3.refs_1_), custom_call_target="tpu_custom_call" | custom-call | flops 1000000000 | bytes 6000000 | tf_op jit(solution)/shard_map/add_rows/pallas_call | solution.py:438
  198.1 49.3 %all-to-all-done.4.got_ref.refs_1_ = bf16[128,35,4,128]{3,2,1,0:T(4,128)(2,1)} async-done(((bf16[128,35,4,128]{3,2,1,0:T(4,128)(2,1)}), bf16[128,35,4,128]{3,2,1,0:T(4,128)(2,1)}, u32[]{:S(2)}, u32[]{:S(2)}) %all-to-all-start.4) | async-done | bytes 4587552 | tf_op jit(solution)/shard_map/all_to_all | solution.py:541
  247.4 2.6 add_peers.1
  250.0 5.6 %all-to-all-start.5 = ((bf16[64,64,128]{2,1,0:T(8,128)(2,1)}), bf16[64,64,128]{2,1,0:T(8,128)(2,1)S(1)}, u32[]{:S(2)}, u32[]{:S(2)}) async-start(bf16[64,64,128]{2,1,0:T(8,128)(2,1)} %bitcast.23), calls=%async_computation.5 | async-start | bytes 2097152 | tf_op jit(solution)/shard_map/all_to_all | solution.py:614
  255.6 7.0 %add_rows.3 = f32[9,128,128]{2,1,0:T(8,128)} custom-call(s32[8,2048]{1,0:T(8,128)} %pad_add_fusion.refs_0_, bf16[128,35,4,128]{3,2,1,0:T(4,128)(2,1)} %all-to-all-done.4.got_ref.refs_1_), custom_call_target="tpu_custom_call" | custom-call | flops 1000000000 | bytes 6000000 | tf_op jit(solution)/shard_map/add_rows/pallas_call | solution.py:438
  262.6 10.2 %all-to-all-done.5 = bf16[64,64,128]{2,1,0:T(8,128)(2,1)S(1)} async-done(((bf16[64,64,128]{2,1,0:T(8,128)(2,1)}), bf16[64,64,128]{2,1,0:T(8,128)(2,1)S(1)}, u32[]{:S(2)}, u32[]{:S(2)}) %all-to-all-start.5) | async-done | bytes 1048608 | tf_op jit(solution)/shard_map/all_to_all | solution.py:614
  277.5 2.9 %unpack.1 = (f32[1,768,512]{2,1,0:T(8,128)}, f32[2,512,256]{2,1,0:T(8,128)}, f32[2,256,128]{2,1,0:T(8,128)}, f32[1,384,384]{2,1,0:T(8,128)}, f32[2,256,256]{2,1,0:T(8,128)}, /*index=5*/f32[2,128,128]{2,1,0:T(8,128)}) custom-call(s32[2]{0:T(128)S(1)} %copy-done, bf16[64,2,32,128]{3,2,1,0:T(8,128)(2,1)S(1)} %bitcast.50, ...), custom_call_target="tpu_custom_call" | custom-call | flops 1000000 | bytes 6000000 | tf_op jit(solution)/shard_map/unpack/pallas_call | solution.py:522
  (79 shorter events, 38.4 us)
Async XLA Ops:
  2.4 28.1 %copy-start.8 = (s32[32]{0:T(128)}, s32[32]{0:T(128)S(1)}, u32[]{:S(2)}) copy-start(s32[32]{0:T(128)S(1)} %reshape.525.own_ref.refs_0_) | copy-start | bytes 388
  5.1 20.8 %all-to-all-start = ((s32[128,1,64]{2,1,0:T(1,128)}), s32[128,1,64]{2,1,0:T(1,128)S(1)}, u32[]{:S(2)}, u32[]{:S(2)}) async-start(s32[128,1,64]{2,1,0:T(1,128)} %copy.46), calls=%async_computation | async-start | bytes 131072 | tf_op jit(solution)/shard_map/all_to_all | solution.py:541
  26.0 1.0 copy-start.1
  30.5 51.4 %all-to-all-start.2 = ((bf16[128,27,4,128]{3,2,1,0:T(4,128)(2,1)}), bf16[128,27,4,128]{3,2,1,0:T(4,128)(2,1)}, u32[]{:S(2)}, u32[]{:S(2)}) async-start(bf16[128,27,4,128]{3,2,1,0:T(4,128)(2,1)} %pick_rows.3), calls=%async_computation.2 | async-start | bytes 7077888 | tf_op jit(solution)/shard_map/all_to_all | solution.py:541
  55.1 11.9 %copy-start.7 = (bf16[2,128,128]{2,1,0:T(8,128)(2,1)S(1)}, bf16[2,128,128]{2,1,0:T(8,128)(2,1)}, u32[]{:S(2)}) copy-start(bf16[2,128,128]{2,1,0:T(8,128)(2,1)} %param.28) | copy-start | bytes 196612
  55.1 12.7 %copy-start.6 = (bf16[2,256,128]{2,1,0:T(8,128)(2,1)S(1)}, bf16[2,256,128]{2,1,0:T(8,128)(2,1)}, u32[]{:S(2)}) copy-start(bf16[2,256,128]{2,1,0:T(8,128)(2,1)} %param.25) | copy-start | bytes 393220
  55.1 13.4 %copy-start.5 = (bf16[2,256,256]{2,1,0:T(8,128)(2,1)S(1)}, bf16[2,256,256]{2,1,0:T(8,128)(2,1)}, u32[]{:S(2)}) copy-start(bf16[2,256,256]{2,1,0:T(8,128)(2,1)} %param.27) | copy-start | bytes 786436
  67.0 2.4 copy-start.3
  68.5 2.0 copy-start.2
  81.9 51.3 %all-to-all-start.1 = ((bf16[128,27,4,128]{3,2,1,0:T(4,128)(2,1)}), bf16[128,27,4,128]{3,2,1,0:T(4,128)(2,1)}, u32[]{:S(2)}, u32[]{:S(2)}) async-start(bf16[128,27,4,128]{3,2,1,0:T(4,128)(2,1)} %pick_rows.2), calls=%async_computation.1 | async-start | bytes 7077888 | tf_op jit(solution)/shard_map/all_to_all | solution.py:541
  133.2 51.3 %all-to-all-start.3 = ((bf16[128,27,4,128]{3,2,1,0:T(4,128)(2,1)}), bf16[128,27,4,128]{3,2,1,0:T(4,128)(2,1)}, u32[]{:S(2)}, u32[]{:S(2)}) async-start(bf16[128,27,4,128]{3,2,1,0:T(4,128)(2,1)} %get-tuple-element.63), calls=%async_computation.3 | async-start | bytes 7077888 | tf_op jit(solution)/shard_map/all_to_all | solution.py:541
  162.8 3.8 %collective-permute-start = (bf16[4096,128]{1,0:T(8,128)(2,1)S(1)}, bf16[4096,128]{1,0:T(8,128)(2,1)S(1)}, u32[]{:S(2)}, u32[]{:S(2)}) collective-permute-start(bf16[4096,128]{1,0:T(8,128)(2,1)S(1)} %constant_dynamic-slice_fusion), channel_id=1, source_target_pairs={{0,1},{1,0},{2,3},{3,2},{4,5},{5,4},{6,7},{7,6},{8,9},{9,8},{10,11... | collective-permute-start | bytes 3145736 | tf_op jit(solution)/shard_map/ppermute | solution.py:454
  166.7 1.0 copy-start.4
  184.5 62.9 %all-to-all-start.4 = ((bf16[128,35,4,128]{3,2,1,0:T(4,128)(2,1)}), bf16[128,35,4,128]{3,2,1,0:T(4,128)(2,1)}, u32[]{:S(2)}, u32[]{:S(2)}) async-start(bf16[128,35,4,128]{3,2,1,0:T(4,128)(2,1)} %pad_maximum_fusion), calls=%async_computation.4 | async-start | bytes 9175040 | tf_op jit(solution)/shard_map/all_to_all | solution.py:541
  250.0 22.7 %all-to-all-start.5 = ((bf16[64,64,128]{2,1,0:T(8,128)(2,1)}), bf16[64,64,128]{2,1,0:T(8,128)(2,1)S(1)}, u32[]{:S(2)}, u32[]{:S(2)}) async-start(bf16[64,64,128]{2,1,0:T(8,128)(2,1)} %bitcast.23), calls=%async_computation.5 | async-start | bytes 2097152 | tf_op jit(solution)/shard_map/all_to_all | solution.py:614
  255.5 22.0 %copy-start = (s32[2]{0:T(128)S(1)}, s32[2]{0:T(128)}, u32[]{:S(2)}) copy-start(s32[2]{0:T(128)} %pad_add_fusion.1.core_ref) | copy-start | bytes 28
  272.7 4.8 %collective-permute-start.1 = (bf16[64,2,32,128]{3,2,1,0:T(8,128)(2,1)S(1)}, bf16[64,2,32,128]{3,2,1,0:T(8,128)(2,1)S(1)}, u32[]{:S(2)}, u32[]{:S(2)}) collective-permute-start(bf16[64,2,32,128]{3,2,1,0:T(8,128)(2,1)S(1)} %bitcast.49), channel_id=1, source_target_pairs={{0,1},{1,0},{2,3},{3,2},{4,5},{5,4},{6,7},{7,6},{8,9},{9,8},{10,11... | collective-permute-start | bytes 3145736 | tf_op jit(solution)/shard_map/ppermute | solution.py:454

commit v6 on v5

--- a/solution.py
+++ b/solution.py
@@ -91,6 +91,39 @@
         out_ref[:, 4 * (j + 3) : 4 * (j + 4)] = got[:, 128:].reshape(PICK, 4, 4, 128)
     last = dot(kinds[0], feat_ref[6]).astype(BF16)
     out_ref[:, 24:27] = last.reshape(PICK, 4, 4, 128)[:, :3]
+
+
+def request_body(blocks_ref, rows_ref, cols_ref, out_ref, seen_ref):
+    peers, ends = out_ref.shape[0], 2 * blocks_ref.shape[0]
+    out_ref[...] = jnp.full(out_ref.shape, -1, jnp.int32)
+
+    def clear(o, carry):
+        seen_ref[o] = 0
+        return carry
+
+    lax.fori_loop(0, peers, clear, 0, unroll=8)
+    cols = cols_ref[...]
+    for end in range(ends):
+        pair, side = divmod(end, 2)
+        owner = blocks_ref[pair, side]
+        slot = seen_ref[owner]
+        seen_ref[owner] = slot + 1
+        line = out_ref[owner]
+        for k in range(6):
+            line = jnp.where(cols == 6 * slot + k, rows_ref[side, k, pair], line)
+        out_ref[owner] = line
+
+
+def request_rows(blocks, rows, peers):
+    cols = jnp.asarray(request_columns()[None], jnp.int32)
+    return pl.pallas_call(
+        request_body,
+        in_specs=[SM, SM, VM],
+        out_specs=VM,
+        out_shape=jax.ShapeDtypeStruct((peers, 1, 64), jnp.int32),
+        scratch_shapes=[pltpu.SMEM((peers,), jnp.int32)],
+        name="request_rows",
+    )(blocks, rows, cols)
 
 
 def pick_rows(idx, eye, feat):
@@ -477,15 +510,15 @@
     chips = peers // 2
 
     def body(got_ref, out_ref):
-        x = got_ref[...].reshape(peers, WR, 128).astype(F32).reshape(chips, 2, WR, 128)
+        x = got_ref[...].reshape(peers, 16, 128).astype(F32).reshape(chips, 2, 16, 128)
         total = jnp.sum(x, axis=0).astype(BF16)
-        out_ref[...] = jnp.broadcast_to(total[None], (chips, 2, WR, 128))
+        out_ref[...] = jnp.broadcast_to(total[None], (chips, 2, 16, 128))
 
     return pl.pallas_call(
         body,
-        grid=(1,),
-        in_specs=[pl.BlockSpec((peers, WR // 4, 4, 128), lambda i: (0, 0, 0, 0))],
-        out_specs=whole((chips, 2, WR, 128)),
+        grid=(WR // 16,),
+        in_specs=[pl.BlockSpec((peers, 4, 4, 128), lambda i: (0, i, 0, 0))],
+        out_specs=pl.BlockSpec((chips, 2, 16, 128), lambda i: (0, 0, i, 0)),
         out_shape=jax.ShapeDtypeStruct((chips, 2, WR, 128), BF16),
         compiler_params=pltpu.CompilerParams(vmem_limit_bytes=VMEM_LIMIT // 2),
         cost_estimate=pl.CostEstimate(flops=10**6, transcendentals=0, bytes_accessed=3 * 10**6),
@@ -501,30 +534,23 @@
 def unpack(core, mine, other):
     chips = mine.shape[0]
 
-    def body(core_ref, mine_ref, other_ref, *refs):
-        outs, all_ref = refs[:-1], refs[-1]
-
-        def place(chip, carry):
-            for half in range(2):
-                at = half * 2 * chips + 2 * chip
-                all_ref[at + core_ref[0]] = mine_ref[chip, half]
-                all_ref[at + 1 - core_ref[0]] = other_ref[chip, half]
-            return carry
-
-        lax.fori_loop(0, chips, place, 0, unroll=4)
+    def body(core_ref, mine_ref, other_ref, *outs):
         for out, (row, parts, height, blocks) in zip(outs, WEIGHT_PARTS):
             for p in range(parts):
                 for n in range(blocks):
-                    low = (row + (p * blocks + n) * height) // WR
-                    value = all_ref[low : low + height // WR].reshape(height, 128)
-                    out[p, :, 128 * n : 128 * n + 128] = value.astype(F32)
+                    cols = slice(128 * n, 128 * n + 128)
+                    for at in range(0, height, 2 * WR):
+                        half, chip = divmod((row + (p * blocks + n) * height + at) // (2 * WR), chips)
+                        low = pl.multiple_of(at + WR * core_ref[0], WR)
+                        out[p, pl.ds(low, WR), cols] = mine_ref[chip, half].astype(F32)
+                        low = pl.multiple_of(at + WR * (1 - core_ref[0]), WR)
+                        out[p, pl.ds(low, WR), cols] = other_ref[chip, half].astype(F32)
 
     return pl.pallas_call(
         body,
         in_specs=[SM, VM, VM],
         out_specs=[VM] * 6,
         out_shape=[jax.ShapeDtypeStruct((parts, height, 128 * blocks), F32) for _, parts, height, blocks in WEIGHT_PARTS],
-        scratch_shapes=[pltpu.VMEM((4 * chips, WR, 128), BF16)],
         compiler_params=pltpu.CompilerParams(vmem_limit_bytes=VMEM_LIMIT // 2),
         cost_estimate=pl.CostEstimate(flops=10**6, transcendentals=0, bytes_accessed=6 * 10**6),
         name="unpack",
@@ -555,16 +581,7 @@
         jnp.logical_and(owners[:, None] == owners[None, :], ends[:, None] > ends[None, :]), axis=1
     ).astype(jnp.int32)
 
-    end_rows = jnp.transpose(pair_rows, (2, 0, 1)).reshape(2 * pairs, 6)
-    cols = request_columns()
-    row_cols = jnp.concatenate([end_rows[:, max(c, 0) % 6 : max(c, 0) % 6 + 1] for c in cols], axis=1)
-    col_slot = jnp.asarray(np.where(cols < 0, -1, cols // 6), jnp.int32)
-    peer = jnp.arange(peers, dtype=jnp.int32)
-    hit = jnp.logical_and(
-        owners[None, :, None] == peer[:, None, None], slots[None, :, None] == col_slot[None, None, :]
-    )
-    request = jnp.sum(jnp.where(hit, row_cols[None] + 1, 0), axis=1) - 1
-    asked = exchange(request)
+    asked = exchange(request_rows(pair_blocks, pair_rows, peers)).reshape(peers, 64)
     asked_rows = jnp.transpose(asked.reshape(peers, 4, 16), (1, 0, 2)).reshape(4, peers * 16)
     asked_rows = jnp.concatenate([asked_rows, asked_rows], axis=0)
     eye = jnp.eye(64, dtype=BF16)

time: 282 us -> 283 us (level)
    unnamed x27 -> x28, local copies, waits for them, and re-layouts: 8.65 us -> 10.5 us
  transfers between devices with their start and end apart: 8 -> 8, of which waited for: 8 -> 8; matrix products, arithmetic and copies ran while one was open for 13% -> 14% of each run, Pallas kernels for 27% -> 27%
where the time goes in v6:
time: 283 us; the launch traced here: 281 us
  waiting for transfers between devices  106 us (37%)
  Pallas kernels  85.3 us (30%)
  starting transfers between devices  45.5 us (16%)
  local copies, waits for them, and re-layouts  30.5 us (11%)
  other arithmetic  12.4 us (4%)
    all_to_all x5, waiting for transfers between devices, exchange(): return lax.all_to_all(x, 'atoms', split_axis=0, concat_axis=0, tiled=True)  92.3 us
    all_to_all x5, starting transfers between devices, exchange(): return lax.all_to_all(x, 'atoms', split_axis=0, concat_axis=0, tiled=True)  35.9 us
    pallas_call x1, Pallas kernels, backward(): pl.pallas_call(body, in_specs=[SM] + [VM] * 15, out_specs=[VM, VM], out_s...  22.5 us
    pallas_call x1, Pallas kernels, forward(): pl.pallas_call(forward_body, in_specs=[SM] + [VM] * 11, out_specs=[VM] *...  19.6 us
    pallas_call x2, Pallas kernels, add_rows(): pl.pallas_call(body, grid=(peers // 16,), in_specs=[pl.BlockSpec((8, 256)...  13.7 us
    pallas_call x1, Pallas kernels, build_turns(): pl.pallas_call(prep_body, grid=(pairs,), in_specs=[pl.BlockSpec((1, 224,...  11.9 us
    unnamed x28, local copies, waits for them, and re-layouts  10.5 us
    all_to_all x1, waiting for transfers between devices, local(): lax.all_to_all(add_peers(got_g).reshape(peers // 2, 2 * WR, 128), 'atoms'...  10.2 us
  transfers between devices with their start and end apart: 8, of which 8 were waited for; matrix products, arithmetic and copies ran while one was open for 14% of the time, Pallas kernels for 27%

profile of v6, /device:TPU:1, one launch (start us, length us, event | category | flops | bytes accessed | tf_op | source)
XLA Modules:
  0.0 281.1 jit_solution(262020742185967127)
XLA Ops:
  5.3 11.5 %all-to-all-start = ((s32[128,1,64]{2,1,0:T(1,128)}), s32[128,1,64]{2,1,0:T(1,128)S(1)}, u32[]{:S(2)}, u32[]{:S(2)}) async-start(s32[128,1,64]{2,1,0:T(1,128)} %request_rows.1), calls=%async_computation | async-start | bytes 131072 | tf_op jit(solution)/shard_map/all_to_all | solution.py:567
  23.0 3.1 %all-to-all-done = s32[128,1,64]{2,1,0:T(1,128)S(1)} async-done(((s32[128,1,64]{2,1,0:T(1,128)}), s32[128,1,64]{2,1,0:T(1,128)S(1)}, u32[]{:S(2)}, u32[]{:S(2)}) %all-to-all-start) | async-done | bytes 32800 | tf_op jit(solution)/shard_map/all_to_all | solution.py:567
  27.1 3.6 %pick_rows.3 = bf16[128,27,4,128]{3,2,1,0:T(4,128)(2,1)} custom-call(s32[128,64]{1,0:T(8,128)S(1)} %bitcast.46, bf16[64,64]{1,0:T(8,128)(2,1)S(1)} %fusion.eye_ref, bf16[9,128,128]{2,1,0:T(8,128)(2,1)S(1)} %bitcast.48), custom_call_target="tpu_custom_call" | custom-call | flops 2000000000 | bytes 4000000 | tf_op jit(solution)/shard_map/pick_rows/pallas_call | solution.py:131
  30.7 7.0 %all-to-all-start.2 = ((bf16[128,27,4,128]{3,2,1,0:T(4,128)(2,1)}), bf16[128,27,4,128]{3,2,1,0:T(4,128)(2,1)}, u32[]{:S(2)}, u32[]{:S(2)}) async-start(bf16[128,27,4,128]{3,2,1,0:T(4,128)(2,1)} %pick_rows.3), calls=%async_computation.2 | async-start | bytes 7077888 | tf_op jit(solution)/shard_map/all_to_all | solution.py:567
  47.4 5.9 %concatenate.45 = f32[32,9,16,24]{0,3,1,2:T(8,128)S(1)} concatenate(f32[9,9,16,24]{0,3,1,2:T(8,128)} %bitcast.52, f32[2,9,16,24]{0,3,1,2:T(8,128)} %broadcast_in_dim.6, f32[5,9,16,24]{0,3,1,2:T(8,128)} %broadcast_in_dim.7, f32[9,9,16,24]{0,3,1,2:T(8,128)} %bitcast.53, f32[7,9,16,24]{0,3,1,2:T(8,128)} %broadcast_in_dim.16), dimensions={0} | concatenate | bytes 884736 | tf_op jit(solution)/shard_map/concatenate | solution.py:603
  56.2 11.9 %build_turns.1 = (bf16[16,224,256]{2,1,0:T(8,128)(2,1)}, bf16[16,224,256]{2,1,0:T(8,128)(2,1)}, bf16[16,224,256]{2,1,0:T(8,128)(2,1)}, bf16[16,224,256]{2,1,0:T(8,128)(2,1)}) custom-call(f32[16,224,32]{2,1,0:T(8,128)} %pad.8.ra_ref, f32[16,32,256]{2,1,0:T(8,128)} %pad.9.rb_ref, bf16[32,256]{1,0:T(8,128)(2,1)} %constant.40.clone.sp_ref, ...), custom_call_target="tpu_custom_call" | custom-call | flops 1000000000 | bytes 10000000 | tf_op jit(solution)/shard_map/build_turns/pallas_call | solution.py:179
  71.6 3.7 %pick_rows.2 = bf16[128,27,4,128]{3,2,1,0:T(4,128)(2,1)} custom-call(s32[128,64]{1,0:T(8,128)S(1)} %bitcast.47, bf16[64,64]{1,0:T(8,128)(2,1)S(1)} %fusion.eye_ref, bf16[9,128,128]{2,1,0:T(8,128)(2,1)S(1)} %bitcast.49), custom_call_target="tpu_custom_call" | custom-call | flops 2000000000 | bytes 4000000 | tf_op jit(solution)/shard_map/pick_rows/pallas_call | solution.py:131
  75.3 7.8 %all-to-all-done.2.r_ref = bf16[128,27,4,128]{3,2,1,0:T(4,128)(2,1)} async-done(((bf16[128,27,4,128]{3,2,1,0:T(4,128)(2,1)}), bf16[128,27,4,128]{3,2,1,0:T(4,128)(2,1)}, u32[]{:S(2)}, u32[]{:S(2)}) %all-to-all-start.2) | async-done | bytes 3538976 | tf_op jit(solution)/shard_map/all_to_all | solution.py:567
  83.1 5.8 %all-to-all-start.1 = ((bf16[128,27,4,128]{3,2,1,0:T(4,128)(2,1)}), bf16[128,27,4,128]{3,2,1,0:T(4,128)(2,1)}, u32[]{:S(2)}, u32[]{:S(2)}) async-start(bf16[128,27,4,128]{3,2,1,0:T(4,128)(2,1)} %pick_rows.2), calls=%async_computation.1 | async-start | bytes 7077888 | tf_op jit(solution)/shard_map/all_to_all | solution.py:567
  88.9 19.6 %forward.1 = (bf16[128,27,4,128]{3,2,1,0:T(4,128)(2,1)}, bf16[768,2304]{1,0:T(8,128)(2,1)}, f32[768,1152]{1,0:T(8,128)}, f32[768,128]{1,0:T(8,128)}, bf16[768,1152]{1,0:T(8,128)(2,1)}) custom-call(s32[32]{0:T(128)} %copy-done.8, bf16[128,27,4,128]{3,2,1,0:T(4,128)(2,1)} %all-to-all-done.2.r_ref, bf16[16,224,256]{2,1,0:T(8,128)(2,1)} %get-tuple-element.47.wt_ref.refs_2_, ...), custom_call_target="tpu_custom_call" | custom-call | flops 10000000000 | bytes 30000000 | tf_op jit(solution)/shard_map/forward/pallas_call | solution.py:282
  108.5 25.8 %all-to-all-done.1.refs_1_ = bf16[128,27,4,128]{3,2,1,0:T(4,128)(2,1)} async-done(((bf16[128,27,4,128]{3,2,1,0:T(4,128)(2,1)}), bf16[128,27,4,128]{3,2,1,0:T(4,128)(2,1)}, u32[]{:S(2)}, u32[]{:S(2)}) %all-to-all-start.1) | async-done | bytes 3538976 | tf_op jit(solution)/shard_map/all_to_all | solution.py:567
  134.4 5.8 %all-to-all-start.3 = ((bf16[128,27,4,128]{3,2,1,0:T(4,128)(2,1)}), bf16[128,27,4,128]{3,2,1,0:T(4,128)(2,1)}, u32[]{:S(2)}, u32[]{:S(2)}) async-start(bf16[128,27,4,128]{3,2,1,0:T(4,128)(2,1)} %get-tuple-element.63), calls=%async_computation.3 | async-start | bytes 7077888 | tf_op jit(solution)/shard_map/all_to_all | solution.py:567
  140.2 22.5 %backward.1 = (bf16[128,27,4,128]{3,2,1,0:T(4,128)(2,1)}, bf16[8192,128]{1,0:T(8,128)(2,1)}) custom-call(s32[32]{0:T(128)} %copy-done.8, bf16[128,27,4,128]{3,2,1,0:T(4,128)(2,1)} %all-to-all-done.1.refs_1_, bf16[16,224,256]{2,1,0:T(8,128)(2,1)} %get-tuple-element.47.wt_ref.refs_2_, bf16[16,224,256]{2,1,0:T(8,128)(2,1)} %get-tuple-element.48.ws_ref.refs_3_, ...), custom_call_target="tpu_custom_call" | custom-call | flops 20000000000 | bytes 30000000 | tf_op jit(solution)/shard_map/backward/pallas_call | solution.py:419
  168.8 3.2 %add_pair.1 = bf16[128,8,4,128]{3,2,1,0:T(4,128)(2,1)} custom-call(s32[2]{0:T(128)} %pad_add_fusion.1.core_ref, bf16[8192,128]{1,0:T(8,128)(2,1)} %get-tuple-element.61.grads_ref, bf16[4096,128]{1,0:T(8,128)(2,1)} %copy-done.4), custom_call_target="tpu_custom_call" | custom-call | flops 1000000 | bytes 4000000 | tf_op jit(solution)/shard_map/add_pair/pallas_call | solution.py:498
  172.0 7.4 %pad_maximum_fusion = bf16[128,35,4,128]{3,2,1,0:T(4,128)(2,1)} fusion(bf16[128,27,4,128]{3,2,1,0:T(4,128)(2,1)} %get-tuple-element.62, bf16[128,8,4,128]{3,2,1,0:T(4,128)(2,1)} %add_pair.1), kind=kLoop, calls=%fused_computation | loop fusion | flops 2293760 | bytes 9175040 | tf_op jit(solution)/shard_map/concatenate | solution.py:626
  179.4 6.2 %all-to-all-done.3.refs_1_ = bf16[128,27,4,128]{3,2,1,0:T(4,128)(2,1)} async-done(((bf16[128,27,4,128]{3,2,1,0:T(4,128)(2,1)}), bf16[128,27,4,128]{3,2,1,0:T(4,128)(2,1)}, u32[]{:S(2)}, u32[]{:S(2)}) %all-to-all-start.3) | async-done | bytes 3538976 | tf_op jit(solution)/shard_map/all_to_all | solution.py:567
  185.7 5.8 %all-to-all-start.4 = ((bf16[128,35,4,128]{3,2,1,0:T(4,128)(2,1)}), bf16[128,35,4,128]{3,2,1,0:T(4,128)(2,1)}, u32[]{:S(2)}, u32[]{:S(2)}) async-start(bf16[128,35,4,128]{3,2,1,0:T(4,128)(2,1)} %pad_maximum_fusion), calls=%async_computation.4 | async-start | bytes 9175040 | tf_op jit(solution)/shard_map/all_to_all | solution.py:567
  192.5 6.7 %add_rows.2 = bf16[9,128,128]{2,1,0:T(8,128)(2,1)} custom-call(s32[8,2048]{1,0:T(8,128)} %pad_add_fusion.refs_0_, bf16[128,27,4,128]{3,2,1,0:T(4,128)(2,1)} %all-to-all-done.3.refs_1_), custom_call_target="tpu_custom_call" | custom-call | flops 1000000000 | bytes 6000000 | tf_op jit(solution)/shard_map/add_rows/pallas_call | solution.py:471
  199.2 49.3 %all-to-all-done.4.got_ref.refs_1_ = bf16[128,35,4,128]{3,2,1,0:T(4,128)(2,1)} async-done(((bf16[128,35,4,128]{3,2,1,0:T(4,128)(2,1)}), bf16[128,35,4,128]{3,2,1,0:T(4,128)(2,1)}, u32[]{:S(2)}, u32[]{:S(2)}) %all-to-all-start.4) | async-done | bytes 4587552 | tf_op jit(solution)/shard_map/all_to_all | solution.py:567
  250.7 5.6 %all-to-all-start.5 = ((bf16[64,64,128]{2,1,0:T(8,128)(2,1)}), bf16[64,64,128]{2,1,0:T(8,128)(2,1)S(1)}, u32[]{:S(2)}, u32[]{:S(2)}) async-start(bf16[64,64,128]{2,1,0:T(8,128)(2,1)} %bitcast.20), calls=%async_computation.5 | async-start | bytes 2097152 | tf_op jit(solution)/shard_map/all_to_all | solution.py:631
  256.3 7.0 %add_rows.3 = f32[9,128,128]{2,1,0:T(8,128)} custom-call(s32[8,2048]{1,0:T(8,128)} %pad_add_fusion.refs_0_, bf16[128,35,4,128]{3,2,1,0:T(4,128)(2,1)} %all-to-all-done.4.got_ref.refs_1_), custom_call_target="tpu_custom_call" | custom-call | flops 1000000000 | bytes 6000000 | tf_op jit(solution)/shard_map/add_rows/pallas_call | solution.py:471
  263.3 10.2 %all-to-all-done.5 = bf16[64,64,128]{2,1,0:T(8,128)(2,1)S(1)} async-done(((bf16[64,64,128]{2,1,0:T(8,128)(2,1)}), bf16[64,64,128]{2,1,0:T(8,128)(2,1)S(1)}, u32[]{:S(2)}, u32[]{:S(2)}) %all-to-all-start.5) | async-done | bytes 1048608 | tf_op jit(solution)/shard_map/all_to_all | solution.py:631
  273.5 2.5 collective-permute-start.1
  278.2 2.9 %unpack.1 = (f32[1,768,512]{2,1,0:T(8,128)}, f32[2,512,256]{2,1,0:T(8,128)}, f32[2,256,128]{2,1,0:T(8,128)}, f32[1,384,384]{2,1,0:T(8,128)}, f32[2,256,256]{2,1,0:T(8,128)}, /*index=5*/f32[2,128,128]{2,1,0:T(8,128)}) custom-call(s32[2]{0:T(128)S(1)} %copy-done, bf16[64,2,32,128]{3,2,1,0:T(8,128)(2,1)S(1)} %bitcast.45, ...), custom_call_target="tpu_custom_call" | custom-call | flops 1000000 | bytes 6000000 | tf_op jit(solution)/shard_map/unpack/pallas_call | solution.py:549
  (71 shorter events, 39.3 us)
Async XLA Ops:
  5.3 20.8 %all-to-all-start = ((s32[128,1,64]{2,1,0:T(1,128)}), s32[128,1,64]{2,1,0:T(1,128)S(1)}, u32[]{:S(2)}, u32[]{:S(2)}) async-start(s32[128,1,64]{2,1,0:T(1,128)} %request_rows.1), calls=%async_computation | async-start | bytes 131072 | tf_op jit(solution)/shard_map/all_to_all | solution.py:567
  17.5 13.1 %copy-start.8 = (s32[32]{0:T(128)}, s32[32]{0:T(128)S(1)}, u32[]{:S(2)}) copy-start(s32[32]{0:T(128)S(1)} %reshape.129.own_ref.refs_0_) | copy-start | bytes 388
  26.1 1.0 copy-start.1
  30.7 52.4 %all-to-all-start.2 = ((bf16[128,27,4,128]{3,2,1,0:T(4,128)(2,1)}), bf16[128,27,4,128]{3,2,1,0:T(4,128)(2,1)}, u32[]{:S(2)}, u32[]{:S(2)}) async-start(bf16[128,27,4,128]{3,2,1,0:T(4,128)(2,1)} %pick_rows.3), calls=%async_computation.2 | async-start | bytes 7077888 | tf_op jit(solution)/shard_map/all_to_all | solution.py:567
  56.2 11.9 %copy-start.7 = (bf16[2,128,128]{2,1,0:T(8,128)(2,1)S(1)}, bf16[2,128,128]{2,1,0:T(8,128)(2,1)}, u32[]{:S(2)}) copy-start(bf16[2,128,128]{2,1,0:T(8,128)(2,1)} %param.28) | copy-start | bytes 196612
  56.2 12.6 %copy-start.6 = (bf16[2,256,128]{2,1,0:T(8,128)(2,1)S(1)}, bf16[2,256,128]{2,1,0:T(8,128)(2,1)}, u32[]{:S(2)}) copy-start(bf16[2,256,128]{2,1,0:T(8,128)(2,1)} %param.25) | copy-start | bytes 393220
  56.2 13.4 %copy-start.5 = (bf16[2,256,256]{2,1,0:T(8,128)(2,1)S(1)}, bf16[2,256,256]{2,1,0:T(8,128)(2,1)}, u32[]{:S(2)}) copy-start(bf16[2,256,256]{2,1,0:T(8,128)(2,1)} %param.27) | copy-start | bytes 786436
  68.1 2.4 copy-start.3
  69.6 2.0 copy-start.2
  83.1 51.3 %all-to-all-start.1 = ((bf16[128,27,4,128]{3,2,1,0:T(4,128)(2,1)}), bf16[128,27,4,128]{3,2,1,0:T(4,128)(2,1)}, u32[]{:S(2)}, u32[]{:S(2)}) async-start(bf16[128,27,4,128]{3,2,1,0:T(4,128)(2,1)} %pick_rows.2), calls=%async_computation.1 | async-start | bytes 7077888 | tf_op jit(solution)/shard_map/all_to_all | solution.py:567
  134.4 51.3 %all-to-all-start.3 = ((bf16[128,27,4,128]{3,2,1,0:T(4,128)(2,1)}), bf16[128,27,4,128]{3,2,1,0:T(4,128)(2,1)}, u32[]{:S(2)}, u32[]{:S(2)}) async-start(bf16[128,27,4,128]{3,2,1,0:T(4,128)(2,1)} %get-tuple-element.63), calls=%async_computation.3 | async-start | bytes 7077888 | tf_op jit(solution)/shard_map/all_to_all | solution.py:567
  164.0 3.8 %collective-permute-start = (bf16[4096,128]{1,0:T(8,128)(2,1)S(1)}, bf16[4096,128]{1,0:T(8,128)(2,1)S(1)}, u32[]{:S(2)}, u32[]{:S(2)}) collective-permute-start(bf16[4096,128]{1,0:T(8,128)(2,1)S(1)} %constant_dynamic-slice_fusion), channel_id=1, source_target_pairs={{0,1},{1,0},{2,3},{3,2},{4,5},{5,4},{6,7},{7,6},{8,9},{9,8},{10,11... | collective-permute-start | bytes 3145736 | tf_op jit(solution)/shard_map/ppermute | solution.py:487
  167.8 1.0 copy-start.4
  185.7 62.8 %all-to-all-start.4 = ((bf16[128,35,4,128]{3,2,1,0:T(4,128)(2,1)}), bf16[128,35,4,128]{3,2,1,0:T(4,128)(2,1)}, u32[]{:S(2)}, u32[]{:S(2)}) async-start(bf16[128,35,4,128]{3,2,1,0:T(4,128)(2,1)} %pad_maximum_fusion), calls=%async_computation.4 | async-start | bytes 9175040 | tf_op jit(solution)/shard_map/all_to_all | solution.py:567
  250.7 22.7 %all-to-all-start.5 = ((bf16[64,64,128]{2,1,0:T(8,128)(2,1)}), bf16[64,64,128]{2,1,0:T(8,128)(2,1)S(1)}, u32[]{:S(2)}, u32[]{:S(2)}) async-start(bf16[64,64,128]{2,1,0:T(8,128)(2,1)} %bitcast.20), calls=%async_computation.5 | async-start | bytes 2097152 | tf_op jit(solution)/shard_map/all_to_all | solution.py:631
  256.3 22.0 %copy-start = (s32[2]{0:T(128)S(1)}, s32[2]{0:T(128)}, u32[]{:S(2)}) copy-start(s32[2]{0:T(128)} %pad_add_fusion.1.core_ref) | copy-start | bytes 28
  273.5 4.8 %collective-permute-start.1 = (bf16[64,2,32,128]{3,2,1,0:T(8,128)(2,1)S(1)}, bf16[64,2,32,128]{3,2,1,0:T(8,128)(2,1)S(1)}, u32[]{:S(2)}, u32[]{:S(2)}) collective-permute-start(bf16[64,2,32,128]{3,2,1,0:T(8,128)(2,1)S(1)} %bitcast.44), channel_id=1, source_target_pairs={{0,1},{1,0},{2,3},{3,2},{4,5},{5,4},{6,7},{7,6},{8,9},{9,8},{10,11... | collective-permute-start | bytes 3145736 | tf_op jit(solution)/shard_map/ppermute | solution.py:487

commit v7 on v6

--- a/solution.py
+++ b/solution.py
@@ -94,7 +94,7 @@
 
 
 def request_body(blocks_ref, rows_ref, cols_ref, out_ref, seen_ref):
-    peers, ends = out_ref.shape[0], 2 * blocks_ref.shape[0]
+    peers, ends = out_ref.shape[0], 2 * blocks_ref.shape[1]
     out_ref[...] = jnp.full(out_ref.shape, -1, jnp.int32)
 
     def clear(o, carry):
@@ -105,12 +105,12 @@
     cols = cols_ref[...]
     for end in range(ends):
         pair, side = divmod(end, 2)
-        owner = blocks_ref[pair, side]
+        owner = blocks_ref[side, pair]
         slot = seen_ref[owner]
         seen_ref[owner] = slot + 1
         line = out_ref[owner]
         for k in range(6):
-            line = jnp.where(cols == 6 * slot + k, rows_ref[side, k, pair], line)
+            line = jnp.where(cols == 6 * slot + k, rows_ref[k, side, pair], line)
         out_ref[owner] = line
 
 
@@ -534,23 +534,32 @@
 def unpack(core, mine, other):
     chips = mine.shape[0]
 
-    def body(core_ref, mine_ref, other_ref, *outs):
-        for out, (row, parts, height, blocks) in zip(outs, WEIGHT_PARTS):
+    shapes = [(parts, height, 128 * blocks) for _, parts, height, blocks in WEIGHT_PARTS]
+
+    def body(core_ref, mine_ref, other_ref, *refs):
+        outs, held, sem = refs[:6], refs[6:12], refs[12]
+        copies = []
+        for i, (row, parts, height, blocks) in enumerate(WEIGHT_PARTS):
             for p in range(parts):
                 for n in range(blocks):
                     cols = slice(128 * n, 128 * n + 128)
                     for at in range(0, height, 2 * WR):
                         half, chip = divmod((row + (p * blocks + n) * height + at) // (2 * WR), chips)
                         low = pl.multiple_of(at + WR * core_ref[0], WR)
-                        out[p, pl.ds(low, WR), cols] = mine_ref[chip, half].astype(F32)
+                        held[i][p, pl.ds(low, WR), cols] = mine_ref[chip, half].astype(F32)
                         low = pl.multiple_of(at + WR * (1 - core_ref[0]), WR)
-                        out[p, pl.ds(low, WR), cols] = other_ref[chip, half].astype(F32)
+                        held[i][p, pl.ds(low, WR), cols] = other_ref[chip, half].astype(F32)
+            copies.append(pltpu.make_async_copy(held[i], outs[i], sem.at[i]))
+            copies[-1].start()
+        for copy in copies:
+            copy.wait()
 
     return pl.pallas_call(
         body,
         in_specs=[SM, VM, VM],
-        out_specs=[VM] * 6,
-        out_shape=[jax.ShapeDtypeStruct((parts, height, 128 * blocks), F32) for _, parts, height, blocks in WEIGHT_PARTS],
+        out_specs=[pl.BlockSpec(memory_space=pl.ANY)] * 6,
+        out_shape=[jax.ShapeDtypeStruct(shape, F32) for shape in shapes],
+        scratch_shapes=[pltpu.VMEM(shape, F32) for shape in shapes] + [pltpu.SemaphoreType.DMA((6,))],
         compiler_params=pltpu.CompilerParams(vmem_limit_bytes=VMEM_LIMIT // 2),
         cost_estimate=pl.CostEstimate(flops=10**6, transcendentals=0, bytes_accessed=6 * 10**6),
         name="unpack",
@@ -581,7 +590,9 @@
         jnp.logical_and(owners[:, None] == owners[None, :], ends[:, None] > ends[None, :]), axis=1
     ).astype(jnp.int32)
 
-    asked = exchange(request_rows(pair_blocks, pair_rows, peers)).reshape(peers, 64)
+    asked = exchange(
+        request_rows(jnp.transpose(pair_blocks), jnp.transpose(pair_rows, (1, 0, 2)), peers)
+    ).reshape(peers, 64)
     asked_rows = jnp.transpose(asked.reshape(peers, 4, 16), (1, 0, 2)).reshape(4, peers * 16)
     asked_rows = jnp.concatenate([asked_rows, asked_rows], axis=0)
     eye = jnp.eye(64, dtype=BF16)

time: 283 us -> 281 us (level)
    unnamed x28 -> x27, local copies, waits for them, and re-layouts: 10.5 us -> 8.65 us
where the time goes in v7:
time: 281 us; the launch traced here: 279 us
  waiting for transfers between devices  106 us (38%)
  Pallas kernels  85.2 us (30%)
  starting transfers between devices  45.6 us (16%)
  local copies, waits for them, and re-layouts  27.9 us (10%)
  other arithmetic  12.4 us (4%)
    all_to_all x5, waiting for transfers between devices, exchange(): return lax.all_to_all(x, 'atoms', split_axis=0, concat_axis=0, tiled=True)  92.3 us
    all_to_all x5, starting transfers between devices, exchange(): return lax.all_to_all(x, 'atoms', split_axis=0, concat_axis=0, tiled=True)  36 us
    pallas_call x1, Pallas kernels, backward(): pl.pallas_call(body, in_specs=[SM] + [VM] * 15, out_specs=[VM, VM], out_s...  22.5 us
    pallas_call x1, Pallas kernels, forward(): pl.pallas_call(forward_body, in_specs=[SM] + [VM] * 11, out_specs=[VM] *...  19.6 us
    pallas_call x2, Pallas kernels, add_rows(): pl.pallas_call(body, grid=(peers // 16,), in_specs=[pl.BlockSpec((8, 256)...  13.7 us
    pallas_call x1, Pallas kernels, build_turns(): pl.pallas_call(prep_body, grid=(pairs,), in_specs=[pl.BlockSpec((1, 224,...  11.9 us
    all_to_all x1, waiting for transfers between devices, local(): lax.all_to_all(add_peers(got_g).reshape(peers // 2, 2 * WR, 128), 'atoms'...  10.2 us
    unnamed x27, local copies, waits for them, and re-layouts  8.65 us
  transfers between devices with their start and end apart: 8, of which 8 were waited for; matrix products, arithmetic and copies ran while one was open for 14% of the time, Pallas kernels for 27%

profile of v7, /device:TPU:1, one launch (start us, length us, event | category | flops | bytes accessed | tf_op | source)
XLA Modules:
  0.0 278.5 jit_solution(219677075516783666)
XLA Ops:
  2.5 11.5 %all-to-all-start = ((s32[128,1,64]{2,1,0:T(1,128)}), s32[128,1,64]{2,1,0:T(1,128)S(1)}, u32[]{:S(2)}, u32[]{:S(2)}) async-start(s32[128,1,64]{2,1,0:T(1,128)} %request_rows.1), calls=%async_computation | async-start | bytes 131072 | tf_op jit(solution)/shard_map/all_to_all | solution.py:576
  20.2 3.1 %all-to-all-done = s32[128,1,64]{2,1,0:T(1,128)S(1)} async-done(((s32[128,1,64]{2,1,0:T(1,128)}), s32[128,1,64]{2,1,0:T(1,128)S(1)}, u32[]{:S(2)}, u32[]{:S(2)}) %all-to-all-start) | async-done | bytes 32800 | tf_op jit(solution)/shard_map/all_to_all | solution.py:576
  24.3 3.6 %pick_rows.3 = bf16[128,27,4,128]{3,2,1,0:T(4,128)(2,1)} custom-call(s32[128,64]{1,0:T(8,128)S(1)} %bitcast.48, bf16[64,64]{1,0:T(8,128)(2,1)S(1)} %fusion.eye_ref, bf16[9,128,128]{2,1,0:T(8,128)(2,1)S(1)} %bitcast.50), custom_call_target="tpu_custom_call" | custom-call | flops 2000000000 | bytes 4000000 | tf_op jit(solution)/shard_map/pick_rows/pallas_call | solution.py:131
  27.9 7.1 %all-to-all-start.2 = ((bf16[128,27,4,128]{3,2,1,0:T(4,128)(2,1)}), bf16[128,27,4,128]{3,2,1,0:T(4,128)(2,1)}, u32[]{:S(2)}, u32[]{:S(2)}) async-start(bf16[128,27,4,128]{3,2,1,0:T(4,128)(2,1)} %pick_rows.3), calls=%async_computation.2 | async-start | bytes 7077888 | tf_op jit(solution)/shard_map/all_to_all | solution.py:576
  44.7 5.9 %concatenate.45 = f32[32,9,16,24]{0,3,1,2:T(8,128)S(1)} concatenate(f32[9,9,16,24]{0,3,1,2:T(8,128)} %bitcast.54, f32[2,9,16,24]{0,3,1,2:T(8,128)} %broadcast_in_dim.6, f32[5,9,16,24]{0,3,1,2:T(8,128)} %broadcast_in_dim.7, f32[9,9,16,24]{0,3,1,2:T(8,128)} %bitcast.55, f32[7,9,16,24]{0,3,1,2:T(8,128)} %broadcast_in_dim.16), dimensions={0} | concatenate | bytes 884736 | tf_op jit(solution)/shard_map/concatenate | solution.py:614
  53.4 11.9 %build_turns.1 = (bf16[16,224,256]{2,1,0:T(8,128)(2,1)}, bf16[16,224,256]{2,1,0:T(8,128)(2,1)}, bf16[16,224,256]{2,1,0:T(8,128)(2,1)}, bf16[16,224,256]{2,1,0:T(8,128)(2,1)}) custom-call(f32[16,224,32]{2,1,0:T(8,128)} %pad.8.ra_ref, f32[16,32,256]{2,1,0:T(8,128)} %pad.9.rb_ref, bf16[32,256]{1,0:T(8,128)(2,1)} %constant.40.clone.sp_ref, ...), custom_call_target="tpu_custom_call" | custom-call | flops 1000000000 | bytes 10000000 | tf_op jit(solution)/shard_map/build_turns/pallas_call | solution.py:179
  68.8 3.7 %pick_rows.2 = bf16[128,27,4,128]{3,2,1,0:T(4,128)(2,1)} custom-call(s32[128,64]{1,0:T(8,128)S(1)} %bitcast.49, bf16[64,64]{1,0:T(8,128)(2,1)S(1)} %fusion.eye_ref, bf16[9,128,128]{2,1,0:T(8,128)(2,1)S(1)} %bitcast.51), custom_call_target="tpu_custom_call" | custom-call | flops 2000000000 | bytes 4000000 | tf_op jit(solution)/shard_map/pick_rows/pallas_call | solution.py:131
  72.5 7.8 %all-to-all-done.2.r_ref = bf16[128,27,4,128]{3,2,1,0:T(4,128)(2,1)} async-done(((bf16[128,27,4,128]{3,2,1,0:T(4,128)(2,1)}), bf16[128,27,4,128]{3,2,1,0:T(4,128)(2,1)}, u32[]{:S(2)}, u32[]{:S(2)}) %all-to-all-start.2) | async-done | bytes 3538976 | tf_op jit(solution)/shard_map/all_to_all | solution.py:576
  80.3 5.8 %all-to-all-start.1 = ((bf16[128,27,4,128]{3,2,1,0:T(4,128)(2,1)}), bf16[128,27,4,128]{3,2,1,0:T(4,128)(2,1)}, u32[]{:S(2)}, u32[]{:S(2)}) async-start(bf16[128,27,4,128]{3,2,1,0:T(4,128)(2,1)} %pick_rows.2), calls=%async_computation.1 | async-start | bytes 7077888 | tf_op jit(solution)/shard_map/all_to_all | solution.py:576
  86.1 19.6 %forward.1 = (bf16[128,27,4,128]{3,2,1,0:T(4,128)(2,1)}, bf16[768,2304]{1,0:T(8,128)(2,1)}, f32[768,1152]{1,0:T(8,128)}, f32[768,128]{1,0:T(8,128)}, bf16[768,1152]{1,0:T(8,128)(2,1)}) custom-call(s32[32]{0:T(128)} %copy-done.8, bf16[128,27,4,128]{3,2,1,0:T(4,128)(2,1)} %all-to-all-done.2.r_ref, bf16[16,224,256]{2,1,0:T(8,128)(2,1)} %get-tuple-element.47.wt_ref.refs_2_, ...), custom_call_target="tpu_custom_call" | custom-call | flops 10000000000 | bytes 30000000 | tf_op jit(solution)/shard_map/forward/pallas_call | solution.py:282
  105.8 25.8 %all-to-all-done.1.refs_1_ = bf16[128,27,4,128]{3,2,1,0:T(4,128)(2,1)} async-done(((bf16[128,27,4,128]{3,2,1,0:T(4,128)(2,1)}), bf16[128,27,4,128]{3,2,1,0:T(4,128)(2,1)}, u32[]{:S(2)}, u32[]{:S(2)}) %all-to-all-start.1) | async-done | bytes 3538976 | tf_op jit(solution)/shard_map/all_to_all | solution.py:576
  131.6 5.8 %all-to-all-start.3 = ((bf16[128,27,4,128]{3,2,1,0:T(4,128)(2,1)}), bf16[128,27,4,128]{3,2,1,0:T(4,128)(2,1)}, u32[]{:S(2)}, u32[]{:S(2)}) async-start(bf16[128,27,4,128]{3,2,1,0:T(4,128)(2,1)} %get-tuple-element.63), calls=%async_computation.3 | async-start | bytes 7077888 | tf_op jit(solution)/shard_map/all_to_all | solution.py:576
  137.4 22.5 %backward.1 = (bf16[128,27,4,128]{3,2,1,0:T(4,128)(2,1)}, bf16[8192,128]{1,0:T(8,128)(2,1)}) custom-call(s32[32]{0:T(128)} %copy-done.8, bf16[128,27,4,128]{3,2,1,0:T(4,128)(2,1)} %all-to-all-done.1.refs_1_, bf16[16,224,256]{2,1,0:T(8,128)(2,1)} %get-tuple-element.47.wt_ref.refs_2_, bf16[16,224,256]{2,1,0:T(8,128)(2,1)} %get-tuple-element.48.ws_ref.refs_3_, ...), custom_call_target="tpu_custom_call" | custom-call | flops 20000000000 | bytes 30000000 | tf_op jit(solution)/shard_map/backward/pallas_call | solution.py:419
  166.0 3.2 %add_pair.1 = bf16[128,8,4,128]{3,2,1,0:T(4,128)(2,1)} custom-call(s32[2]{0:T(128)} %pad_add_fusion.1.core_ref, bf16[8192,128]{1,0:T(8,128)(2,1)} %get-tuple-element.61.grads_ref, bf16[4096,128]{1,0:T(8,128)(2,1)} %copy-done.4), custom_call_target="tpu_custom_call" | custom-call | flops 1000000 | bytes 4000000 | tf_op jit(solution)/shard_map/add_pair/pallas_call | solution.py:498
  169.3 7.4 %pad_maximum_fusion = bf16[128,35,4,128]{3,2,1,0:T(4,128)(2,1)} fusion(bf16[128,27,4,128]{3,2,1,0:T(4,128)(2,1)} %get-tuple-element.62, bf16[128,8,4,128]{3,2,1,0:T(4,128)(2,1)} %add_pair.1), kind=kLoop, calls=%fused_computation | loop fusion | flops 2293760 | bytes 9175040 | tf_op jit(solution)/shard_map/concatenate | solution.py:637
  176.7 6.2 %all-to-all-done.3.refs_1_ = bf16[128,27,4,128]{3,2,1,0:T(4,128)(2,1)} async-done(((bf16[128,27,4,128]{3,2,1,0:T(4,128)(2,1)}), bf16[128,27,4,128]{3,2,1,0:T(4,128)(2,1)}, u32[]{:S(2)}, u32[]{:S(2)}) %all-to-all-start.3) | async-done | bytes 3538976 | tf_op jit(solution)/shard_map/all_to_all | solution.py:576
  182.9 5.8 %all-to-all-start.4 = ((bf16[128,35,4,128]{3,2,1,0:T(4,128)(2,1)}), bf16[128,35,4,128]{3,2,1,0:T(4,128)(2,1)}, u32[]{:S(2)}, u32[]{:S(2)}) async-start(bf16[128,35,4,128]{3,2,1,0:T(4,128)(2,1)} %pad_maximum_fusion), calls=%async_computation.4 | async-start | bytes 9175040 | tf_op jit(solution)/shard_map/all_to_all | solution.py:576
  189.8 6.7 %add_rows.2 = bf16[9,128,128]{2,1,0:T(8,128)(2,1)} custom-call(s32[8,2048]{1,0:T(8,128)} %pad_add_fusion.refs_0_, bf16[128,27,4,128]{3,2,1,0:T(4,128)(2,1)} %all-to-all-done.3.refs_1_), custom_call_target="tpu_custom_call" | custom-call | flops 1000000000 | bytes 6000000 | tf_op jit(solution)/shard_map/add_rows/pallas_call | solution.py:471
  196.5 49.3 %all-to-all-done.4.got_ref.refs_1_ = bf16[128,35,4,128]{3,2,1,0:T(4,128)(2,1)} async-done(((bf16[128,35,4,128]{3,2,1,0:T(4,128)(2,1)}), bf16[128,35,4,128]{3,2,1,0:T(4,128)(2,1)}, u32[]{:S(2)}, u32[]{:S(2)}) %all-to-all-start.4) | async-done | bytes 4587552 | tf_op jit(solution)/shard_map/all_to_all | solution.py:576
  248.0 5.6 %all-to-all-start.5 = ((bf16[64,64,128]{2,1,0:T(8,128)(2,1)}), bf16[64,64,128]{2,1,0:T(8,128)(2,1)S(1)}, u32[]{:S(2)}, u32[]{:S(2)}) async-start(bf16[64,64,128]{2,1,0:T(8,128)(2,1)} %bitcast.22), calls=%async_computation.5 | async-start | bytes 2097152 | tf_op jit(solution)/shard_map/all_to_all | solution.py:642
  253.5 7.0 %add_rows.3 = f32[9,128,128]{2,1,0:T(8,128)} custom-call(s32[8,2048]{1,0:T(8,128)} %pad_add_fusion.refs_0_, bf16[128,35,4,128]{3,2,1,0:T(4,128)(2,1)} %all-to-all-done.4.got_ref.refs_1_), custom_call_target="tpu_custom_call" | custom-call | flops 1000000000 | bytes 6000000 | tf_op jit(solution)/shard_map/add_rows/pallas_call | solution.py:471
  260.6 10.2 %all-to-all-done.5 = bf16[64,64,128]{2,1,0:T(8,128)(2,1)S(1)} async-done(((bf16[64,64,128]{2,1,0:T(8,128)(2,1)}), bf16[64,64,128]{2,1,0:T(8,128)(2,1)S(1)}, u32[]{:S(2)}, u32[]{:S(2)}) %all-to-all-start.5) | async-done | bytes 1048608 | tf_op jit(solution)/shard_map/all_to_all | solution.py:642
  270.7 2.5 collective-permute-start.1
  275.5 2.9 %unpack.1 = (f32[1,768,512]{2,1,0:T(8,128)}, f32[2,512,256]{2,1,0:T(8,128)}, f32[2,256,128]{2,1,0:T(8,128)}, f32[1,384,384]{2,1,0:T(8,128)}, f32[2,256,256]{2,1,0:T(8,128)}, /*index=5*/f32[2,128,128]{2,1,0:T(8,128)}) custom-call(s32[2]{0:T(128)S(1)} %copy-done, bf16[64,2,32,128]{3,2,1,0:T(8,128)(2,1)S(1)} %bitcast.47, ...), custom_call_target="tpu_custom_call" | custom-call | flops 1000000 | bytes 6000000 | tf_op jit(solution)/shard_map/unpack/pallas_call | solution.py:557
  (70 shorter events, 36.5 us)
Async XLA Ops:
  2.5 20.8 %all-to-all-start = ((s32[128,1,64]{2,1,0:T(1,128)}), s32[128,1,64]{2,1,0:T(1,128)S(1)}, u32[]{:S(2)}, u32[]{:S(2)}) async-start(s32[128,1,64]{2,1,0:T(1,128)} %request_rows.1), calls=%async_computation | async-start | bytes 131072 | tf_op jit(solution)/shard_map/all_to_all | solution.py:576
  14.8 13.1 %copy-start.8 = (s32[32]{0:T(128)}, s32[32]{0:T(128)S(1)}, u32[]{:S(2)}) copy-start(s32[32]{0:T(128)S(1)} %reshape.129.own_ref.refs_0_) | copy-start | bytes 388
  23.3 1.0 copy-start.1
  27.9 52.4 %all-to-all-start.2 = ((bf16[128,27,4,128]{3,2,1,0:T(4,128)(2,1)}), bf16[128,27,4,128]{3,2,1,0:T(4,128)(2,1)}, u32[]{:S(2)}, u32[]{:S(2)}) async-start(bf16[128,27,4,128]{3,2,1,0:T(4,128)(2,1)} %pick_rows.3), calls=%async_computation.2 | async-start | bytes 7077888 | tf_op jit(solution)/shard_map/all_to_all | solution.py:576
  53.4 11.9 %copy-start.7 = (bf16[2,128,128]{2,1,0:T(8,128)(2,1)S(1)}, bf16[2,128,128]{2,1,0:T(8,128)(2,1)}, u32[]{:S(2)}) copy-start(bf16[2,128,128]{2,1,0:T(8,128)(2,1)} %param.28) | copy-start | bytes 196612
  53.4 12.6 %copy-start.6 = (bf16[2,256,128]{2,1,0:T(8,128)(2,1)S(1)}, bf16[2,256,128]{2,1,0:T(8,128)(2,1)}, u32[]{:S(2)}) copy-start(bf16[2,256,128]{2,1,0:T(8,128)(2,1)} %param.25) | copy-start | bytes 393220
  53.4 13.4 %copy-start.5 = (bf16[2,256,256]{2,1,0:T(8,128)(2,1)S(1)}, bf16[2,256,256]{2,1,0:T(8,128)(2,1)}, u32[]{:S(2)}) copy-start(bf16[2,256,256]{2,1,0:T(8,128)(2,1)} %param.27) | copy-start | bytes 786436
  65.3 2.4 copy-start.3
  66.9 2.0 copy-start.2
  80.3 51.3 %all-to-all-start.1 = ((bf16[128,27,4,128]{3,2,1,0:T(4,128)(2,1)}), bf16[128,27,4,128]{3,2,1,0:T(4,128)(2,1)}, u32[]{:S(2)}, u32[]{:S(2)}) async-start(bf16[128,27,4,128]{3,2,1,0:T(4,128)(2,1)} %pick_rows.2), calls=%async_computation.1 | async-start | bytes 7077888 | tf_op jit(solution)/shard_map/all_to_all | solution.py:576
  131.6 51.3 %all-to-all-start.3 = ((bf16[128,27,4,128]{3,2,1,0:T(4,128)(2,1)}), bf16[128,27,4,128]{3,2,1,0:T(4,128)(2,1)}, u32[]{:S(2)}, u32[]{:S(2)}) async-start(bf16[128,27,4,128]{3,2,1,0:T(4,128)(2,1)} %get-tuple-element.63), calls=%async_computation.3 | async-start | bytes 7077888 | tf_op jit(solution)/shard_map/all_to_all | solution.py:576
  161.2 3.8 %collective-permute-start = (bf16[4096,128]{1,0:T(8,128)(2,1)S(1)}, bf16[4096,128]{1,0:T(8,128)(2,1)S(1)}, u32[]{:S(2)}, u32[]{:S(2)}) collective-permute-start(bf16[4096,128]{1,0:T(8,128)(2,1)S(1)} %constant_dynamic-slice_fusion), channel_id=1, source_target_pairs={{0,1},{1,0},{2,3},{3,2},{4,5},{5,4},{6,7},{7,6},{8,9},{9,8},{10,11... | collective-permute-start | bytes 3145736 | tf_op jit(solution)/shard_map/ppermute | solution.py:487
  165.0 1.0 copy-start.4
  182.9 62.8 %all-to-all-start.4 = ((bf16[128,35,4,128]{3,2,1,0:T(4,128)(2,1)}), bf16[128,35,4,128]{3,2,1,0:T(4,128)(2,1)}, u32[]{:S(2)}, u32[]{:S(2)}) async-start(bf16[128,35,4,128]{3,2,1,0:T(4,128)(2,1)} %pad_maximum_fusion), calls=%async_computation.4 | async-start | bytes 9175040 | tf_op jit(solution)/shard_map/all_to_all | solution.py:576
  248.0 22.7 %all-to-all-start.5 = ((bf16[64,64,128]{2,1,0:T(8,128)(2,1)}), bf16[64,64,128]{2,1,0:T(8,128)(2,1)S(1)}, u32[]{:S(2)}, u32[]{:S(2)}) async-start(bf16[64,64,128]{2,1,0:T(8,128)(2,1)} %bitcast.22), calls=%async_computation.5 | async-start | bytes 2097152 | tf_op jit(solution)/shard_map/all_to_all | solution.py:642
  253.5 22.0 %copy-start = (s32[2]{0:T(128)S(1)}, s32[2]{0:T(128)}, u32[]{:S(2)}) copy-start(s32[2]{0:T(128)} %pad_add_fusion.1.core_ref) | copy-start | bytes 28
  270.7 4.8 %collective-permute-start.1 = (bf16[64,2,32,128]{3,2,1,0:T(8,128)(2,1)S(1)}, bf16[64,2,32,128]{3,2,1,0:T(8,128)(2,1)S(1)}, u32[]{:S(2)}, u32[]{:S(2)}) collective-permute-start(bf16[64,2,32,128]{3,2,1,0:T(8,128)(2,1)S(1)} %bitcast.46), channel_id=1, source_target_pairs={{0,1},{1,0},{2,3},{3,2},{4,5},{5,4},{6,7},{7,6},{8,9},{9,8},{10,11... | collective-permute-start | bytes 3145736 | tf_op jit(solution)/shard_map/ppermute | solution.py:487

commit v8 on v7

--- a/solution.py
+++ b/solution.py
@@ -69,7 +69,7 @@
 SM = pl.BlockSpec(memory_space=pltpu.SMEM)
 
 
-def gather_body(idx_ref, eye_ref, feat_ref, out_ref):
+def gather_body(idx_ref, eye_ref, right_ref, six_ref, out_ref):
     turned = dot_nt(eye_ref[...], idx_ref[...].astype(F32).astype(BF16))
     lane = lax.broadcasted_iota(jnp.int32, (64, 128), 1).astype(F32)
     picks = []
@@ -79,17 +79,10 @@
     kinds = [jnp.concatenate([x[16 * v : 16 * v + 16] for x in picks], axis=0) for v in range(4)]
     for j in range(3):
         left = jnp.concatenate([kinds[0], kinds[j + 1]], axis=1)
-        right = jnp.concatenate(
-            [
-                jnp.concatenate([feat_ref[j], feat_ref[j + 3]], axis=1),
-                jnp.concatenate([feat_ref[7], feat_ref[8]], axis=1),
-            ],
-            axis=0,
-        )
-        got = dot(left, right).astype(BF16)
+        got = dot(left, right_ref[j]).astype(BF16)
         out_ref[:, 4 * j : 4 * j + 4] = got[:, :128].reshape(PICK, 4, 4, 128)
         out_ref[:, 4 * (j + 3) : 4 * (j + 4)] = got[:, 128:].reshape(PICK, 4, 4, 128)
-    last = dot(kinds[0], feat_ref[6]).astype(BF16)
+    last = dot(kinds[0], six_ref[...]).astype(BF16)
     out_ref[:, 24:27] = last.reshape(PICK, 4, 4, 128)[:, :3]
 
 
@@ -126,7 +119,14 @@
     )(blocks, rows, cols)
 
 
-def pick_rows(idx, eye, feat):
+def stacked(block):
+    feat = jnp.transpose(block, (1, 0, 2))
+    upper = jnp.concatenate([feat[0:3], feat[3:6]], axis=2)
+    lower = jnp.broadcast_to(jnp.concatenate([feat[7:8], feat[8:9]], axis=2), upper.shape)
+    return jnp.concatenate([upper, lower], axis=1), feat[6]
+
+
+def pick_rows(idx, eye, right, six):
     peers = idx.shape[0]
     return pl.pallas_call(
         gather_body,
@@ -134,14 +134,15 @@
         in_specs=[
             pl.BlockSpec((PICK, 64), lambda c: (c, 0)),
             whole((64, 64)),
-            whole((9, 128, 128)),
+            whole((3, 256, 256)),
+            whole((128, 128)),
         ],
         out_specs=pl.BlockSpec((PICK, GROUPS, 4, 128), lambda c: (c, 0, 0, 0)),
         out_shape=jax.ShapeDtypeStruct((peers, GROUPS, 4, 128), BF16),
         compiler_params=pltpu.CompilerParams(vmem_limit_bytes=VMEM_LIMIT // 2),
         cost_estimate=pl.CostEstimate(flops=2 * 10**9, transcendentals=0, bytes_accessed=4 * 10**6),
         name="pick_rows",
-    )(idx, eye, feat)
+    )(idx, eye, right, six)
 
 
 def prep_body(ra_ref, rb_ref, sp_ref, spt_ref, rows_ref, rowst_ref, wt_ref, ws_ref, vt_ref, vs_ref):
@@ -597,7 +598,7 @@
     asked_rows = jnp.concatenate([asked_rows, asked_rows], axis=0)
     eye = jnp.eye(64, dtype=BF16)
 
-    got_f = exchange(pick_rows(asked, eye, jnp.transpose(features, (1, 0, 2))))
+    got_f = exchange(pick_rows(asked, eye, *stacked(features)))
 
     turned = jnp.stack([wigner[i] for i in COEF_ORDER]).reshape(9, 9, pairs, each)
     pos = jnp.stack(
@@ -622,7 +623,7 @@
         first_m0, widen_pair(first_m1), widen_pair(first_m2),
         second_m0, widen_pair(second_m1), widen_pair(second_m2),
     )
-    picked_c = pick_rows(asked, eye, jnp.transpose(cotangent, (1, 0, 2)))
+    picked_c = pick_rows(asked, eye, *stacked(cotangent))
     picked_c, turns, weights = lax.optimization_barrier((picked_c, turns, weights))
     got_c = exchange(picked_c)
     back_m, *kept = forward(owners, got_f, turns, weights, 2 * edges)

time: 281 us -> 284 us (1.011)
  starting transfers between devices: 45.6 us -> 48.6 us
    all_to_all x5, starting transfers between devices: 36 us -> 39.1 us  [exchange(): return lax.all_to_all(x, 'atoms', split_axis=0, concat_axis=0, tiled=True)]
    unnamed x27 -> x25, local copies, waits for them, and re-layouts: 8.65 us -> 7.68 us
  transfers between devices with their start and end apart: 8 -> 8, of which waited for: 8 -> 7; matrix products, arithmetic and copies ran while one was open for 14% -> 14% of each run, Pallas kernels for 27% -> 27%
where the time goes in v8:
time: 284 us; the launch traced here: 282 us
  waiting for transfers between devices  106 us (37%)
  Pallas kernels  85.2 us (30%)
  starting transfers between devices  48.6 us (17%)
  local copies, waits for them, and re-layouts  28.7 us (10%)
  other arithmetic  12.5 us (4%)
    all_to_all x5, waiting for transfers between devices, exchange(): return lax.all_to_all(x, 'atoms', split_axis=0, concat_axis=0, tiled=True)  91.4 us
    all_to_all x5, starting transfers between devices, exchange(): return lax.all_to_all(x, 'atoms', split_axis=0, concat_axis=0, tiled=True)  39.1 us
    pallas_call x1, Pallas kernels, backward(): pl.pallas_call(body, in_specs=[SM] + [VM] * 15, out_specs=[VM, VM], out_s...  22.5 us
    pallas_call x1, Pallas kernels, forward(): pl.pallas_call(forward_body, in_specs=[SM] + [VM] * 11, out_specs=[VM] *...  19.6 us
    pallas_call x2, Pallas kernels, add_rows(): pl.pallas_call(body, grid=(peers // 16,), in_specs=[pl.BlockSpec((8, 256)...  13.7 us
    pallas_call x1, Pallas kernels, build_turns(): pl.pallas_call(prep_body, grid=(pairs,), in_specs=[pl.BlockSpec((1, 224,...  11.9 us
    all_to_all x1, waiting for transfers between devices, local(): lax.all_to_all(add_peers(got_g).reshape(peers // 2, 2 * WR, 128), 'atoms'...  10.2 us
    unnamed x25, local copies, waits for them, and re-layouts  7.68 us
  transfers between devices with their start and end apart: 8, of which 7 were waited for; matrix products, arithmetic and copies ran while one was open for 14% of the time, Pallas kernels for 27%

profile of v8, /device:TPU:1, one launch (start us, length us, event | category | flops | bytes accessed | tf_op | source)
XLA Modules:
  0.0 281.7 jit_solution(16870882014655245343)
XLA Ops:
  2.5 11.5 %all-to-all-start = ((s32[128,1,64]{2,1,0:T(1,128)}), s32[128,1,64]{2,1,0:T(1,128)S(1)}, u32[]{:S(2)}, u32[]{:S(2)}) async-start(s32[128,1,64]{2,1,0:T(1,128)} %request_rows.1), calls=%async_computation | async-start | bytes 131072 | tf_op jit(solution)/shard_map/all_to_all | solution.py:577
  24.3 3.6 %pick_rows.3 = bf16[128,27,4,128]{3,2,1,0:T(4,128)(2,1)} custom-call(s32[128,64]{1,0:T(8,128)S(1)} %bitcast.56, bf16[64,64]{1,0:T(8,128)(2,1)S(1)} %fusion.eye_ref, bf16[3,256,256]{2,1,0:T(8,128)(2,1)S(1)} %pad_maximum_fusion.2.right_ref, bf16[128,128]{1,0:T(8,128)(2,1)S(1)} %get-tuple-element.82.six_ref), custom_call_target="tpu_custom_call" | custom-call | flops 2000000000 | bytes 4000000 | tf_op jit(solution)/shard_map/pick_rows/pallas_call | solution.py:131
  27.9 10.2 %all-to-all-start.2 = ((bf16[128,27,4,128]{3,2,1,0:T(4,128)(2,1)}), bf16[128,27,4,128]{3,2,1,0:T(4,128)(2,1)}, u32[]{:S(2)}, u32[]{:S(2)}) async-start(bf16[128,27,4,128]{3,2,1,0:T(4,128)(2,1)} %pick_rows.3), calls=%async_computation.2 | async-start | bytes 7077888 | tf_op jit(solution)/shard_map/all_to_all | solution.py:577
  45.5 5.9 %concatenate.66 = f32[32,9,16,24]{0,3,1,2:T(8,128)S(1)} concatenate(f32[9,9,16,24]{0,3,1,2:T(8,128)} %bitcast.60, f32[2,9,16,24]{0,3,1,2:T(8,128)} %broadcast_in_dim.30, f32[5,9,16,24]{0,3,1,2:T(8,128)} %broadcast_in_dim.31, f32[9,9,16,24]{0,3,1,2:T(8,128)} %bitcast.61, f32[7,9,16,24]{0,3,1,2:T(8,128)} %broadcast_in_dim.32), dimensions={0} | concatenate | bytes 884736 | tf_op jit(solution)/shard_map/concatenate | solution.py:615
  54.3 11.9 %build_turns.1 = (bf16[16,224,256]{2,1,0:T(8,128)(2,1)}, bf16[16,224,256]{2,1,0:T(8,128)(2,1)}, bf16[16,224,256]{2,1,0:T(8,128)(2,1)}, bf16[16,224,256]{2,1,0:T(8,128)(2,1)}) custom-call(f32[16,224,32]{2,1,0:T(8,128)} %pad.8.ra_ref, f32[16,32,256]{2,1,0:T(8,128)} %pad.9.rb_ref, bf16[32,256]{1,0:T(8,128)(2,1)} %constant.40.clone.sp_ref, ...), custom_call_target="tpu_custom_call" | custom-call | flops 1000000000 | bytes 10000000 | tf_op jit(solution)/shard_map/build_turns/pallas_call | solution.py:180
  69.8 3.7 %pick_rows.2 = bf16[128,27,4,128]{3,2,1,0:T(4,128)(2,1)} custom-call(s32[128,64]{1,0:T(8,128)S(1)} %bitcast.57, bf16[64,64]{1,0:T(8,128)(2,1)S(1)} %fusion.eye_ref, bf16[3,256,256]{2,1,0:T(8,128)(2,1)S(1)} %pad_maximum_fusion.1.right_ref, bf16[128,128]{1,0:T(8,128)(2,1)S(1)} %get-tuple-element.87.six_ref), custom_call_target="tpu_custom_call" | custom-call | flops 2000000000 | bytes 4000000 | tf_op jit(solution)/shard_map/pick_rows/pallas_call | solution.py:131
  73.5 9.9 %all-to-all-done.2.r_ref = bf16[128,27,4,128]{3,2,1,0:T(4,128)(2,1)} async-done(((bf16[128,27,4,128]{3,2,1,0:T(4,128)(2,1)}), bf16[128,27,4,128]{3,2,1,0:T(4,128)(2,1)}, u32[]{:S(2)}, u32[]{:S(2)}) %all-to-all-start.2) | async-done | bytes 3538976 | tf_op jit(solution)/shard_map/all_to_all | solution.py:577
  83.4 5.8 %all-to-all-start.1 = ((bf16[128,27,4,128]{3,2,1,0:T(4,128)(2,1)}), bf16[128,27,4,128]{3,2,1,0:T(4,128)(2,1)}, u32[]{:S(2)}, u32[]{:S(2)}) async-start(bf16[128,27,4,128]{3,2,1,0:T(4,128)(2,1)} %pick_rows.2), calls=%async_computation.1 | async-start | bytes 7077888 | tf_op jit(solution)/shard_map/all_to_all | solution.py:577
  89.3 19.6 %forward.1 = (bf16[128,27,4,128]{3,2,1,0:T(4,128)(2,1)}, bf16[768,2304]{1,0:T(8,128)(2,1)}, f32[768,1152]{1,0:T(8,128)}, f32[768,128]{1,0:T(8,128)}, bf16[768,1152]{1,0:T(8,128)(2,1)}) custom-call(s32[32]{0:T(128)} %copy-done.7, bf16[128,27,4,128]{3,2,1,0:T(4,128)(2,1)} %all-to-all-done.2.r_ref, bf16[16,224,256]{2,1,0:T(8,128)(2,1)} %get-tuple-element.47.wt_ref.refs_2_, ...), custom_call_target="tpu_custom_call" | custom-call | flops 10000000000 | bytes 30000000 | tf_op jit(solution)/shard_map/forward/pallas_call | solution.py:283
  108.9 25.8 %all-to-all-done.1.refs_1_ = bf16[128,27,4,128]{3,2,1,0:T(4,128)(2,1)} async-done(((bf16[128,27,4,128]{3,2,1,0:T(4,128)(2,1)}), bf16[128,27,4,128]{3,2,1,0:T(4,128)(2,1)}, u32[]{:S(2)}, u32[]{:S(2)}) %all-to-all-start.1) | async-done | bytes 3538976 | tf_op jit(solution)/shard_map/all_to_all | solution.py:577
  134.7 5.8 %all-to-all-start.3 = ((bf16[128,27,4,128]{3,2,1,0:T(4,128)(2,1)}), bf16[128,27,4,128]{3,2,1,0:T(4,128)(2,1)}, u32[]{:S(2)}, u32[]{:S(2)}) async-start(bf16[128,27,4,128]{3,2,1,0:T(4,128)(2,1)} %get-tuple-element.63), calls=%async_computation.3 | async-start | bytes 7077888 | tf_op jit(solution)/shard_map/all_to_all | solution.py:577
  140.6 22.5 %backward.1 = (bf16[128,27,4,128]{3,2,1,0:T(4,128)(2,1)}, bf16[8192,128]{1,0:T(8,128)(2,1)}) custom-call(s32[32]{0:T(128)} %copy-done.7, bf16[128,27,4,128]{3,2,1,0:T(4,128)(2,1)} %all-to-all-done.1.refs_1_, bf16[16,224,256]{2,1,0:T(8,128)(2,1)} %get-tuple-element.47.wt_ref.refs_2_, bf16[16,224,256]{2,1,0:T(8,128)(2,1)} %get-tuple-element.48.ws_ref.refs_3_, ...), custom_call_target="tpu_custom_call" | custom-call | flops 20000000000 | bytes 30000000 | tf_op jit(solution)/shard_map/backward/pallas_call | solution.py:420
  169.1 3.2 %add_pair.1 = bf16[128,8,4,128]{3,2,1,0:T(4,128)(2,1)} custom-call(s32[2]{0:T(128)} %pad_add_fusion.1.core_ref, bf16[8192,128]{1,0:T(8,128)(2,1)} %get-tuple-element.61.grads_ref, bf16[4096,128]{1,0:T(8,128)(2,1)} %copy-done.2), custom_call_target="tpu_custom_call" | custom-call | flops 1000000 | bytes 4000000 | tf_op jit(solution)/shard_map/add_pair/pallas_call | solution.py:499
  172.4 7.4 %pad_maximum_fusion = bf16[128,35,4,128]{3,2,1,0:T(4,128)(2,1)} fusion(bf16[128,27,4,128]{3,2,1,0:T(4,128)(2,1)} %get-tuple-element.62, bf16[128,8,4,128]{3,2,1,0:T(4,128)(2,1)} %add_pair.1), kind=kLoop, calls=%fused_computation | loop fusion | flops 2293760 | bytes 9175040 | tf_op jit(solution)/shard_map/concatenate | solution.py:638
  179.8 6.3 %all-to-all-done.3.refs_1_ = bf16[128,27,4,128]{3,2,1,0:T(4,128)(2,1)} async-done(((bf16[128,27,4,128]{3,2,1,0:T(4,128)(2,1)}), bf16[128,27,4,128]{3,2,1,0:T(4,128)(2,1)}, u32[]{:S(2)}, u32[]{:S(2)}) %all-to-all-start.3) | async-done | bytes 3538976 | tf_op jit(solution)/shard_map/all_to_all | solution.py:577
  186.0 5.8 %all-to-all-start.4 = ((bf16[128,35,4,128]{3,2,1,0:T(4,128)(2,1)}), bf16[128,35,4,128]{3,2,1,0:T(4,128)(2,1)}, u32[]{:S(2)}, u32[]{:S(2)}) async-start(bf16[128,35,4,128]{3,2,1,0:T(4,128)(2,1)} %pad_maximum_fusion), calls=%async_computation.4 | async-start | bytes 9175040 | tf_op jit(solution)/shard_map/all_to_all | solution.py:577
  192.9 6.7 %add_rows.2 = bf16[9,128,128]{2,1,0:T(8,128)(2,1)} custom-call(s32[8,2048]{1,0:T(8,128)} %pad_add_fusion.refs_0_, bf16[128,27,4,128]{3,2,1,0:T(4,128)(2,1)} %all-to-all-done.3.refs_1_), custom_call_target="tpu_custom_call" | custom-call | flops 1000000000 | bytes 6000000 | tf_op jit(solution)/shard_map/add_rows/pallas_call | solution.py:472
  199.6 49.3 %all-to-all-done.4.got_ref.refs_1_ = bf16[128,35,4,128]{3,2,1,0:T(4,128)(2,1)} async-done(((bf16[128,35,4,128]{3,2,1,0:T(4,128)(2,1)}), bf16[128,35,4,128]{3,2,1,0:T(4,128)(2,1)}, u32[]{:S(2)}, u32[]{:S(2)}) %all-to-all-start.4) | async-done | bytes 4587552 | tf_op jit(solution)/shard_map/all_to_all | solution.py:577
  251.1 5.6 %all-to-all-start.5 = ((bf16[64,64,128]{2,1,0:T(8,128)(2,1)}), bf16[64,64,128]{2,1,0:T(8,128)(2,1)S(1)}, u32[]{:S(2)}, u32[]{:S(2)}) async-start(bf16[64,64,128]{2,1,0:T(8,128)(2,1)} %bitcast.26), calls=%async_computation.5 | async-start | bytes 2097152 | tf_op jit(solution)/shard_map/all_to_all | solution.py:643
  256.7 7.0 %add_rows.3 = f32[9,128,128]{2,1,0:T(8,128)} custom-call(s32[8,2048]{1,0:T(8,128)} %pad_add_fusion.refs_0_, bf16[128,35,4,128]{3,2,1,0:T(4,128)(2,1)} %all-to-all-done.4.got_ref.refs_1_), custom_call_target="tpu_custom_call" | custom-call | flops 1000000000 | bytes 6000000 | tf_op jit(solution)/shard_map/add_rows/pallas_call | solution.py:472
  263.7 10.2 %all-to-all-done.5 = bf16[64,64,128]{2,1,0:T(8,128)(2,1)S(1)} async-done(((bf16[64,64,128]{2,1,0:T(8,128)(2,1)}), bf16[64,64,128]{2,1,0:T(8,128)(2,1)S(1)}, u32[]{:S(2)}, u32[]{:S(2)}) %all-to-all-start.5) | async-done | bytes 1048608 | tf_op jit(solution)/shard_map/all_to_all | solution.py:643
  273.9 2.5 collective-permute-start.1
  276.3 2.3 collective-permute-done.1.other_ref
  278.6 2.9 %unpack.1 = (f32[1,768,512]{2,1,0:T(8,128)}, f32[2,512,256]{2,1,0:T(8,128)}, f32[2,256,128]{2,1,0:T(8,128)}, f32[1,384,384]{2,1,0:T(8,128)}, f32[2,256,256]{2,1,0:T(8,128)}, /*index=5*/f32[2,128,128]{2,1,0:T(8,128)}) custom-call(s32[2]{0:T(128)S(1)} %copy-done, bf16[64,2,32,128]{3,2,1,0:T(8,128)(2,1)S(1)} %bitcast.55, ...), custom_call_target="tpu_custom_call" | custom-call | flops 1000000 | bytes 6000000 | tf_op jit(solution)/shard_map/unpack/pallas_call | solution.py:558
  (78 shorter events, 35.2 us)
Async XLA Ops:
  2.5 21.8 %all-to-all-start = ((s32[128,1,64]{2,1,0:T(1,128)}), s32[128,1,64]{2,1,0:T(1,128)S(1)}, u32[]{:S(2)}, u32[]{:S(2)}) async-start(s32[128,1,64]{2,1,0:T(1,128)} %request_rows.1), calls=%async_computation | async-start | bytes 131072 | tf_op jit(solution)/shard_map/all_to_all | solution.py:577
  16.6 11.3 %copy-start.7 = (s32[32]{0:T(128)}, s32[32]{0:T(128)S(1)}, u32[]{:S(2)}) copy-start(s32[32]{0:T(128)S(1)} %reshape.129.own_ref.refs_0_) | copy-start | bytes 388
  27.9 55.5 %all-to-all-start.2 = ((bf16[128,27,4,128]{3,2,1,0:T(4,128)(2,1)}), bf16[128,27,4,128]{3,2,1,0:T(4,128)(2,1)}, u32[]{:S(2)}, u32[]{:S(2)}) async-start(bf16[128,27,4,128]{3,2,1,0:T(4,128)(2,1)} %pick_rows.3), calls=%async_computation.2 | async-start | bytes 7077888 | tf_op jit(solution)/shard_map/all_to_all | solution.py:577
  54.3 11.9 %copy-start.4 = (bf16[128,9,128]{2,0,1:T(8,128)(2,1)S(1)}, bf16[128,9,128]{2,0,1:T(8,128)(2,1)}, u32[]{:S(2)}) copy-start(bf16[128,9,128]{2,0,1:T(8,128)(2,1)} %param.18) | copy-start | bytes 884740
  54.3 12.0 %copy-start.6 = (bf16[2,128,128]{2,1,0:T(8,128)(2,1)S(1)}, bf16[2,128,128]{2,1,0:T(8,128)(2,1)}, u32[]{:S(2)}) copy-start(bf16[2,128,128]{2,1,0:T(8,128)(2,1)} %param.28) | copy-start | bytes 196612
  54.3 12.7 %copy-start.5 = (bf16[2,256,128]{2,1,0:T(8,128)(2,1)S(1)}, bf16[2,256,128]{2,1,0:T(8,128)(2,1)}, u32[]{:S(2)}) copy-start(bf16[2,256,128]{2,1,0:T(8,128)(2,1)} %param.25) | copy-start | bytes 393220
  66.2 1.6 copy-start.3
  66.3 2.4 copy-start.1
  83.4 51.3 %all-to-all-start.1 = ((bf16[128,27,4,128]{3,2,1,0:T(4,128)(2,1)}), bf16[128,27,4,128]{3,2,1,0:T(4,128)(2,1)}, u32[]{:S(2)}, u32[]{:S(2)}) async-start(bf16[128,27,4,128]{3,2,1,0:T(4,128)(2,1)} %pick_rows.2), calls=%async_computation.1 | async-start | bytes 7077888 | tf_op jit(solution)/shard_map/all_to_all | solution.py:577
  134.7 51.3 %all-to-all-start.3 = ((bf16[128,27,4,128]{3,2,1,0:T(4,128)(2,1)}), bf16[128,27,4,128]{3,2,1,0:T(4,128)(2,1)}, u32[]{:S(2)}, u32[]{:S(2)}) async-start(bf16[128,27,4,128]{3,2,1,0:T(4,128)(2,1)} %get-tuple-element.63), calls=%async_computation.3 | async-start | bytes 7077888 | tf_op jit(solution)/shard_map/all_to_all | solution.py:577
  164.4 3.8 %collective-permute-start = (bf16[4096,128]{1,0:T(8,128)(2,1)S(1)}, bf16[4096,128]{1,0:T(8,128)(2,1)S(1)}, u32[]{:S(2)}, u32[]{:S(2)}) collective-permute-start(bf16[4096,128]{1,0:T(8,128)(2,1)S(1)} %constant_dynamic-slice_fusion), channel_id=1, source_target_pairs={{0,1},{1,0},{2,3},{3,2},{4,5},{5,4},{6,7},{7,6},{8,9},{9,8},{10,11... | collective-permute-start | bytes 3145736 | tf_op jit(solution)/shard_map/ppermute | solution.py:488
  168.2 1.0 copy-start.2
  186.0 62.9 %all-to-all-start.4 = ((bf16[128,35,4,128]{3,2,1,0:T(4,128)(2,1)}), bf16[128,35,4,128]{3,2,1,0:T(4,128)(2,1)}, u32[]{:S(2)}, u32[]{:S(2)}) async-start(bf16[128,35,4,128]{3,2,1,0:T(4,128)(2,1)} %pad_maximum_fusion), calls=%async_computation.4 | async-start | bytes 9175040 | tf_op jit(solution)/shard_map/all_to_all | solution.py:577
  251.1 22.7 %all-to-all-start.5 = ((bf16[64,64,128]{2,1,0:T(8,128)(2,1)}), bf16[64,64,128]{2,1,0:T(8,128)(2,1)S(1)}, u32[]{:S(2)}, u32[]{:S(2)}) async-start(bf16[64,64,128]{2,1,0:T(8,128)(2,1)} %bitcast.26), calls=%async_computation.5 | async-start | bytes 2097152 | tf_op jit(solution)/shard_map/all_to_all | solution.py:643
  256.7 22.0 %copy-start = (s32[2]{0:T(128)S(1)}, s32[2]{0:T(128)}, u32[]{:S(2)}) copy-start(s32[2]{0:T(128)} %pad_add_fusion.1.core_ref) | copy-start | bytes 28
  273.9 4.8 %collective-permute-start.1 = (bf16[64,2,32,128]{3,2,1,0:T(8,128)(2,1)S(1)}, bf16[64,2,32,128]{3,2,1,0:T(8,128)(2,1)S(1)}, u32[]{:S(2)}, u32[]{:S(2)}) collective-permute-start(bf16[64,2,32,128]{3,2,1,0:T(8,128)(2,1)S(1)} %bitcast.54), channel_id=1, source_target_pairs={{0,1},{1,0},{2,3},{3,2},{4,5},{5,4},{6,7},{7,6},{8,9},{9,8},{10,11... | collective-permute-start | bytes 3145736 | tf_op jit(solution)/shard_map/ppermute | solution.py:488
